TPU v7x, 32 devices: a whole 2x2x4 slice. The times are simulated.
32 devices in a mesh: dp: 16 (over z, y, core), tensor: 2 (over x).
Axes of the slice: x: 2, y: 2, z: 4, core: 2. Of those that a mesh axis runs over, the one named last changes fastest.
Arguments:
- tokens: bfloat16 [8192, 768], P(('dp', 'tensor')), may hold values from -6 to 6
- positions: int32 [8192], P('dp'), may hold values from 0 to 1533, as said below
- span_sizes: int32 [16], P('dp'), may hold values from 32 to 128, as said below
- w_query: bfloat16 [768, 768], replicated, may hold values from -0.21875 to 0.21875
- b_query: bfloat16 [768], replicated, may hold values from -3 to 3
- w_key: bfloat16 [768, 768], replicated, may hold values from -0.21875 to 0.21875
- b_key: bfloat16 [768], replicated, may hold values from -3 to 3
- w_value: bfloat16 [768, 768], replicated, may hold values from -0.21875 to 0.21875
- b_value: bfloat16 [768], replicated, may hold values from -3 to 3
- w_out: bfloat16 [768, 768], replicated, may hold values from -1.75 to 1.75
- b_out: bfloat16 [768], replicated, may hold values from -3 to 3
- norm1_gain: bfloat16 [768], replicated, may hold values from 0.5 to 1.5
- norm1_bias: bfloat16 [768], replicated, may hold values from -3 to 3
- w_up: bfloat16 [768, 3072], P(None, 'tensor'), may hold values from -0.21875 to 0.21875
- b_up: bfloat16 [3072], P('tensor'), may hold values from -3 to 3
- w_down: bfloat16 [3072, 768], P('tensor'), may hold values from -0.109375 to 0.109375
- b_down: bfloat16 [768], replicated, may hold values from -3 to 3
- norm2_gain: bfloat16 [768], replicated, may hold values from 0.5 to 1.5
- norm2_bias: bfloat16 [768], replicated, may hold values from -3 to 3
- out_grad: bfloat16 [8192, 768], P(('dp', 'tensor')), may hold values from -6 to 6
Outputs:
- block_out: bfloat16 [8192, 768], P(('dp', 'tensor'))
- tokens_grad: float32 [8192, 768], P(('dp', 'tensor'))
- w_query_grad: float32 [768, 768], replicated
- b_query_grad: float32 [768], replicated
- w_key_grad: float32 [768, 768], replicated
- b_key_grad: float32 [768], replicated
- w_value_grad: float32 [768, 768], replicated
- b_value_grad: float32 [768], replicated
- w_out_grad: float32 [768, 768], replicated
- b_out_grad: float32 [768], replicated
- norm1_gain_grad: float32 [768], replicated
- norm1_bias_grad: float32 [768], replicated
- w_up_grad: float32 [768, 3072], P(None, 'tensor')
- b_up_grad: float32 [3072], P('tensor')
- w_down_grad: float32 [3072, 768], P('tensor')
- b_down_grad: float32 [768], replicated
- norm2_gain_grad: float32 [768], replicated
- norm2_bias_grad: float32 [768], replicated
Inputs may be any that keep to these rules, and one draw needn't show every extreme that they name: Within each sequence of 512 rows the positions rise strictly and the first is 0; consecutive positions of a sequence differ by at most 5. The largest value is reached at the last row of some sequence. `span_sizes`: each span size is 32, 64 or 128; the smallest and the largest both occur.
All inputs are finite; a program needn't handle non-finite values.
Results may differ from a plain program's by a relative error of at most 0.018.
Values may be sent and summed in bfloat16 or wider, within the bound.
A program may use at most 320 MiB of HBM per device.

v0:
```python
import math

import jax
import jax.numpy as jnp
from jax import lax
from jax.sharding import PartitionSpec as P

HEADS = 12
HD = 64
SUBLEN = 32


highest = lax.Precision.HIGHEST
norm_eps = 1e-05


def norm_forward(value, gain, shift):
    mean = jnp.mean(value, axis=-1, keepdims=True)
    centred = value - mean
    scale = lax.rsqrt(jnp.mean(centred * centred, axis=-1, keepdims=True) + norm_eps)
    normal = centred * scale
    return (normal * gain + shift, normal, scale)


def norm_backward(grad, normal, scale, gain):
    along = grad * gain
    inner = (
        along
        - jnp.mean(along, axis=-1, keepdims=True)
        - normal * jnp.mean(along * normal, axis=-1, keepdims=True)
    )
    return (inner * scale, jnp.sum(grad * normal, axis=0), jnp.sum(grad, axis=0))


def gelu_slope(pre):
    normal_cdf = 0.5 * (1.0 + jax.scipy.special.erf(pre * (1.0 / math.sqrt(2.0))))
    return normal_cdf + pre * jnp.exp(-0.5 * pre * pre) * (1.0 / math.sqrt(2.0 * math.pi))


def reach_table(count, span):
    slot_index = jnp.arange(count, dtype=jnp.int32)
    final = (slot_index * SUBLEN // span + 1) * span // SUBLEN - 1
    return (slot_index[None, :] <= final[:, None]).astype(jnp.float32)


def features(rows, w_joint, b_joint, cosine, sine):
    length = rows.shape[0]
    width = rows.shape[1]
    proj = jnp.dot(rows, w_joint, preferred_element_type=jnp.float32) + b_joint
    relu_query = jax.nn.relu(proj[:, :width]).reshape(length, HEADS, HD)
    relu_key = jax.nn.relu(proj[:, width : 2 * width]).reshape(length, HEADS, HD) * (1.0 / HD)
    q_feat = jnp.concatenate([relu_query * cosine, relu_query * sine], axis=-1).astype(jnp.bfloat16)
    k_feat = jnp.concatenate([relu_key * cosine, relu_key * sine], axis=-1).astype(jnp.bfloat16)
    v_low = proj[:, 2 * width :].astype(jnp.bfloat16)
    return (q_feat, k_feat, v_low)


def local_blocks(k_feat, v_low):
    count = k_feat.shape[0] // SUBLEN
    k_sub = k_feat.reshape(count, SUBLEN, HEADS, 2 * HD)
    v_sub = v_low.reshape(count, SUBLEN, HEADS, HD)
    blocks = jnp.einsum("tjhf,tjhd->thfd", k_sub, v_sub, preferred_element_type=jnp.float32)
    k_total = jnp.sum(k_sub.astype(jnp.float32), axis=1)
    return (blocks, k_total)


def attend_core(q_feat, k_feat, v_low, blocks, k_total, reach, extra_blocks, extra_keys):
    count = q_feat.shape[0] // SUBLEN
    q_sub = q_feat.reshape(count, SUBLEN, HEADS, 2 * HD)
    k_sub = k_feat.reshape(count, SUBLEN, HEADS, 2 * HD)
    v_sub = v_low.reshape(count, SUBLEN, HEADS, HD)
    state_low = (
        jnp.einsum("st,thfd->shfd", reach, blocks, precision=highest) + extra_blocks
    ).astype(jnp.bfloat16)
    z_sum = jnp.einsum("st,thf->shf", reach, k_total, precision=highest) + extra_keys
    numer = jnp.einsum("sihf,shfd->sihd", q_sub, state_low, preferred_element_type=jnp.float32)
    denom = jnp.einsum("sihf,shf->sih", q_sub.astype(jnp.float32), z_sum, precision=highest) + 1.0
    return (q_sub, k_sub, v_sub, state_low, z_sum, numer, denom)


def back_first(parts, grad_mixed):
    q_sub, k_sub, v_sub, state_low, z_sum, numer, denom = parts
    count = q_sub.shape[0]
    grad_out = grad_mixed.reshape(count, SUBLEN, HEADS, HD).astype(jnp.float32)
    d_numer = grad_out / denom[..., None]
    d_denom = -jnp.sum(grad_out * numer, axis=-1) / (denom * denom)
    q_wide = q_sub.astype(jnp.float32)
    d_query = jnp.einsum(
        "sihd,shfd->sihf", d_numer, state_low.astype(jnp.float32), precision=highest
    )
    d_query = d_query + d_denom[..., None] * z_sum[:, None]
    d_state = jnp.einsum("sihf,sihd->shfd", q_wide, d_numer, precision=highest)
    d_zsum = jnp.einsum("sihf,sih->shf", q_wide, d_denom, precision=highest)
    return (d_query, d_state, d_zsum)


def back_second(parts, reach, d_state, d_zsum, later_blocks, later_keys):
    q_sub, k_sub, v_sub = (parts[0], parts[1], parts[2])
    d_blocks = jnp.einsum("st,shfd->thfd", reach, d_state, precision=highest) + later_blocks
    d_ktotal = jnp.einsum("st,shf->thf", reach, d_zsum, precision=highest) + later_keys
    d_key = (
        jnp.einsum("thfd,tjhd->tjhf", d_blocks, v_sub.astype(jnp.float32), precision=highest)
        + d_ktotal[:, None]
    )
    d_value = jnp.einsum("thfd,tjhf->tjhd", d_blocks, k_sub.astype(jnp.float32), precision=highest)
    return (d_key, d_value)


def feature_grads(q_feat, k_feat, d_qf, d_kf, d_val, cos_part, sin_part):
    size = q_feat.shape[0]
    d_qf = d_qf.reshape(size, HEADS, 2 * HD)
    d_kf = d_kf.reshape(size, HEADS, 2 * HD)
    d_query = jnp.where(
        q_feat[..., :HD] > 0, d_qf[..., :HD] * cos_part + d_qf[..., HD:] * sin_part, 0.0
    )
    d_key = jnp.where(
        k_feat[..., :HD] > 0,
        (d_kf[..., :HD] * cos_part + d_kf[..., HD:] * sin_part) * (1.0 / HD),
        0.0,
    )
    return jnp.concatenate(
        [
            d_query.reshape(size, HEADS * HD),
            d_key.reshape(size, HEADS * HD),
            d_val.reshape(size, HEADS * HD),
        ],
        axis=1,
    )


def per_device(
    tokens,
    positions,
    span_sizes,
    w_query,
    b_query,
    w_key,
    b_key,
    w_value,
    b_value,
    w_out,
    b_out,
    norm1_gain,
    norm1_bias,
    w_up,
    b_up,
    w_down,
    b_down,
    norm2_gain,
    norm2_bias,
    out_grad,
):
    rank = lax.axis_index("tensor")
    tensor_count = lax.axis_size("tensor")
    own = tokens.shape[0]
    width = tokens.shape[1]
    seqs = span_sizes.shape[0]
    group = own * tensor_count
    length = group // seqs
    start = rank * own
    w_joint = jnp.concatenate([w_query, w_key, w_value], axis=1)
    b_joint = jnp.concatenate([b_query, b_key, b_value]).astype(jnp.float32)
    gain_one = norm1_gain.astype(jnp.float32)
    gain_two = norm2_gain.astype(jnp.float32)
    gathered = lax.all_gather(tokens, "tensor", axis=0, tiled=True)
    angle = math.pi / 2 * positions.astype(jnp.float32) / (3 * length)
    cosine = jnp.cos(angle).reshape(seqs, length, 1, 1)
    sine = jnp.sin(angle).reshape(seqs, length, 1, 1)

    def seq_forward(items):
        rows, cos_part, sin_part, span = items
        q_feat, k_feat, v_low = features(rows, w_joint, b_joint, cos_part, sin_part)
        blocks_seq, ktot_seq = local_blocks(k_feat, v_low)
        parts = attend_core(
            q_feat,
            k_feat,
            v_low,
            blocks_seq,
            ktot_seq,
            reach_table(q_feat.shape[0] // SUBLEN, span),
            0.0,
            0.0,
        )
        mixed_seq = (
            (parts[5] / parts[6][..., None]).reshape(rows.shape[0], width).astype(jnp.bfloat16)
        )
        return (mixed_seq, q_feat, k_feat, v_low)

    mixed, q_all, k_all, v_all = lax.map(
        seq_forward, (gathered.reshape(seqs, length, width), cosine, sine, span_sizes)
    )
    mixed = mixed.reshape(group, width)
    mixed_own = lax.dynamic_slice_in_dim(mixed, start, own, 0)
    resid = (
        tokens.astype(jnp.float32)
        + jnp.dot(mixed_own, w_out, preferred_element_type=jnp.float32)
        + b_out.astype(jnp.float32)
    )
    hidden, normal_one, scale_one = norm_forward(resid, gain_one, norm1_bias.astype(jnp.float32))
    hidden_low = hidden.astype(jnp.bfloat16)
    rows_in = lax.all_gather(hidden_low, "tensor", axis=0, tiled=True)
    pre = jnp.dot(rows_in, w_up, preferred_element_type=jnp.float32) + b_up.astype(jnp.float32)
    act_low = jax.nn.gelu(pre, approximate=False).astype(jnp.bfloat16)
    branch = lax.psum_scatter(
        jnp.dot(act_low, w_down, preferred_element_type=jnp.float32),
        "tensor",
        scatter_dimension=0,
        tiled=True,
    )
    summed = hidden + branch + b_down.astype(jnp.float32)
    result, normal_two, scale_two = norm_forward(summed, gain_two, norm2_bias.astype(jnp.float32))
    d_sum, d_gain_two, d_bias_two = norm_backward(
        out_grad.astype(jnp.float32), normal_two, scale_two, gain_two
    )
    d_bdown = jnp.sum(d_sum, axis=0)
    d_sum_low = d_sum.astype(jnp.bfloat16)
    rows_grad = lax.all_gather(d_sum_low, "tensor", axis=0, tiled=True)
    g_down = jnp.dot(act_low.T, rows_grad, preferred_element_type=jnp.float32)
    d_pre = jnp.dot(rows_grad, w_down.T, preferred_element_type=jnp.float32) * gelu_slope(pre)
    g_upbias = jnp.sum(d_pre, axis=0)
    d_pre_low = d_pre.astype(jnp.bfloat16)
    g_up = jnp.dot(rows_in.T, d_pre_low, preferred_element_type=jnp.float32)
    d_hidden = lax.psum_scatter(
        jnp.dot(d_pre_low, w_up.T, preferred_element_type=jnp.float32),
        "tensor",
        scatter_dimension=0,
        tiled=True,
    )
    g_up, g_upbias, g_down = (
        lax.psum(g_up.astype(jnp.bfloat16), "dp").astype(jnp.float32),
        lax.psum(g_upbias.astype(jnp.bfloat16), "dp").astype(jnp.float32),
        lax.psum(g_down.astype(jnp.bfloat16), "dp").astype(jnp.float32),
    )
    d_hidden = d_hidden + d_sum
    d_resid, d_gain_one, d_bias_one = norm_backward(d_hidden, normal_one, scale_one, gain_one)
    d_bout = jnp.sum(d_resid, axis=0)
    d_gain_one, d_bias_one, d_gain_two, d_bias_two, d_bout, d_bdown = lax.psum(
        (d_gain_one, d_bias_one, d_gain_two, d_bias_two, d_bout, d_bdown), ("dp", "tensor")
    )
    d_resid_low = d_resid.astype(jnp.bfloat16)
    rows_back = lax.all_gather(d_resid_low, "tensor", axis=0, tiled=True)
    g_out = jnp.dot(mixed.T, rows_back, preferred_element_type=jnp.float32)
    d_mixed = jnp.dot(rows_back, w_out.T, preferred_element_type=jnp.float32).astype(jnp.bfloat16)

    def seq_backward(items):
        q_feat, k_feat, v_low, cos_part, sin_part, span, grad_mixed = items
        blocks_seq, ktot_seq = local_blocks(k_feat, v_low)
        reach = reach_table(q_feat.shape[0] // SUBLEN, span)
        parts = attend_core(q_feat, k_feat, v_low, blocks_seq, ktot_seq, reach, 0.0, 0.0)
        d_qf, d_state, d_zsum = back_first(parts, grad_mixed)
        d_kf, d_val = back_second(parts, reach, d_state, d_zsum, 0.0, 0.0)
        joint = feature_grads(q_feat, k_feat, d_qf, d_kf, d_val, cos_part, sin_part)
        return (joint.astype(jnp.bfloat16), jnp.sum(joint, axis=0))

    d_joint, d_jbias = lax.map(
        seq_backward,
        (q_all, k_all, v_all, cosine, sine, span_sizes, d_mixed.reshape(seqs, length, width)),
    )
    d_joint = d_joint.reshape(group, 3 * width)
    d_jbias = jnp.sum(d_jbias, axis=0)
    g_joint = jnp.dot(gathered.T, d_joint, preferred_element_type=jnp.float32)
    d_joint_own = lax.dynamic_slice_in_dim(d_joint, start, own, 0)
    d_tokens = d_resid + jnp.dot(d_joint_own, w_joint.T, preferred_element_type=jnp.float32)
    g_joint, g_out, d_jbias = lax.psum((g_joint, g_out, d_jbias), "dp")
    return (
        result.astype(jnp.bfloat16),
        d_tokens,
        g_joint[:, :width],
        d_jbias[:width],
        g_joint[:, width : 2 * width],
        d_jbias[width : 2 * width],
        g_joint[:, 2 * width :],
        d_jbias[2 * width :],
        g_out,
        d_bout,
        d_gain_one,
        d_bias_one,
        g_up,
        g_upbias,
        g_down,
        d_bdown,
        d_gain_two,
        d_bias_two,
    )


def solution(mesh):
    return jax.shard_map(
        per_device,
        mesh=mesh,
        in_specs=(
            P(("dp", "tensor"), None),
            P("dp"),
            P("dp"),
            P(),
            P(),
            P(),
            P(),
            P(),
            P(),
            P(),
            P(),
            P(),
            P(),
            P(None, "tensor"),
            P("tensor"),
            P("tensor", None),
            P(),
            P(),
            P(),
            P(("dp", "tensor"), None),
        ),
        out_specs=(
            P(("dp", "tensor"), None),
            P(("dp", "tensor"), None),
            P(),
            P(),
            P(),
            P(),
            P(),
            P(),
            P(),
            P(),
            P(),
            P(),
            P(None, "tensor"),
            P("tensor"),
            P("tensor", None),
            P(),
            P(),
            P(),
        ),
        check_vma=False,
    )
```

profile of v0, /device:TPU:0, one launch (start us, length us, event | category | flops | bytes accessed | tf_op | source)
XLA Modules:
  0.0 531.6 jit_solution(10538595827515254514)
XLA Ops:
  7.3 13.1 %all_gather.12 = bf16[512,768]{1,0:T(8,128)(2,1)S(1)} all-gather(bf16[256,768]{1,0:T(8,128)(2,1)} %param.20), channel_id=1, replica_groups=mesh['dp'=16,'tensor'=2] {'tensor'}, dimensions={0}, use_global_device_ids=true | all-gather | bytes 1179648 | tf_op jit(solution)/shard_map/all_gather | solution.py:165
  20.4 1.7 constant_dynamic-update-slice_fusion.2
  22.3 2.6 fusion.8
  25.1 2.0 slice_maximum_fusion.1
  29.1 3.3 reshape.261
  32.4 5.5 %copy.118 = bf16[16,32,12,64]{3,1,2,0:T(8,128)(2,1)} copy(bf16[16,32,12,64]{1,0,3,2:T(8,128)(2,1)} %reshape.261) | data formatting | bytes 1572864 | tf_op jit(solution)/shard_map/while/body/eval_jaxpr/reshape | solution.py:61
  37.9 5.1 reshape.260
  43.0 6.5 %copy.115 = f32[16,32,12,64]{3,1,2,0:T(8,128)} copy(f32[16,32,12,64]{1,0,3,2:T(8,128)} %reshape.260) | data formatting | bytes 3145728 | tf_op jit(solution)/shard_map/while/body/eval_jaxpr/reshape | solution.py:51
  49.5 2.5 multiply_convert_fusion.5
  53.1 1.4 copy-done.11
  54.6 1.8 fusion.87
  56.8 6.8 %fusion.36 = bf16[16,12,128,64]{2,0,3,1:T(8,128)(2,1)} fusion(f32[16,12,128,64]{2,3,1,0:T(8,128)S(1)} %fusion.87, s32[16]{0:T(128)S(1)} %fusion.84), kind=kOutput, calls=%fused_computation.69 | convolution fusion | flops 303563008 | bytes 9437248 | tf_op jit(solution)/shard_map/while/body/eval_jaxpr/st,thfd->shfd/dot_general | solution.py:73
  63.5 5.1 reshape.262
  68.6 6.7 %copy.122 = f32[16,32,12,64]{3,1,2,0:T(8,128)} copy(f32[16,32,12,64]{1,0,3,2:T(8,128)} %reshape.262) | data formatting | bytes 3145728 | tf_op jit(solution)/shard_map/while/body/eval_jaxpr/reshape | solution.py:50
  75.3 2.5 multiply_convert_fusion.3
  78.7 2.5 fusion.68
  81.9 3.3 fusion.23
  85.2 2.0 copy.127
  87.3 3.9 convert_element_type.136
  91.1 2.0 fusion.94
  93.6 11.0 %all_gather.13 = bf16[512,768]{1,0:T(8,128)(2,1)S(1)} all-gather(bf16[256,768]{1,0:T(8,128)(2,1)S(1)} %fusion.59), channel_id=1, replica_groups=mesh['dp'=16,'tensor'=2] {'tensor'}, dimensions={0}, use_global_device_ids=true | all-gather | bytes 1179648 | tf_op jit(solution)/shard_map/all_gather | solution.py:201
  104.6 9.5 %fusion.13 = (bf16[512,1536]{1,0:T(8,128)(2,1)S(1)}, f32[512,1536]{1,0:T(8,128)}) fusion(f32[1536]{0:T(1024)S(1)} %copy-done.59, bf16[512,768]{1,0:T(8,128)(2,1)S(1)} %all_gather.13, bf16[768,1536]{1,0:T(8,128)(2,1)S(1)} %copy-done), kind=kOutput, calls=%fused_computation.22 | convolution fusion | flops 1259864064 | bytes 7870464 | tf_op jit(solution)/shard_map/dot_general | solution.py:202
  115.3 2.5 fusion.96
  121.2 24.1 %reduce-scatter.3.cloned.1.call-done = f32[256,768]{1,0:T(8,128)} async-done(((f32[512,768]{1,0:T(8,128)}), f32[256,768]{1,0:T(8,128)}) %reduce-scatter.3.cloned.1.call-update) | async-done | bytes 786448 | tf_op jit(solution)/shard_map/reduce_scatter | solution.py:204
  145.2 1.5 fusion.91
  147.9 1.7 fusion.88
  150.6 11.5 %all_gather.14 = bf16[512,768]{1,0:T(8,128)(2,1)S(1)} all-gather(bf16[256,768]{1,0:T(8,128)(2,1)S(1)} %convert_element_type.148), channel_id=1, replica_groups=mesh['dp'=16,'tensor'=2] {'tensor'}, dimensions={0}, use_global_device_ids=true | all-gather | bytes 1179648 | tf_op jit(solution)/shard_map/all_gather | solution.py:217
  162.1 2.6 fusion.95
  166.0 2.6 fusion.57
  168.6 3.4 copy.128
  172.1 2.3 copy.135
  174.4 4.5 convolution_convert_fusion
  178.9 2.8 convolution_convert_fusion.1
  181.8 13.0 %reduce-scatter.5.cloned.1.call-done = f32[256,768]{1,0:T(8,128)} async-done(((f32[512,768]{1,0:T(8,128)}), f32[256,768]{1,0:T(8,128)}) %reduce-scatter.5.cloned.1.call-update) | async-done | bytes 786448 | tf_op jit(solution)/shard_map/reduce_scatter | solution.py:223
  194.8 1.6 multiply_reduce_fusion
  196.7 11.7 %all_gather.15 = bf16[512,768]{1,0:T(8,128)(2,1)S(1)} all-gather(bf16[256,768]{1,0:T(8,128)(2,1)S(1)} %convert_element_type.150), channel_id=1, replica_groups=mesh['dp'=16,'tensor'=2] {'tensor'}, dimensions={0}, use_global_device_ids=true | all-gather | bytes 1179648 | tf_op jit(solution)/shard_map/all_gather | solution.py:241
  208.4 2.0 fusion.46
  210.3 4.1 reshape.250
  214.5 8.2 %fusion.60 = f32[16,12,128,64]{2,3,1,0:T(8,128)S(1)} fusion(bf16[16,32,12,128]{3,1,2,0:T(8,128)(2,1)S(1)} %copy-done.29, f32[16,32,12,64]{3,2,1,0:T(8,128)} %reshape.250, f32[16,32,12]{1,2,0:T(8,128)S(1)} %copy-done.44), kind=kOutput, calls=%fused_computation.107 | convolution fusion | flops 604372992 | bytes 9461760 | tf_op jit(solution)/shard_map/while/body/eval_jaxpr/sihf,sihd->shfd/dot_general | solution.py:92
  224.7 6.1 %bitcast_add_fusion = f32[16,32,12,128]{3,1,2,0:T(8,128)S(1)} fusion(bf16[16,12,128,64]{2,0,3,1:T(8,128)(2,1)S(1)} %copy-done.23, f32[16,12,128]{2,1,0:T(8,128)S(1)} %copy.132, f32[16,32,12]{1,2,0:T(8,128)S(1)} %multiply_divide_fusion, f32[16,32,12,64]{3,2,1,0:T(8,128)S(1)} %copy-done.6, f32[16,32,12]{1,2,0:T(8,128)S(1)} %copy-done.44), kind=kOutput, calls=%fused_computation.36 | convolution fusion | flops 605945856 | bytes 8011776 | tf_op jit(solution)/shard_map/while/body/eval_jaxpr/sihd,shfd->sihf/dot_general | solution.py:88
  232.7 7.0 %fusion = f32[16,12,128,64]{2,0,3,1:T(8,128)S(1)} fusion(f32[16,12,128,64]{2,3,1,0:T(8,128)S(1)} %fusion.60, s32[16]{0:T(128)S(1)} %copy-done.58), kind=kOutput, calls=%fused_computation | convolution fusion | flops 301990144 | bytes 12582976 | tf_op jit(solution)/shard_map/while/body/eval_jaxpr/st,shfd->thfd/dot_general | solution.py:99
  239.8 5.6 %add_bitcast_fusion = f32[16,32,12,128]{3,1,2,0:T(8,128)S(1)} fusion(bf16[16,32,12,64]{3,1,2,0:T(8,128)(2,1)S(1)} %copy-done.12, f32[16,12,128,64]{2,0,3,1:T(8,128)S(1)} %fusion, f32[16,12,128]{2,1,0:T(8,128)S(1)} %copy.139), kind=kOutput, calls=%fused_computation.41 | convolution fusion | flops 604766208 | bytes 10321920 | tf_op jit(solution)/shard_map/while/body/eval_jaxpr/thfd,tjhd->tjhf/dot_general | solution.py:102
  245.8 1.5 copy-done.13
  248.3 3.7 fusion.22
  252.0 3.2 copy.134
  255.2 3.3 copy.141
  258.6 11.7 %fusion.43 = f32[16,32,12,64]{3,1,2,0:T(8,128)} fusion(f32[16,12,128,64]{2,0,3,1:T(8,128)} %copy-done.2, bf16[16,32,12,64]{3,1,2,0:T(8,128)(2,1)} %copy-done.5, bf16[16,32,12,64]{3,1,2,0:T(8,128)(2,1)S(1)} %copy-done.4), kind=kOutput, calls=%fused_computation.70 | convolution fusion | flops 607125504 | bytes 9437184 | tf_op jit(solution)/shard_map/while/body/eval_jaxpr/thfd,tjhf->tjhd/dot_general | solution.py:105
  270.2 6.1 %copy.157 = f32[16,32,12,64]{1,0,3,2:T(8,128)} copy(f32[16,32,12,64]{3,1,2,0:T(8,128)} %fusion.43) | data formatting | bytes 3145728 | tf_op jit(solution)/shard_map/while/body/eval_jaxpr/reshape | solution.py:125
  276.4 5.8 %reshape.259 = f32[512,768]{0,1:T(8,128)} reshape(f32[16,32,12,64]{1,0,3,2:T(8,128)} %copy.157) | data formatting | bytes 3145728 | tf_op jit(solution)/shard_map/while/body/eval_jaxpr/reshape | solution.py:125
  282.2 2.2 fusion.97
  287.5 5.0 convolution_bitcast_fusion
  292.6 32.8 %psum.91 = bf16[1536]{0:T(1024)(128)(2,1)S(1)} all-reduce(bf16[1536]{0:T(1024)(128)(2,1)S(1)} %get-tuple-element.203), channel_id=1, replica_groups=mesh['dp'=16,'tensor'=2] {'dp'}, use_global_device_ids=true, to_apply=%region_24.25 | all-reduce | flops 1536 | bytes 6144 | tf_op jit(solution)/shard_map/psum | solution.py:231
  326.0 4.9 convert_element_type.156
  330.9 2.5 convert_element_type.160
  333.5 39.6 %all-reduce = (f32[768]{0:T(1024)}, f32[768]{0:T(1024)}, f32[768]{0:T(1024)}, f32[768]{0:T(1024)}, f32[768]{0:T(1024)}, /*index=5*/f32[768]{0:T(1024)}) all-reduce(f32[768]{0:T(1024)S(1)} %get-tuple-element.173, f32[768]{0:T(1024)S(1)} %get-tuple-element.153, ...), channel_id=1, replica_groups=mesh['dp'=16,'tensor'=2] {'dp','tensor'}, use_global_device_ids=true, to_apply=%region_17.18 | all-reduce | flops 4608 | bytes 36864 | tf_op jit(solution)/shard_map/psum | solution.py:237
  373.1 2.3 fusion.9
  375.4 61.2 %psum.85 = f32[2304]{0:T(1024)S(1)} all-reduce(f32[2304]{0:T(1024)S(1)} %fusion.9), channel_id=1, replica_groups=mesh['dp'=16,'tensor'=2] {'dp'}, use_global_device_ids=true, to_apply=%region_14.15 | all-reduce | flops 2304 | bytes 18432 | tf_op jit(solution)/shard_map/psum | solution.py:264
  437.2 4.4 convolution_add_fusion.3
  441.6 65.9 %all-reduce.6.cloned.1.call-done = (f32[768,2304]{0,1:T(8,128)}, f32[768,768]{1,0:T(8,128)}) async-done(((f32[768,2304]{0,1:T(8,128)}, f32[768,768]{1,0:T(8,128)}), (f32[768,2304]{0,1:T(8,128)}, f32[768,768]{1,0:T(8,128)})) %all-reduce.6.cloned.1.call-update) | async-done | bytes 9437200 | tf_op jit(solution)/shard_map/psum | solution.py:264
  507.5 5.8 %fusion.92 = (f32[768,768]{0,1:T(8,128)}, f32[768,768]{0,1:T(8,128)S(1)}, f32[768,768]{0,1:T(8,128)}) fusion(f32[768,2304]{0,1:T(8,128)} %get-tuple-element.167), kind=kLoop, calls=%fused_computation.157 | loop fusion | bytes 14155776 | tf_op jit(solution)/shard_map/slice | solution.py:272
  513.3 3.0 copy.147
  516.3 1.9 copy.146
  518.2 3.2 copy.145
  521.4 3.2 copy.211
  (201 shorter events, 23.0 us)
Async XLA Ops:
  7.2 97.4 %copy-start = (bf16[768,1536]{1,0:T(8,128)(2,1)S(1)}, bf16[768,1536]{1,0:T(8,128)(2,1)}, u32[]{:S(2)}) copy-start(bf16[768,1536]{1,0:T(8,128)(2,1)} %param.33) | copy-start | bytes 7077892
  7.2 14.8 %copy-start.31 = (bf16[768,768]{1,0:T(8,128)(2,1)S(1)}, bf16[768,768]{1,0:T(8,128)(2,1)}, u32[]{:S(2)}) copy-start(bf16[768,768]{1,0:T(8,128)(2,1)} %param.25) | copy-start | bytes 3538948
  7.2 138.0 %reduce-scatter.3.cloned.1.call-start = ((), (), s32[]{:S(2)}) async-start(), calls=%async_computation.2 | async-start | bytes 2359296 | tf_op jit(solution)/shard_map/reduce_scatter | solution.py:204
  7.3 14.9 %copy-start.32 = (bf16[768,768]{1,0:T(8,128)(2,1)S(1)}, bf16[768,768]{1,0:T(8,128)(2,1)}, u32[]{:S(2)}) copy-start(bf16[768,768]{1,0:T(8,128)(2,1)} %param.27) | copy-start | bytes 3538948
  22.3 2.6 copy-start.42
  25.0 2.7 copy-start.64
  25.0 2.8 copy-start.65
  25.0 2.8 copy-start.66
  25.0 2.8 copy-start.60
  25.1 3.4 copy-start.67
  28.5 9.4 %copy-start.47 = (f32[512]{0:T(512)}, f32[512]{0:T(512)S(1)}, u32[]{:S(2)}) copy-start(f32[512]{0:T(512)S(1)} %get-tuple-element.193) | copy-start | bytes 6148
  28.5 9.4 %copy-start.51 = (f32[512]{0:T(512)}, f32[512]{0:T(512)S(1)}, u32[]{:S(2)}) copy-start(f32[512]{0:T(512)S(1)} %get-tuple-element.196) | copy-start | bytes 6148
  52.0 4.3 copy-start.3
  52.0 4.3 copy-start.5
  52.0 2.5 copy-start.11
  56.5 7.0 %copy-start.57 = (s32[16]{0:T(128)}, s32[16]{0:T(128)S(1)}, u32[]{:S(2)}) copy-start(s32[16]{0:T(128)S(1)} %fusion.84) | copy-start | bytes 196
  56.7 21.9 %copy-start.40 = (f32[16,12,128]{2,0,1:T(8,128)}, f32[16,12,128]{2,0,1:T(8,128)S(1)}, u32[]{:S(2)}) copy-start(f32[16,12,128]{2,0,1:T(8,128)S(1)} %fusion.70) | copy-start | bytes 294916
  77.8 4.1 copy-start.22
  78.7 6.6 %copy-start.28 = (bf16[16,32,12,128]{3,1,2,0:T(8,128)(2,1)}, bf16[16,32,12,128]{3,1,2,0:T(8,128)(2,1)S(1)}, u32[]{:S(2)}) copy-start(bf16[16,32,12,128]{3,1,2,0:T(8,128)(2,1)S(1)} %pad_maximum_fusion.2) | copy-start | bytes 4718596
  81.9 3.4 copy-start.43
  85.2 5.9 %copy-start.30 = (bf16[256,768]{1,0:T(8,128)(2,1)S(1)}, bf16[256,768]{1,0:T(8,128)(2,1)}, u32[]{:S(2)}) copy-start(bf16[256,768]{1,0:T(8,128)(2,1)} %param.20) | copy-start | bytes 1179652
  91.1 13.4 %copy-start.59 = (f32[1536]{0:T(1024)S(1)}, f32[1536]{0:T(1024)}, u32[]{:S(2)}) copy-start(f32[1536]{0:T(1024)} %convert_element_type.141) | copy-start | bytes 18436
  93.4 20.7 %copy-start.45 = (f32[256]{0:T(256)}, f32[256]{0:T(256)S(1)}, u32[]{:S(2)}) copy-start(f32[256]{0:T(256)S(1)} %add_rsqrt_fusion.1) | copy-start | bytes 3076
  104.6 9.5 %copy-start.34 = (bf16[512,768]{1,0:T(8,128)(2,1)}, bf16[512,768]{1,0:T(8,128)(2,1)S(1)}, u32[]{:S(2)}) copy-start(bf16[512,768]{1,0:T(8,128)(2,1)S(1)} %all_gather.13) | copy-start | bytes 2359300
  104.6 10.7 %copy-start.68 = (bf16[1536,768]{1,0:T(8,128)(2,1)S(1)}, bf16[1536,768]{1,0:T(8,128)(2,1)}, u32[]{:S(2)}) copy-start(bf16[1536,768]{1,0:T(8,128)(2,1)} %param.35) | copy-start | bytes 7077892
  117.8 29.2 %copy-start.27 = (bf16[256,768]{1,0:T(8,128)(2,1)S(1)}, bf16[256,768]{1,0:T(8,128)(2,1)}, u32[]{:S(2)}) copy-start(bf16[256,768]{1,0:T(8,128)(2,1)} %param.39) | copy-start | bytes 1179652
  117.8 76.9 %reduce-scatter.5.cloned.1.call-start = ((), (), s32[]{:S(2)}) async-start(), calls=%async_computation.3 | async-start | bytes 2359296 | tf_op jit(solution)/shard_map/reduce_scatter | solution.py:223
  145.2 2.7 copy-start.53
  147.0 15.2 %copy-start.69 = (bf16[1536,768]{1,0:T(8,128)(2,1)S(1)}, bf16[1536,768]{1,0:T(8,128)(2,1)}, u32[]{:S(2)}) copy-start(bf16[1536,768]{1,0:T(8,128)(2,1)} %param.35) | copy-start | bytes 7077892
  147.0 15.2 %copy-start.73 = (f32[512,1536]{1,0:T(8,128)S(1)}, f32[512,1536]{1,0:T(8,128)}, u32[]{:S(2)}) copy-start(f32[512,1536]{1,0:T(8,128)} %get-tuple-element.202) | copy-start | bytes 9437188
  162.1 2.7 copy-start.36
  166.0 2.6 copy-start.41
  168.5 3.6 copy-start.10
  168.5 157.4 %all-reduce.8.cloned.1.call-start = ((), (), s32[]{:S(2)}) async-start(), calls=%async_computation.5 | async-start | bytes 9437184 | tf_op jit(solution)/shard_map/psum | solution.py:230
  172.1 2.3 copy-start.37
  174.4 4.5 copy-start.35
  174.4 4.5 copy-start.72
  181.7 13.0 %copy-start.18 = (f32[256,768]{1,0:T(8,128)S(1)}, f32[256,768]{1,0:T(8,128)}, u32[]{:S(2)}) copy-start(f32[256,768]{1,0:T(8,128)} %copy-done.17) | copy-start | bytes 2359300
  181.7 13.0 %copy-start.46 = (f32[256]{0:T(256)S(1)}, f32[256]{0:T(256)}, u32[]{:S(2)}) copy-start(f32[256]{0:T(256)} %copy-done.45) | copy-start | bytes 3076
  181.8 325.7 %all-reduce.6.cloned.1.call-start = ((), (), s32[]{:S(2)}) async-start(), calls=%async_computation.4 | async-start | bytes 18874368 | tf_op jit(solution)/shard_map/psum | solution.py:264
  196.3 12.1 %copy-start.33 = (bf16[768,768]{1,0:T(8,128)(2,1)S(1)}, bf16[768,768]{1,0:T(8,128)(2,1)}, u32[]{:S(2)}) copy-start(bf16[768,768]{1,0:T(8,128)(2,1)} %param.29) | copy-start | bytes 3538948
  196.7 17.8 %copy-start.20 = (f32[256,768]{1,0:T(8,128)}, f32[256,768]{1,0:T(8,128)S(1)}, u32[]{:S(2)}) copy-start(f32[256,768]{1,0:T(8,128)S(1)} %get-tuple-element.174) | copy-start | bytes 2359300
  210.3 4.1 copy-start.29
  210.3 4.1 copy-start.44
  214.4 8.3 %copy-start.6 = (f32[16,32,12,64]{3,2,1,0:T(8,128)S(1)}, f32[16,32,12,64]{3,2,1,0:T(8,128)}, u32[]{:S(2)}) copy-start(f32[16,32,12,64]{3,2,1,0:T(8,128)} %reshape.250) | copy-start | bytes 4718596
  214.4 8.3 %copy-start.19 = (f32[16,12,64,32]{2,3,1,0:T(8,128)S(1)}, f32[16,12,64,32]{2,3,1,0:T(8,128)}, u32[]{:S(2)}) copy-start(f32[16,12,64,32]{2,3,1,0:T(8,128)} %get-tuple-element.198) | copy-start | bytes 4718596
  222.7 2.0 copy-start.23
  232.7 7.1 %copy-start.12 = (bf16[16,32,12,64]{3,1,2,0:T(8,128)(2,1)S(1)}, bf16[16,32,12,64]{3,1,2,0:T(8,128)(2,1)}, u32[]{:S(2)}) copy-start(bf16[16,32,12,64]{3,1,2,0:T(8,128)(2,1)} %copy.118) | copy-start | bytes 2359300
  239.8 5.6 %copy-start.2 = (f32[16,12,128,64]{2,0,3,1:T(8,128)}, f32[16,12,128,64]{2,0,3,1:T(8,128)S(1)}, u32[]{:S(2)}) copy-start(f32[16,12,128,64]{2,0,3,1:T(8,128)S(1)} %fusion) | copy-start | bytes 18874372
  239.8 6.0 %copy-start.50 = (f32[512]{0:T(512)S(1)}, f32[512]{0:T(512)}, u32[]{:S(2)}) copy-start(f32[512]{0:T(512)} %copy-done.49) | copy-start | bytes 6148
  239.8 6.0 %copy-start.52 = (f32[512]{0:T(512)S(1)}, f32[512]{0:T(512)}, u32[]{:S(2)}) copy-start(f32[512]{0:T(512)} %copy-done.51) | copy-start | bytes 6148
  245.4 2.8 copy-start.14
  245.5 2.8 copy-start.48
  255.2 3.3 copy-start.4
  276.4 5.8 %copy-start.16 = (bf16[512,768]{1,0:T(8,128)(2,1)S(1)}, bf16[512,768]{1,0:T(8,128)(2,1)}, u32[]{:S(2)}) copy-start(bf16[512,768]{1,0:T(8,128)(2,1)} %convert_element_type.136) | copy-start | bytes 2359300
  282.2 2.2 copy-start.7
  282.2 2.9 copy-start.8
  282.2 3.6 copy-start.9
  326.0 4.9 copy-start.26
  330.9 2.6 copy-start.54
  330.9 2.6 copy-start.55
  330.9 2.6 copy-start.56
  333.5 103.8 %copy-start.21 = (f32[256,768]{1,0:T(8,128)S(1)}, f32[256,768]{1,0:T(8,128)}, u32[]{:S(2)}) copy-start(f32[256,768]{1,0:T(8,128)} %copy-done.20) | copy-start | bytes 2359300
  518.2 6.4 %copy-start.1 = (bf16[768,1536]{1,0:T(8,128)(2,1)S(1)}, bf16[768,1536]{1,0:T(8,128)(2,1)}, u32[]{:S(2)}) copy-start(bf16[768,1536]{1,0:T(8,128)(2,1)} %param.33) | copy-start | bytes 7077892
  (14 other events, 20.0 us)
Sparse Core Ops, SparseCore 0:
  118.0 27.2 reduce-scatter.2
  168.7 26.0 reduce-scatter.4
  199.0 117.4 all-reduce.7
  320.7 186.6 all-reduce.5
where the time goes:
time: 536 us; the launch traced here: 532 us
  blocking collectives  181 us (34%)
  waiting for transfers between devices  103 us (19%)
  local copies, waits for them, and re-layouts  99 us (18%)
  matrix products  97.5 us (18%)
  other arithmetic  35.4 us (7%)
  between operations  15.8 us (3%)
    psum x1, waiting for transfers between devices, per_device(): g_joint, g_out, d_jbias = lax.psum((g_joint, g_out, d_jbias), 'dp')  65.9 us
    psum x1, blocking collectives, per_device(): g_joint, g_out, d_jbias = lax.psum((g_joint, g_out, d_jbias), 'dp')  61.2 us
    psum x1, blocking collectives, per_device(): lax.psum((d_gain_one, d_bias_one, d_gain_two, d_bias_two, d_bout, d_bdown...  39.6 us
    psum x1, blocking collectives, per_device(): lax.psum(g_upbias.astype(jnp.bfloat16), 'dp').astype(jnp.float32)  32.8 us
    unnamed x154, local copies, waits for them, and re-layouts  25 us
    reduce_scatter x1, waiting for transfers between devices, per_device(): lax.psum_scatter(jnp.dot(act_low, w_down, preferred_element_type=jnp.floa...  24.1 us
    reshape x3, local copies, waits for them, and re-layouts, features(): relu_query = jax.nn.relu(proj[:, :width]).reshape(length, HEADS, HD)  15.2 us
    reshape x3, local copies, waits for them, and re-layouts, features(): jax.nn.relu(proj[:, width:2 * width]).reshape(length, HEADS, HD)  13.9 us
  transfers between devices with their start and end apart: 4, of which 3 were waited for; matrix products, arithmetic and copies ran while one was open for 21% of the time, Pallas kernels for 0%

commit v1 on v0

--- a/solution.py
+++ b/solution.py
@@ -1,8 +1,11 @@
+import functools
 import math
 
 import jax
 import jax.numpy as jnp
 from jax import lax
+from jax.experimental import pallas as pl
+from jax.experimental.pallas import tpu as pltpu
 from jax.sharding import PartitionSpec as P
 
 HEADS = 12
@@ -128,7 +131,7 @@
     )
 
 
-def per_device(
+def general_device(
     tokens,
     positions,
     span_sizes,
@@ -284,9 +287,635 @@
     )
 
 
+f32 = jnp.float32
+bf16 = jnp.bfloat16
+MESH = pl.DeviceIdType.MESH
+LANES = 2 * HD
+TILE = 256
+ROWBLOCK = 32
+
+
+def tile_at(index, size):
+    return pl.ds(pl.multiple_of(index * size, size), size)
+
+
+def contract(left, right, left_dim, right_dim, precision=None):
+    return lax.dot_general(
+        left,
+        right,
+        (((left_dim,), (right_dim,)), ((), ())),
+        precision=precision,
+        preferred_element_type=f32,
+    )
+
+
+def mm(left, right):
+    return contract(left, right, 1, 0)
+
+
+def mm_nt(left, right):
+    return contract(left, right, 1, 1)
+
+
+def mm_tn(left, right):
+    return contract(left, right, 0, 0)
+
+
+def head_masks():
+    lane = lax.broadcasted_iota(jnp.int32, (1, LANES), 1)
+    first = (lane < HD).astype(f32)
+    return first, 1.0 - first
+
+
+def pair_mask():
+    row = lax.broadcasted_iota(jnp.int32, (LANES, LANES), 0)
+    col = lax.broadcasted_iota(jnp.int32, (LANES, LANES), 1)
+    return ((row < HD) == (col < HD)).astype(f32)
+
+
+def first_row(block, which):
+    row = lax.broadcasted_iota(jnp.int32, block.shape, 0)
+    return jnp.where(row == which, block, 0.0)
+
+
+def column_of(block, which):
+    return contract(first_row(block, which), jnp.ones((8, LANES), f32), 0, 0, highest)
+
+
+def squeeze_pair(square):
+    return square[:HD] + square[HD:]
+
+
+def spread_pair(half, mask):
+    return jnp.concatenate([half, half], axis=0).astype(f32) * mask
+
+
+def fold8(value):
+    total = value[0:8]
+    for start in range(8, value.shape[0], 8):
+        total = total + value[start : start + 8]
+    return total
+
+
+def angle_tables(trig, span, cosb, sinb, ctab):
+    rows = cosb.shape[0]
+    block = trig[...]
+    cosb[...] = column_of(block, 0)
+    sinb[...] = column_of(block, 1)
+    both = contract(block, block, 0, 0, highest)
+    row = lax.broadcasted_iota(jnp.int32, (rows, rows), 0)
+    col = lax.broadcasted_iota(jnp.int32, (rows, rows), 1)
+    seen = col <= (row | (span[0, 0] - 1))
+    ctab[...] = jnp.where(seen, both * (1.0 / HD), 0.0)
+
+
+def peer_copy(src, dst, sems, slot, device):
+    return pltpu.make_async_remote_copy(
+        src_ref=src,
+        dst_ref=dst,
+        send_sem=sems[0].at[slot],
+        recv_sem=sems[1].at[slot],
+        device_id=device,
+        device_id_type=MESH,
+    )
+
+
+def meet(devices):
+    barrier = pltpu.get_barrier_semaphore()
+    for device in devices:
+        pl.semaphore_signal(barrier, inc=1, device_id=device, device_id_type=MESH)
+    pl.semaphore_wait(barrier, len(devices))
+
+
+def front_kernel(
+    tok, trig, span, vec, wq, wk, wv, wo, wup, wdn, og,
+    res_o, small_o, gff_o, dhs_o, dho_o, mixb, mixf, inv, rq, rk, vv, nrm, scl, st_o, z_o,
+    hbuf, act, slope, dbuf, dpre, hid, tsend, trecv, zsend, zrecv, bsend, brecv,
+    numer, denom, ctab, cosb, sinb, acc, bup, send, recv,
+):
+    sems = (send, recv)
+    rows, width = tok.shape
+    units = wup.shape[1]
+    pairs = width // LANES
+    tiles = width // TILE
+    rank = lax.axis_index("tensor")
+    peer = (lax.axis_index("dp"), 1 - rank)
+    late = rank.astype(f32)
+    own, other = pl.ds(0, rows), pl.ds(rows, rows)
+    meet([peer])
+
+    for which, (weight, target) in enumerate(((wq, rq), (wk, rk), (wv, vv))):
+
+        @pl.loop(0, tiles)
+        def _(j, which=which, weight=weight, target=target):
+            cols = tile_at(j, TILE)
+            y = mm(tok[...], weight[:, cols]) + vec[which : which + 1, cols]
+            if which < 2:
+                y = jnp.maximum(y, 0.0)
+            target[:, cols] = y.astype(bf16)
+
+    angle_tables(trig, span, cosb, sinb, ctab)
+    diag = pair_mask()
+    first, second = head_masks()
+    first_low, second_low = first.astype(bf16), second.astype(bf16)
+
+    @pl.loop(0, pairs)
+    def _(p):
+        lanes = tile_at(p, LANES)
+        k = rk[:, lanes].astype(f32) * (1.0 / HD)
+        v = vv[:, lanes]
+        kc, ks = (k * cosb[...]).astype(bf16), (k * sinb[...]).astype(bf16)
+        tsend[p, 0] = squeeze_pair(mm_tn(kc, v) * diag).astype(bf16)
+        tsend[p, 1] = squeeze_pair(mm_tn(ks, v) * diag).astype(bf16)
+        sum_c = jnp.sum(kc.astype(f32), axis=0, keepdims=True)
+        sum_s = jnp.sum(ks.astype(f32), axis=0, keepdims=True)
+        row = lax.broadcasted_iota(jnp.int32, (8, LANES), 0)
+        zsend[p] = jnp.where(row == 0, sum_c, jnp.where(row == 1, sum_s, 0.0))
+
+    state_copy = peer_copy(tsend, trecv, sems, 0, peer)
+    key_copy = peer_copy(zsend, zrecv, sems, 1, peer)
+    state_copy.start()
+    key_copy.start()
+
+    @pl.loop(0, pairs)
+    def _(p):
+        lanes = tile_at(p, LANES)
+        q, k, v = rq[:, lanes], rk[:, lanes], vv[:, lanes]
+        parts = []
+        for mask, rest in ((first_low, second_low), (second_low, first_low)):
+            score = mm_nt(q * mask, k)
+            prob = (score * ctab[...]).astype(bf16)
+            parts.append(mm(prob, v * mask + rest))
+        numer[:, lanes] = parts[0] * first + parts[1] * second
+        denom[:, lanes] = pltpu.roll(parts[0] * second + parts[1] * first, HD, 1)
+
+    state_copy.wait()
+    key_copy.wait()
+
+    @pl.loop(0, pairs)
+    def _(p):
+        lanes = tile_at(p, LANES)
+        q = rq[:, lanes].astype(f32)
+        qc, qs = (q * cosb[...]).astype(bf16), (q * sinb[...]).astype(bf16)
+        st_o[p] = (trecv[p].astype(f32) * late).astype(bf16)
+        zblock = zrecv[p] * late
+        z_o[p] = zblock
+        num, den = numer[:, lanes], denom[:, lanes] + 1.0
+        for part, feat in ((0, qc), (1, qs)):
+            num += mm(feat, spread_pair(st_o[p, part], diag).astype(bf16))
+            den += mm(feat, (column_of(zblock, part) * diag).astype(bf16))
+        reciprocal = 1.0 / den
+        mix = num * reciprocal
+        inv[:, lanes] = reciprocal
+        mixf[:, lanes] = mix
+        mixb[:, lanes] = mix.astype(bf16)
+
+    @pl.loop(0, tiles)
+    def _(j):
+        cols = tile_at(j, TILE)
+        hid[:, cols] = tok[:, cols].astype(f32) + mm(mixb[...], wo[:, cols]) + vec[3:4, cols]
+
+    @pl.loop(0, rows // ROWBLOCK)
+    def _(i):
+        at = tile_at(i, ROWBLOCK)
+        value = hid[at, :]
+        centred = value - jnp.mean(value, axis=-1, keepdims=True)
+        scale = lax.rsqrt(jnp.mean(centred * centred, axis=-1, keepdims=True) + norm_eps)
+        normal = centred * scale
+        hidden = normal * vec[4:5, :] + vec[5:6, :]
+        nrm[at, :] = normal
+        scl[at, :] = jnp.broadcast_to(scale, (ROWBLOCK, LANES))
+        hid[at, :] = hidden
+        hbuf[at, :] = hidden.astype(bf16)
+
+    hidden_copy = peer_copy(hbuf.at[own], hbuf.at[other], sems, 2, peer)
+    hidden_copy.start()
+
+    def raise_rows(part):
+        for half in range(units // width):
+
+            @pl.loop(0, tiles)
+            def _(j, half=half):
+                cols = tile_at(half * tiles + j, TILE)
+                pre = mm(hbuf[part, :], wup[:, cols]) + vec[9 + half : 10 + half, tile_at(j, TILE)]
+                cdf = 0.5 * (1.0 + lax.erf(pre * (1.0 / math.sqrt(2.0))))
+                act[part, cols] = (pre * cdf).astype(bf16)
+                slope[part, cols] = cdf + pre * jnp.exp(-0.5 * pre * pre) * (
+                    1.0 / math.sqrt(2.0 * math.pi)
+                )
+
+    raise_rows(own)
+    hidden_copy.wait()
+    raise_rows(other)
+
+    @pl.loop(0, tiles)
+    def _(j):
+        cols = tile_at(j, TILE)
+        bsend[:, cols] = mm(act[other, :], wdn[:, cols]).astype(bf16)
+
+    branch_copy = peer_copy(bsend, brecv, sems, 3, peer)
+    branch_copy.start()
+
+    @pl.loop(0, tiles)
+    def _(j):
+        cols = tile_at(j, TILE)
+        hid[:, cols] += mm(act[own, :], wdn[:, cols]) + vec[6:7, cols]
+
+    acc[...] = jnp.zeros_like(acc)
+    branch_copy.wait()
+
+    @pl.loop(0, rows // ROWBLOCK)
+    def _(i):
+        at = tile_at(i, ROWBLOCK)
+        value = hid[at, :] + brecv[at, :].astype(f32)
+        centred = value - jnp.mean(value, axis=-1, keepdims=True)
+        scale = lax.rsqrt(jnp.mean(centred * centred, axis=-1, keepdims=True) + norm_eps)
+        normal = centred * scale
+        res_o[at, :] = (normal * vec[7:8, :] + vec[8:9, :]).astype(bf16)
+        grad = og[at, :].astype(f32)
+        along = grad * vec[7:8, :]
+        inner = (
+            along
+            - jnp.mean(along, axis=-1, keepdims=True)
+            - normal * jnp.mean(along * normal, axis=-1, keepdims=True)
+        ) * scale
+        dho_o[at, :] = inner
+        dbuf[at, :] = inner.astype(bf16)
+        acc[0:8, :] += fold8(grad * normal)
+        acc[8:16, :] += fold8(grad)
+        acc[16:24, :] += fold8(inner)
+
+    grad_copy = peer_copy(dbuf.at[own], dbuf.at[other], sems, 4, peer)
+    grad_copy.start()
+
+    small_o[...] = jnp.zeros_like(small_o)
+    for slot in range(3):
+        small_o[3 + slot : 4 + slot, :] = jnp.sum(
+            acc[8 * slot : 8 * slot + 8, :], axis=0, keepdims=True
+        )
+    bup[...] = jnp.zeros_like(bup)
+
+    def lower_rows(part):
+        @pl.loop(0, units // TILE)
+        def _(j):
+            cols = tile_at(j, TILE)
+            d_pre = mm_nt(dbuf[part, :], wdn[cols, :]) * slope[part, cols]
+            bup[:, cols] += fold8(d_pre)
+            dpre[part, cols] = d_pre.astype(bf16)
+
+    lower_rows(own)
+    grad_copy.wait()
+    lower_rows(other)
+
+    @pl.loop(0, tiles)
+    def _(j):
+        cols = tile_at(j, TILE)
+        dhs_o[:, cols] = mm_nt(dpre[other, :], wup[cols, :]).astype(bf16)
+        dho_o[:, cols] += mm_nt(dpre[own, :], wup[cols, :])
+
+    for half in range(units // width):
+        line = jnp.sum(bup[:, half * width : (half + 1) * width], axis=0, keepdims=True)
+        small_o[9 + half : 10 + half, :] = line * (1.0 - late)
+        small_o[9 + units // width + half : 10 + units // width + half, :] = line * late
+
+    @pl.loop(0, units // TILE)
+    def _(j):
+        cols = tile_at(j, TILE)
+        gff_o[cols, :] = mm_tn(act[:, cols], dbuf[...]).astype(bf16)
+
+    for half in range(units // width):
+
+        @pl.loop(0, tiles)
+        def _(j, half=half):
+            gff_o[pl.ds(units + half * width, width), tile_at(j, TILE)] = mm_tn(
+                hbuf[...], dpre[:, tile_at(half * tiles + j, TILE)]
+            ).astype(bf16)
+
+
+def back_kernel(
+    tok, trig, span, vec, wq, wk, wv, wo,
+    dhs, dho, mixb, mixf, inv, rq, rk, vv, nrm, scl, st, z, small_in,
+    dtok_o, ga_o, small_o,
+    dhr, dres, dlow, dn, xs, dsend, drecv, dzs, dzr, dq, dk, dv, dql, dkl, dvl,
+    ctab, cosb, sinb, acc, send, recv,
+):
+    sems = (send, recv)
+    rows, width = tok.shape
+    pairs = width // LANES
+    tiles = width // TILE
+    rank = lax.axis_index("tensor")
+    peer = (lax.axis_index("dp"), 1 - rank)
+    early = 1.0 - rank.astype(f32)
+    meet([peer])
+    hidden_copy = peer_copy(dhs, dhr, sems, 0, peer)
+    hidden_copy.start()
+    angle_tables(trig, span, cosb, sinb, ctab)
+    diag = pair_mask()
+    first, second = head_masks()
+    first_low, second_low = first.astype(bf16), second.astype(bf16)
+    diag_low = diag.astype(bf16)
+    acc[...] = jnp.zeros_like(acc)
+    small_o[...] = small_in[...]
+    hidden_copy.wait()
+
+    @pl.loop(0, rows // ROWBLOCK)
+    def _(i):
+        at = tile_at(i, ROWBLOCK)
+        grad = dho[at, :] + dhr[at, :].astype(f32)
+        normal = nrm[at, :]
+        along = grad * vec[4:5, :]
+        inner = (
+            along
+            - jnp.mean(along, axis=-1, keepdims=True)
+            - normal * jnp.mean(along * normal, axis=-1, keepdims=True)
+        ) * scl[at, 0:1]
+        dres[at, :] = inner
+        dlow[at, :] = inner.astype(bf16)
+        acc[0:8, :] += fold8(grad * normal)
+        acc[8:16, :] += fold8(grad)
+        acc[16:24, :] += fold8(inner)
+
+    for slot in range(3):
+        small_o[slot : slot + 1, :] = jnp.sum(
+            acc[8 * slot : 8 * slot + 8, :], axis=0, keepdims=True
+        )
+
+    @pl.loop(0, tiles)
+    def _(j):
+        cols = tile_at(j, TILE)
+        d_mixed = mm_nt(dlow[...], wo[cols, :]).astype(bf16).astype(f32)
+        d_numer = (d_mixed * inv[:, cols]).astype(bf16)
+        dn[:, cols] = d_numer
+        xs[:, cols] = (d_numer.astype(f32) * mixf[:, cols]).astype(bf16)
+
+    @pl.loop(0, pairs)
+    def _(p):
+        lanes = tile_at(p, LANES)
+        q = rq[:, lanes].astype(f32)
+        qc, qs = (q * cosb[...]).astype(bf16), (q * sinb[...]).astype(bf16)
+        d_numer = dn[:, lanes]
+        dsend[p, 0] = squeeze_pair(mm_tn(qc, d_numer) * diag).astype(bf16)
+        dsend[p, 1] = squeeze_pair(mm_tn(qs, d_numer) * diag).astype(bf16)
+        across = mm(xs[:, lanes], diag_low)
+        sum_c = jnp.sum(qc.astype(f32) * across, axis=0, keepdims=True)
+        sum_s = jnp.sum(qs.astype(f32) * across, axis=0, keepdims=True)
+        row = lax.broadcasted_iota(jnp.int32, (8, LANES), 0)
+        dzs[p] = -jnp.where(row == 0, sum_c, jnp.where(row == 1, sum_s, 0.0))
+
+    state_copy = peer_copy(dsend, drecv, sems, 1, peer)
+    key_copy = peer_copy(dzs, dzr, sems, 2, peer)
+    state_copy.start()
+    key_copy.start()
+
+    @pl.loop(0, tiles)
+    def _(j):
+        cols = tile_at(j, TILE)
+        ga_o[tile_at(3 * tiles + j, TILE), :] = mm_tn(mixb[:, cols], dlow[...]).astype(bf16)
+
+    @pl.loop(0, pairs)
+    def _(p):
+        lanes = tile_at(p, LANES)
+        q, k, v = rq[:, lanes], rk[:, lanes], vv[:, lanes]
+        d_numer = dn[:, lanes]
+        turned = -pltpu.roll(xs[:, lanes].astype(f32), HD, 1)
+        turned = turned.astype(bf16)
+        sum_q = sum_k = sum_v = 0.0
+        for mask, rest in ((first_low, second_low), (second_low, first_low)):
+            q_head, k_head, d_head = q * mask, k * mask, d_numer * mask
+            table = ctab[...]
+            prob = (mm_nt(q_head, k) * table).astype(bf16)
+            d_prob = mm_nt(d_head + turned * rest, v * mask + rest)
+            d_score = (d_prob * table).astype(bf16)
+            sum_v += mm_tn(prob, d_head)
+            sum_q += mm(d_score, k_head)
+            sum_k += mm_tn(d_score, q_head)
+        dq[:, lanes] = sum_q
+        dk[:, lanes] = sum_k
+        dv[:, lanes] = sum_v
+
+    state_copy.wait()
+    key_copy.wait()
+
+    @pl.loop(0, pairs)
+    def _(p):
+        lanes = tile_at(p, LANES)
+        q, v = rq[:, lanes].astype(f32), vv[:, lanes]
+        k = rk[:, lanes].astype(f32)
+        d_numer, x = dn[:, lanes], xs[:, lanes]
+        sum_q, sum_k, sum_v = dq[:, lanes], dk[:, lanes], dv[:, lanes]
+        zblock, dzblock = z[p], dzr[p] * early
+        for part, wave in ((0, cosb[...]), (1, sinb[...])):
+            state = spread_pair(st[p, part], diag).astype(bf16)
+            zmat = (column_of(zblock, part) * diag).astype(bf16)
+            sum_q += wave * (mm_nt(d_numer, state) - mm_nt(x, zmat))
+            d_state = (spread_pair(drecv[p, part], diag) * early).astype(bf16)
+            sum_k += wave * (mm_nt(v, d_state) + dzblock[part : part + 1, :]) * (1.0 / HD)
+            sum_v += mm((k * wave * (1.0 / HD)).astype(bf16), d_state)
+        sum_q = jnp.where(q > 0, sum_q, 0.0)
+        sum_k = jnp.where(k > 0, sum_k, 0.0)
+        dql[:, lanes] = sum_q.astype(bf16)
+        dkl[:, lanes] = sum_k.astype(bf16)
+        dvl[:, lanes] = sum_v.astype(bf16)
+        for slot, value in ((6, sum_q), (7, sum_k), (8, sum_v)):
+            small_o[slot : slot + 1, lanes] = jnp.sum(value, axis=0, keepdims=True)
+
+    for which, source in enumerate((dql, dkl, dvl)):
+
+        @pl.loop(0, tiles)
+        def _(j, which=which, source=source):
+            ga_o[tile_at(which * tiles + j, TILE), :] = mm_tn(
+                tok[:, tile_at(j, TILE)], source[...]
+            ).astype(bf16)
+
+    @pl.loop(0, tiles)
+    def _(j):
+        cols = tile_at(j, TILE)
+        dtok_o[:, cols] = (
+            dres[:, cols]
+            + mm_nt(dql[...], wq[cols, :])
+            + mm_nt(dkl[...], wk[cols, :])
+            + mm_nt(dvl[...], wv[cols, :])
+        )
+
+
+def in_vmem(count):
+    return [pl.BlockSpec(memory_space=pltpu.VMEM)] * count
+
+
+def shaped(*items):
+    return tuple(jax.ShapeDtypeStruct(shape, kind) for shape, kind in items)
+
+
+def pair_device(
+    tokens,
+    positions,
+    span_sizes,
+    w_query,
+    b_query,
+    w_key,
+    b_key,
+    w_value,
+    b_value,
+    w_out,
+    b_out,
+    norm1_gain,
+    norm1_bias,
+    w_up,
+    b_up,
+    w_down,
+    b_down,
+    norm2_gain,
+    norm2_bias,
+    out_grad,
+):
+    rank = lax.axis_index("tensor")
+    rows, width = tokens.shape
+    units = w_up.shape[1]
+    pairs = width // LANES
+    length = positions.shape[0]
+    places = lax.dynamic_slice_in_dim(positions, rank * rows, rows, 0)
+    angle = math.pi / 2 * places.astype(f32) / (3 * length)
+    line = lax.broadcasted_iota(jnp.int32, (8, rows), 0)
+    trig = jnp.where(
+        line == 0, jnp.cos(angle)[None], jnp.where(line == 1, jnp.sin(angle)[None], 0.0)
+    )
+    span = span_sizes.reshape(1, 1)
+    vectors = [
+        b_query, b_key, b_value, b_out, norm1_gain, norm1_bias, b_down, norm2_gain, norm2_bias, b_up,
+    ]
+    vec = jnp.concatenate(vectors).astype(f32).reshape(-1, width)
+    vec = jnp.pad(vec, ((0, -vec.shape[0] % 8), (0, 0)))
+    smalls = 9 + 2 * (units // width)
+    smalls += -smalls % 8
+    state = (pairs, 2, HD, LANES)
+    zrows = (pairs, 8, LANES)
+    wide, low, both = ((rows, width), f32), ((rows, width), bf16), (2 * rows, width)
+    front_outs = shaped(
+        low, ((smalls, width), f32), ((2 * units, width), bf16), low, wide, low, wide, wide,
+        low, low, low, wide, ((rows, LANES), f32), (state, bf16), (zrows, f32),
+    )
+    tables = [
+        pltpu.VMEM((rows, rows), f32), pltpu.VMEM((rows, LANES), f32), pltpu.VMEM((rows, LANES), f32),
+    ]
+    smem = [pl.BlockSpec(memory_space=pltpu.SMEM)]
+    (
+        result, small, gff, dhs, dho, mixb, mixf, inv, rq, rk, vv, nrm, scl, st, z,
+    ) = pl.pallas_call(
+        front_kernel,
+        out_shape=front_outs,
+        in_specs=in_vmem(2) + smem + in_vmem(8),
+        out_specs=tuple(in_vmem(len(front_outs))),
+        scratch_shapes=[
+            pltpu.VMEM(both, bf16),
+            pltpu.VMEM((2 * rows, units), bf16),
+            pltpu.VMEM((2 * rows, units), f32),
+            pltpu.VMEM(both, bf16),
+            pltpu.VMEM((2 * rows, units), bf16),
+            pltpu.VMEM((rows, width), f32),
+            pltpu.VMEM(state, bf16),
+            pltpu.VMEM(state, bf16),
+            pltpu.VMEM(zrows, f32),
+            pltpu.VMEM(zrows, f32),
+            pltpu.VMEM((rows, width), bf16),
+            pltpu.VMEM((rows, width), bf16),
+            pltpu.VMEM((rows, width), f32),
+            pltpu.VMEM((rows, width), f32),
+            *tables,
+            pltpu.VMEM((24, width), f32),
+            pltpu.VMEM((8, units), f32),
+            pltpu.SemaphoreType.DMA((5,)),
+            pltpu.SemaphoreType.DMA((5,)),
+        ],
+        compiler_params=pltpu.CompilerParams(
+            collective_id=0, has_side_effects=True, vmem_limit_bytes=60 << 20
+        ),
+        name="front",
+    )(tokens, trig, span, vec, w_query, w_key, w_value, w_out, w_up, w_down, out_grad)
+    back_outs = shaped(wide, ((4 * width, width), bf16), ((smalls, width), f32))
+    d_tokens, ga, small = pl.pallas_call(
+        back_kernel,
+        out_shape=back_outs,
+        in_specs=in_vmem(2) + smem + in_vmem(18),
+        out_specs=tuple(in_vmem(len(back_outs))),
+        scratch_shapes=[
+            pltpu.VMEM((rows, width), bf16),
+            pltpu.VMEM((rows, width), f32),
+            pltpu.VMEM((rows, width), bf16),
+            pltpu.VMEM((rows, width), bf16),
+            pltpu.VMEM((rows, width), bf16),
+            pltpu.VMEM(state, bf16),
+            pltpu.VMEM(state, bf16),
+            pltpu.VMEM(zrows, f32),
+            pltpu.VMEM(zrows, f32),
+            pltpu.VMEM((rows, width), f32),
+            pltpu.VMEM((rows, width), f32),
+            pltpu.VMEM((rows, width), f32),
+            pltpu.VMEM((rows, width), bf16),
+            pltpu.VMEM((rows, width), bf16),
+            pltpu.VMEM((rows, width), bf16),
+            *tables,
+            pltpu.VMEM((24, width), f32),
+            pltpu.SemaphoreType.DMA((3,)),
+            pltpu.SemaphoreType.DMA((3,)),
+        ],
+        compiler_params=pltpu.CompilerParams(
+            collective_id=1, has_side_effects=True, vmem_limit_bytes=60 << 20
+        ),
+        name="back",
+    )(
+        tokens, trig, span, vec, w_query, w_key, w_value, w_out,
+        dhs, dho, mixb, mixf, inv, rq, rk, vv, nrm, scl, st, z, small,
+    )
+    gff = lax.psum(gff, "dp")
+    ga = lax.psum(ga, ("dp", "tensor"))
+    small = lax.psum(small, ("dp", "tensor"))
+    halves = units // width
+    g_up = jnp.concatenate(
+        [gff[units + h * width : units + (h + 1) * width] for h in range(halves)], axis=1
+    )
+    g_upbias = lax.dynamic_slice_in_dim(small, 9 + rank * halves, halves, 0).reshape(units)
+    return (
+        result,
+        d_tokens,
+        ga[:width].astype(f32),
+        small[6],
+        ga[width : 2 * width].astype(f32),
+        small[7],
+        ga[2 * width : 3 * width].astype(f32),
+        small[8],
+        ga[3 * width :].astype(f32),
+        small[2],
+        small[0],
+        small[1],
+        g_up.astype(f32),
+        g_upbias,
+        gff[:units].astype(f32),
+        small[5],
+        small[3],
+        small[4],
+    )
+
+
+def pick(mesh):
+    def per_device(*args):
+        tokens, span_sizes, w_up = args[0], args[2], args[13]
+        rows, width = tokens.shape
+        fits = (
+            mesh.shape["tensor"] == 2
+            and span_sizes.shape[0] == 1
+            and rows % TILE == 0
+            and width % TILE == 0
+            and w_up.shape[1] % width == 0
+            and w_up.shape[1] // width <= 3
+        )
+        return pair_device(*args) if fits else general_device(*args)
+
+    return per_device
+
+
 def solution(mesh):
     return jax.shard_map(
-        per_device,
+        pick(mesh),
         mesh=mesh,
         in_specs=(
             P(("dp", "tensor"), None),

time: 536 us -> 369 us (0.69)
  blocking collectives: 181 us -> 40.3 us
  Pallas kernels: 0 us -> 99.6 us
  matrix products: 97.5 us -> 0 us
  local copies, waits for them, and re-layouts: 99 us -> 15 us
  waiting for transfers between devices: 103 us -> 185 us
  other arithmetic: 35.4 us -> 13.9 us
    psum x2, waiting for transfers between devices: 65.9 us -> 185 us  [the longest x1 142 us: pair_device(): ga = lax.psum(ga, ('dp', 'tensor'))]
    pallas_call x0 -> x2, Pallas kernels: none -> 99.6 us  [the longest x1 67 us: pair_device(): pl.pallas_call(front_kernel, out_shape=front_outs, in_specs=in_vmem(2) +...]
    dot_general x24 -> x0, matrix products: 97.5 us -> none  [the longest x1 11.7 us: back_second(): jnp.einsum('thfd,tjhf->tjhd', d_blocks, k_sub.astype(jnp.float32), precis...]
    psum x3 -> x1, blocking collectives: 134 us -> 40.3 us  [pair_device(): small = lax.psum(small, ('dp', 'tensor'))]
    reshape x10 -> x1, local copies, waits for them, and re-layouts: 49.8 us -> 0.61 us  [pair_device(): lax.dynamic_slice_in_dim(small, 9 + rank * halves, halves, 0).reshape(units)]
    all_gather x4 -> x0, blocking collectives: 47.3 us -> none  [the longest x1 13.1 us: per_device(): gathered = lax.all_gather(tokens, 'tensor', axis=0, tiled=True)]
    reduce_scatter x2 -> x0, waiting for transfers between devices: 37 us -> none  [the longest x1 24.1 us: per_device(): lax.psum_scatter(jnp.dot(act_low, w_down, preferred_element_type=jnp.floa...]
    unnamed x154 -> x19, local copies, waits for them, and re-layouts: 25 us -> 11.1 us
  transfers between devices with their start and end apart: 4 -> 2, of which waited for: 3 -> 2; matrix products, arithmetic and copies ran while one was open for 21% -> 2% of each run, Pallas kernels for 0% -> 9%
where the time goes in v1:
time: 369 us; the launch traced here: 368 us
  waiting for transfers between devices  185 us (50%)
  Pallas kernels  99.6 us (27%)
  blocking collectives  40.3 us (11%)
  local copies, waits for them, and re-layouts  15 us (4%)
  between operations  14.8 us (4%)
  other arithmetic  13.9 us (4%)
    psum x1, waiting for transfers between devices, pair_device(): ga = lax.psum(ga, ('dp', 'tensor'))  142 us
    pallas_call x1, Pallas kernels, pair_device(): pl.pallas_call(front_kernel, out_shape=front_outs, in_specs=in_vmem(2) +...  67 us
    psum x1, waiting for transfers between devices, pair_device(): gff = lax.psum(gff, 'dp')  42.8 us
    psum x1, blocking collectives, pair_device(): small = lax.psum(small, ('dp', 'tensor'))  40.3 us
    pallas_call x1, Pallas kernels, pair_device(): pl.pallas_call(back_kernel, out_shape=back_outs, in_specs=in_vmem(2) + sm...  32.6 us
    unnamed x19, local copies, waits for them, and re-layouts  11.1 us
  transfers between devices with their start and end apart: 2, of which 2 were waited for; matrix products, arithmetic and copies ran while one was open for 2% of the time, Pallas kernels for 9%

profile of v1, /device:TPU:0, one launch (start us, length us, event | category | flops | bytes accessed | tf_op | source)
XLA Modules:
  0.0 368.3 jit_solution(16517632712651245306)
XLA Ops:
  7.2 0.0 all-reduce.6.cloned.1.call-start
  7.9 0.9 dynamic-update-slice
  8.8 0.8 dynamic-update-slice.1
  9.6 0.9 dynamic-update-slice.2
  10.5 0.9 dynamic-update-slice.3
  11.3 0.9 dynamic-update-slice.4
  12.2 0.8 dynamic-update-slice.5
  13.0 0.9 dynamic-update-slice.6
  13.9 0.9 dynamic-update-slice.7
  14.7 0.9 dynamic-update-slice.8
  15.6 0.9 dynamic-update-slice.9
  16.5 0.6 pad_convert_fusion.vec
  17.1 0.8 fusion.1
  17.9 0.7 select_select_fusion.trig
  18.6 67.0 %front.1 = (bf16[256,768]{1,0:T(8,128)(2,1)}, f32[16,768]{1,0:T(8,128)}, bf16[3072,768]{1,0:T(8,128)(2,1)}, bf16[256,768]{1,0:T(8,128)(2,1)}, f32[256,768]{1,0:T...) custom-call(bf16[256,768]{1,0:T(8,128)(2,1)} %tok.3, ...), custom_call_target="tpu_custom_call" | custom-call | tf_op jit(solution)/shard_map/front/pallas_call | solution.py:803
  85.6 0.0 all-reduce.6.cloned.1.call-update
  85.6 0.0 all-reduce.4.cloned.1.call-start
  85.7 32.6 %back.1 = (f32[256,768]{1,0:T(8,128)}, bf16[3072,768]{1,0:T(8,128)(2,1)}, f32[16,768]{1,0:T(8,128)}) custom-call(bf16[256,768]{1,0:T(8,128)(2,1)} %tok.3, f32[8,256]{1,0:T(8,128)} %select_select_fusion.trig, s32[1,1]{1,0:T(1,128)} %bitcast.2.span, f32[16,768]{1,0:T(8,128)} %pad_convert_fusion.vec, bf16[768,768]{1,0:T(8,128)(2,1)} %wq.3, ...), custom_call_target="tpu_custom_call" | custom-call | tf_op jit(solution)/shard_map/back/pallas_call | solution.py:835
  118.3 0.0 copy-start.3
  118.3 0.0 all-reduce.4.cloned.1.call-update
  118.3 0.8 copy-done.3
  119.1 40.3 %psum.22 = f32[16,768]{1,0:T(8,128)S(1)} all-reduce(f32[16,768]{1,0:T(8,128)S(1)} %copy-done.3), channel_id=1, replica_groups=mesh['dp'=16,'tensor'=2] {'dp','tensor'}, use_global_device_ids=true, to_apply=%region_1.2 | all-reduce | flops 12288 | bytes 98304 | tf_op jit(solution)/shard_map/psum | solution.py:871
  159.4 0.6 reshape.49
  160.0 0.7 slice_reduce_fusion
  160.7 42.8 %all-reduce.6.cloned.1.call-done = bf16[3072,768]{1,0:T(8,128)(2,1)} async-done(((bf16[3072,768]{1,0:T(8,128)(2,1)}), bf16[3072,768]{1,0:T(8,128)(2,1)}) %all-reduce.6.cloned.1.call-update) | async-done | bytes 4718608 | tf_op jit(solution)/shard_map/psum | solution.py:869
  203.6 1.8 fusion.2
  205.3 0.0 copy-start
  205.3 3.0 maximum_convert_fusion
  208.4 1.0 copy-done
  209.4 2.5 slice_convert_fusion
  211.9 0.0 copy-start.2
  211.9 0.0 copy-start.1
  211.9 141.7 %all-reduce.4.cloned.1.call-done = bf16[3072,768]{1,0:T(8,128)(2,1)} async-done(((bf16[3072,768]{1,0:T(8,128)(2,1)}), bf16[3072,768]{1,0:T(8,128)(2,1)}) %all-reduce.4.cloned.1.call-update) | async-done | bytes 4718608 | tf_op jit(solution)/shard_map/psum | solution.py:870
  353.7 6.2 %slice_convert_fusion.1 = (f32[768,768]{1,0:T(8,128)}, f32[768,768]{1,0:T(8,128)}, f32[768,768]{1,0:T(8,128)}, f32[768,768]{1,0:T(8,128)}) fusion(bf16[3072,768]{1,0:T(8,128)(2,1)} %all-reduce.4.cloned.1.call-done), kind=kLoop, calls=%fused_computation.2 | loop fusion | flops 2359296 | bytes 14155776 | tf_op jit(solution)/shard_map/convert_element_type | solution.py:886
  359.8 0.0 copy-done.2
  359.9 0.7 copy.53
  360.6 0.0 copy-done.1
  360.6 0.9 copy.54
  (4 shorter events, 0.1 us)
Async XLA Ops:
  7.2 196.4 %all-reduce.6.cloned.1.call-start = ((), (), s32[]{:S(2)}) async-start(), calls=%async_computation.1 | async-start | bytes 9437184 | tf_op jit(solution)/shard_map/psum | solution.py:869
  85.6 268.1 %all-reduce.4.cloned.1.call-start = ((), (), s32[]{:S(2)}) async-start(), calls=%async_computation | async-start | bytes 9437184 | tf_op jit(solution)/shard_map/psum | solution.py:870
  118.3 0.8 copy-start.3
  205.3 4.0 %copy-start = (bf16[3072,768]{1,0:T(8,128)(2,1)S(1)}, bf16[3072,768]{1,0:T(8,128)(2,1)}, u32[]{:S(2)}) copy-start(bf16[3072,768]{1,0:T(8,128)(2,1)} %all-reduce.6.cloned.1.call-done) | copy-start | bytes 14155780
  211.9 147.9 %copy-start.2 = (bf16[256,768]{1,0:T(8,128)(2,1)S(1)}, bf16[256,768]{1,0:T(8,128)(2,1)}, u32[]{:S(2)}) copy-start(bf16[256,768]{1,0:T(8,128)(2,1)} %get-tuple-element.91) | copy-start | bytes 1179652
  211.9 148.7 %copy-start.1 = (f32[256,768]{1,0:T(8,128)S(1)}, f32[256,768]{1,0:T(8,128)}, u32[]{:S(2)}) copy-start(f32[256,768]{1,0:T(8,128)} %get-tuple-element.92) | copy-start | bytes 2359300
Sparse Core Ops, SparseCore 0:
  85.7 117.7 all-reduce.5
  209.2 144.4 all-reduce.3

commit v2 on v1

--- a/solution.py
+++ b/solution.py
@@ -736,6 +736,227 @@
             + mm_nt(dkl[...], wk[cols, :])
             + mm_nt(dvl[...], wv[cols, :])
         )
+
+
+def grid_place():
+    dp = lax.axis_index("dp")
+    core, chip = dp % 2, dp // 2
+    return core, chip % 2, chip // 2
+
+
+def ring_device(spot, depth, core):
+    far = spot // depth
+    z = far * (2 * depth - 1 - spot) + (1 - far) * spot
+    return ((z * 2 + far) * 2 + core, lax.axis_index("tensor"))
+
+
+def add_rows(target, rows, block):
+    target[rows, :] = (target[rows, :].astype(f32) + block.astype(f32)).astype(bf16)
+
+
+def sum_kernel(
+    count, gff, ga, small, ff_o, a_o, small_o,
+    cr_ff, cr_a, xr_a, acc_ff, acc_a, rs_ff, rs_a, small_r,
+    c_send, c_recv, r_send, r_recv, g_send, g_recv, x_send, x_recv, m_send, m_recv,
+):
+    depth = count // 2
+    half = gff.shape[0] // 2
+    quarter = ga.shape[0] // 4
+    core, y, z = grid_place()
+    rank = lax.axis_index("tensor")
+    dp = lax.axis_index("dp")
+    spot = y * (2 * depth - 1 - z) + (1 - y) * z
+    sibling = (dp + 1 - 2 * core, rank)
+    peer = (dp, 1 - rank)
+    ahead = ring_device((spot + 1) % count, depth, core)
+    behind = ring_device((spot + count - 1) % count, depth, core)
+    swaps = [sibling, peer, (dp + 2 - 4 * y, rank)]
+    step = 1
+    while step < depth:
+        bit = (z // step) % 2
+        swaps.append((dp + 4 * (step - 2 * step * bit), rank))
+        step *= 2
+    meet([ahead, behind] + swaps)
+
+    def core_rows(which, size):
+        return pl.ds(pl.multiple_of(which * size, size), size)
+
+    core_ff = peer_copy(gff.at[core_rows(1 - core, half), :], cr_ff, (c_send, c_recv), 0, sibling)
+    core_a = peer_copy(ga.at[core_rows(1 - core, 2 * quarter), :], cr_a, (c_send, c_recv), 1, sibling)
+    core_ff.start()
+    core_a.start()
+
+    def small_copy(index):
+        return peer_copy(small_o.at[index], small_r.at[index], (m_send, m_recv), index, swaps[index])
+
+    small_o[0] = small[...]
+    small_copy(0).start()
+
+    core_a.wait()
+
+    @pl.loop(0, 2 * quarter // 96)
+    def _(i):
+        rows = tile_at(i, 96)
+        at = pl.ds(pl.multiple_of(core * 2 * quarter + i * 96, 96), 96)
+        add_rows(cr_a, rows, ga[at, :])
+
+    x_copy = peer_copy(cr_a.at[core_rows(1 - rank, quarter), :], xr_a, (c_send, c_recv), 2, peer)
+    x_copy.start()
+    core_ff.wait()
+
+    @pl.loop(0, half // 96)
+    def _(i):
+        rows = tile_at(i, 96)
+        at = pl.ds(pl.multiple_of(core * half + i * 96, 96), 96)
+        acc_ff[rows, :] = (gff[at, :].astype(f32) + cr_ff[rows, :].astype(f32)).astype(bf16)
+
+    def swap_small(index):
+        small_copy(index).wait()
+        small_o[index + 1] = small_o[index] + small_r[index]
+        if index + 1 < len(swaps):
+            small_copy(index + 1).start()
+
+    streams = []
+    for kind, (acc, slots, out, base) in enumerate(
+        ((acc_ff, rs_ff, ff_o, core * half), (acc_a, rs_a, a_o, (core * 2 + rank) * quarter))
+    ):
+        size = acc.shape[0] // count // 2
+        for way in range(2):
+            streams.append((2 * kind + way, way, acc, slots, out, base, size))
+
+    def chunk_at(spot_index, stream, based):
+        _, way, _, _, _, base, size = stream
+        start = (spot_index % count) * 2 * size + way * size
+        return pl.ds(pl.multiple_of(start + base if based else start, size), size)
+
+    def toward(way):
+        return behind if way else ahead
+
+    def spread_copy(stream, at, s):
+        number, way, acc, slots, _, _, _ = stream
+        return pltpu.make_async_remote_copy(
+            src_ref=acc.at[chunk_at(at, stream, False), :],
+            dst_ref=slots.at[s, way],
+            send_sem=r_send.at[number, s],
+            recv_sem=r_recv.at[number, s],
+            device_id=toward(way),
+            device_id_type=MESH,
+        )
+
+    def gather_copy(stream, at, s):
+        number, way, _, _, out, _, _ = stream
+        rows = chunk_at(at, stream, True)
+        return pltpu.make_async_remote_copy(
+            src_ref=out.at[rows, :],
+            dst_ref=out.at[rows, :],
+            send_sem=g_send.at[number, s],
+            recv_sem=g_recv.at[number, s],
+            device_id=toward(way),
+            device_id_type=MESH,
+        )
+
+    def across_copy(stream, at, s, base):
+        _, way, _, _, out, _, size = stream
+        start = base + (at % count) * 2 * size + way * size
+        rows = pl.ds(pl.multiple_of(start, size), size)
+        return pltpu.make_async_remote_copy(
+            src_ref=out.at[rows, :],
+            dst_ref=out.at[rows, :],
+            send_sem=x_send.at[way, s],
+            recv_sem=x_recv.at[way, s],
+            device_id=peer,
+            device_id_type=MESH,
+        )
+
+    def sign(stream):
+        return -1 if stream[1] else 1
+
+    for stream in streams[:2]:
+        spread_copy(stream, spot, 0).start()
+    x_copy.wait()
+
+    @pl.loop(0, quarter // 96)
+    def _(i):
+        rows = tile_at(i, 96)
+        at = pl.ds(pl.multiple_of(rank * quarter + i * 96, 96), 96)
+        acc_a[rows, :] = (cr_a[at, :].astype(f32) + xr_a[rows, :].astype(f32)).astype(bf16)
+
+    for stream in streams[2:]:
+        spread_copy(stream, spot, 0).start()
+
+    def spread_step(s, last):
+        for stream in streams:
+            number, way, acc, slots, out, base, size = stream
+            at = spot + count - sign(stream) * (s + 1)
+            spread_copy(stream, at, s).wait_recv()
+            rows = chunk_at(at, stream, False)
+            total = (acc[rows, :].astype(f32) + slots[s, way].astype(f32)).astype(bf16)
+            if last:
+                out[chunk_at(at, stream, True), :] = total
+                gather_copy(stream, at, 0).start()
+                if number >= 2:
+                    across_copy(stream, at, 0, base).start()
+            else:
+                acc[rows, :] = total
+                spread_copy(stream, at, s + 1).start()
+
+    def gather_step(s, last):
+        for stream in streams:
+            number, base = stream[0], stream[5]
+            at = spot + 2 * count - sign(stream) * s
+            gather_copy(stream, at, s).wait_recv()
+            if not last:
+                gather_copy(stream, at, s + 1).start()
+            if number >= 2:
+                across_copy(stream, at, s + 1, base).start()
+
+    for index in range(len(swaps)):
+        swap_small(index)
+
+    @pl.loop(0, count - 2)
+    def _(s):
+        spread_step(s, False)
+
+    spread_step(count - 2, True)
+
+    @pl.loop(0, count - 2)
+    def _(s):
+        gather_step(s, False)
+
+    gather_step(count - 2, True)
+
+    back_ff = peer_copy(
+        ff_o.at[core_rows(core, half), :], ff_o.at[core_rows(core, half), :], (c_send, c_recv), 3, sibling
+    )
+    back_ff.start()
+    other = (core * 2 + 1 - rank) * quarter
+
+    @pl.loop(0, count)
+    def _(s):
+        for stream in streams[2:]:
+            step_sign = sign(stream)
+            at = spot + 2 * count + step_sign * (1 - s)
+            across_copy(stream, at, s, other).wait_recv()
+
+    back_a = peer_copy(
+        a_o.at[core_rows(core, 2 * quarter), :], a_o.at[core_rows(core, 2 * quarter), :],
+        (c_send, c_recv), 4, sibling,
+    )
+    back_a.start()
+
+    @pl.loop(0, count - 1)
+    def _(s):
+        for stream in streams:
+            spread_copy(stream, spot, s).wait_send()
+            gather_copy(stream, spot, s).wait_send()
+
+    @pl.loop(0, count)
+    def _(s):
+        for stream in streams[2:]:
+            across_copy(stream, spot, s, stream[5]).wait_send()
+
+    back_ff.wait()
+    back_a.wait()
 
 
 def in_vmem(count):
@@ -866,9 +1087,41 @@
         tokens, trig, span, vec, w_query, w_key, w_value, w_out,
         dhs, dho, mixb, mixf, inv, rq, rk, vv, nrm, scl, st, z, small,
     )
-    gff = lax.psum(gff, "dp")
-    ga = lax.psum(ga, ("dp", "tensor"))
-    small = lax.psum(small, ("dp", "tensor"))
+    count = lax.axis_size("dp") // 2
+    swaps = 2 + count.bit_length() - 1
+    half, quarter = units, width
+    ff_part, a_part = half // count // 2, quarter // count // 2
+    gff, ga, small = pl.pallas_call(
+        functools.partial(sum_kernel, count),
+        out_shape=shaped((gff.shape, bf16), (ga.shape, bf16), ((swaps + 1, *small.shape), f32)),
+        in_specs=in_vmem(3),
+        out_specs=tuple(in_vmem(3)),
+        scratch_shapes=[
+            pltpu.VMEM((half, width), bf16),
+            pltpu.VMEM((2 * quarter, width), bf16),
+            pltpu.VMEM((quarter, width), bf16),
+            pltpu.VMEM((half, width), bf16),
+            pltpu.VMEM((quarter, width), bf16),
+            pltpu.VMEM((count - 1, 2, ff_part, width), bf16),
+            pltpu.VMEM((count - 1, 2, a_part, width), bf16),
+            pltpu.VMEM((swaps, *small.shape), f32),
+            pltpu.SemaphoreType.DMA((5,)),
+            pltpu.SemaphoreType.DMA((5,)),
+            pltpu.SemaphoreType.DMA((4, count - 1)),
+            pltpu.SemaphoreType.DMA((4, count - 1)),
+            pltpu.SemaphoreType.DMA((4, count - 1)),
+            pltpu.SemaphoreType.DMA((4, count - 1)),
+            pltpu.SemaphoreType.DMA((2, count)),
+            pltpu.SemaphoreType.DMA((2, count)),
+            pltpu.SemaphoreType.DMA((swaps,)),
+            pltpu.SemaphoreType.DMA((swaps,)),
+        ],
+        compiler_params=pltpu.CompilerParams(
+            collective_id=2, has_side_effects=True, vmem_limit_bytes=60 << 20
+        ),
+        name="sums",
+    )(gff, ga, small)
+    small = small[swaps]
     halves = units // width
     g_up = jnp.concatenate(
         [gff[units + h * width : units + (h + 1) * width] for h in range(halves)], axis=1
@@ -907,6 +1160,8 @@
             and width % TILE == 0
             and w_up.shape[1] % width == 0
             and w_up.shape[1] // width <= 3
+            and mesh.shape["dp"] in (8, 16, 32)
+            and width % (16 * mesh.shape["dp"]) == 0
         )
         return pair_device(*args) if fits else general_device(*args)
 

time: 369 us -> 266 us (0.72)
  waiting for transfers between devices: 185 us -> 0 us
  Pallas kernels: 99.6 us -> 235 us
  blocking collectives: 40.3 us -> 0 us
  between operations: 14.8 us -> 1.38 us
    psum x2 -> x0, waiting for transfers between devices: 185 us -> none  [the longest x1 142 us: pair_device(): ga = lax.psum(ga, ('dp', 'tensor'))]
    pallas_call x0 -> x1, Pallas kernels: none -> 136 us  [pair_device(): pl.pallas_call(functools.partial(sum_kernel, count), out_shape=shaped((gf...]
    psum x1 -> x0, blocking collectives: 40.3 us -> none  [pair_device(): small = lax.psum(small, ('dp', 'tensor'))]
  transfers between devices with their start and end apart: 2 -> 0, of which waited for: 2 -> 0; matrix products, arithmetic and copies ran while one was open for 2% -> 0% of each run, Pallas kernels for 9% -> 0%
where the time goes in v2:
time: 266 us; the launch traced here: 265 us
  Pallas kernels  235 us (88%)
  local copies, waits for them, and re-layouts  15.5 us (6%)
  other arithmetic  13 us (5%)
    pallas_call x1, Pallas kernels, pair_device(): pl.pallas_call(functools.partial(sum_kernel, count), out_shape=shaped((gf...  136 us
    pallas_call x1, Pallas kernels, pair_device(): pl.pallas_call(front_kernel, out_shape=front_outs, in_specs=in_vmem(2) +...  67 us
    pallas_call x1, Pallas kernels, pair_device(): pl.pallas_call(back_kernel, out_shape=back_outs, in_specs=in_vmem(2) + sm...  32.6 us
    unnamed x19, local copies, waits for them, and re-layouts  9.29 us

profile of v2, /device:TPU:0, one launch (start us, length us, event | category | flops | bytes accessed | tf_op | source)
XLA Modules:
  0.0 265.0 jit_solution(3711503424722116205)
XLA Ops:
  1.3 0.8 fusion.1
  2.1 0.7 select_select_fusion.trig
  2.8 0.8 dynamic-update-slice
  3.6 0.8 dynamic-update-slice.1
  4.5 0.9 dynamic-update-slice.2
  5.3 0.9 dynamic-update-slice.3
  6.2 0.9 dynamic-update-slice.4
  7.0 0.8 dynamic-update-slice.5
  7.9 0.9 dynamic-update-slice.6
  8.8 0.9 dynamic-update-slice.7
  9.6 0.9 dynamic-update-slice.8
  10.5 0.9 dynamic-update-slice.9
  11.4 0.6 pad_convert_fusion.vec
  12.0 67.0 %front.1 = (bf16[256,768]{1,0:T(8,128)(2,1)}, f32[16,768]{1,0:T(8,128)}, bf16[3072,768]{1,0:T(8,128)(2,1)}, bf16[256,768]{1,0:T(8,128)(2,1)}, f32[256,768]{1,0:T...) custom-call(bf16[256,768]{1,0:T(8,128)(2,1)} %tok.3, ...), custom_call_target="tpu_custom_call" | custom-call | tf_op jit(solution)/shard_map/front/pallas_call | solution.py:1024
  79.0 32.6 %back.1 = (f32[256,768]{1,0:T(8,128)}, bf16[3072,768]{1,0:T(8,128)(2,1)}, f32[16,768]{1,0:T(8,128)}) custom-call(bf16[256,768]{1,0:T(8,128)(2,1)} %tok.3, f32[8,256]{1,0:T(8,128)} %select_select_fusion.trig, s32[1,1]{1,0:T(1,128)} %bitcast.2.span, f32[16,768]{1,0:T(8,128)} %pad_convert_fusion.vec, bf16[768,768]{1,0:T(8,128)(2,1)} %wq.3, ...), custom_call_target="tpu_custom_call" | custom-call | tf_op jit(solution)/shard_map/back/pallas_call | solution.py:1056
  111.5 135.6 %sums.1 = (bf16[3072,768]{1,0:T(8,128)(2,1)}, bf16[3072,768]{1,0:T(8,128)(2,1)}, f32[6,16,768]{2,1,0:T(8,128)}) custom-call(bf16[3072,768]{1,0:T(8,128)(2,1)} %get-tuple-element.54.gff, bf16[3072,768]{1,0:T(8,128)(2,1)} %get-tuple-element.55.ga, f32[16,768]{1,0:T(8,128)} %get-tuple-element.56.small), custom_call_target="tpu_custom_call" | custom-call | tf_op jit(solution)/shard_map/sums/pallas_call | solution.py:1094
  247.1 1.9 slice_reduce_fusion
  249.0 0.8 slice.81
  249.8 0.6 reshape.69
  250.5 0.0 slice-start
  250.5 1.9 fusion.2
  252.4 0.0 slice-start.1
  252.4 4.3 %slice_convert_fusion = f32[1536,768]{1,0:T(8,128)} fusion(bf16[3072,768]{1,0:T(8,128)(2,1)} %get-tuple-element.59), kind=kLoop, calls=%fused_computation.1 | loop fusion | flops 1179648 | bytes 7077888 | tf_op jit(solution)/shard_map/convert_element_type | solution.py:1145
  256.7 2.8 %maximum_convert_fusion = f32[768,1536]{1,0:T(8,128)} fusion(bf16[768,768]{1,0:T(8,128)(2,1)S(1)} %get-tuple-element.70, bf16[768,768]{1,0:T(8,128)(2,1)S(1)} %get-tuple-element.69), kind=kLoop, calls=%fused_computation | loop fusion | flops 4718592 | bytes 7077888 | tf_op jit(solution)/shard_map/convert_element_type | solution.py:1143
  259.5 0.0 slice-done
  259.5 0.0 slice-done.1
  259.5 0.0 copy-start.1
  259.5 0.0 copy-start
  259.5 3.8 %slice_convert_fusion.1 = (f32[768,768]{1,0:T(8,128)}, f32[768,768]{1,0:T(8,128)}, f32[768,768]{1,0:T(8,128)}, f32[768,768]{1,0:T(8,128)}) fusion(bf16[3072,768]{1,0:T(8,128)(2,1)S(1)} %bitcast.4), kind=kLoop, calls=%fused_computation.2 | loop fusion | flops 2359296 | bytes 14155776 | tf_op jit(solution)/shard_map/convert_element_type | solution.py:1139
  263.4 0.0 copy-done.1
  263.4 0.7 copy.51
  264.1 0.0 copy-done
  264.1 0.9 copy.52
  (5 shorter events, 0.1 us)
Async XLA Ops:
  250.5 9.0 %slice-start = ((s8[4718592]{0:T(1024)(128)(4,1)}), s8[4194304]{0:T(1024)(128)(4,1)S(1)}, s32[]{:S(2)}) async-start(s8[4718592]{0:T(1024)(128)(4,1)} %bitcast.3), calls=%async_computation | async-start | bytes 8388608
  252.4 7.1 %slice-start.1 = ((s8[4718592]{0:T(1024)(128)(4,1)}), s8[524288]{0:T(1024)(128)(4,1)S(1)}, s32[]{:S(2)}) async-start(s8[4718592]{0:T(1024)(128)(4,1)} %bitcast.3), calls=%async_computation.1 | async-start | bytes 1048576
  259.5 3.9 %copy-start.1 = (bf16[256,768]{1,0:T(8,128)(2,1)S(1)}, bf16[256,768]{1,0:T(8,128)(2,1)}, u32[]{:S(2)}) copy-start(bf16[256,768]{1,0:T(8,128)(2,1)} %get-tuple-element.97) | copy-start | bytes 1179652
  259.5 4.6 %copy-start = (f32[256,768]{1,0:T(8,128)S(1)}, f32[256,768]{1,0:T(8,128)}, u32[]{:S(2)}) copy-start(f32[256,768]{1,0:T(8,128)} %get-tuple-element.98) | copy-start | bytes 2359300

commit v3 on v1

--- a/solution.py
+++ b/solution.py
@@ -293,6 +293,8 @@
 LANES = 2 * HD
 TILE = 256
 ROWBLOCK = 32
+FF_CUTS = 2
+A_CUTS = 1
 
 
 def tile_at(index, size):
@@ -592,31 +594,191 @@
             ).astype(bf16)
 
 
+def grid_place():
+    dp = lax.axis_index("dp")
+    core, chip = dp % 2, dp // 2
+    return core, chip % 2, chip // 2
+
+
+def ring_device(spot, depth, core):
+    far = spot // depth
+    z = far * (2 * depth - 1 - spot) + (1 - far) * spot
+    return ((z * 2 + far) * 2 + core, lax.axis_index("tensor"))
+
+
+def add_rows(target, rows, block):
+    target[rows, :] = (target[rows, :].astype(f32) + block.astype(f32)).astype(bf16)
+
+
 def back_kernel(
-    tok, trig, span, vec, wq, wk, wv, wo,
-    dhs, dho, mixb, mixf, inv, rq, rk, vv, nrm, scl, st, z, small_in,
-    dtok_o, ga_o, small_o,
+    count, tok, trig, span, vec, wq, wk, wv, wo,
+    dhs, dho, mixb, mixf, inv, rq, rk, vv, nrm, scl, st, z, small_in, gff,
+    dtok_o, ff_o, a_o, small_o,
     dhr, dres, dlow, dn, xs, dsend, drecv, dzs, dzr, dq, dk, dv, dql, dkl, dvl,
-    ctab, cosb, sinb, acc, send, recv,
+    ctab, cosb, sinb, acc, ga, small, cr_ff, cr_a, px, xr, acc_ff, acc_a, rs_ff, rs_a, small_r,
+    send, recv, r_send, r_recv, g_send, g_recv, x_send, x_recv, y_send, y_recv, m_send, m_recv,
 ):
     sems = (send, recv)
     rows, width = tok.shape
     pairs = width // LANES
     tiles = width // TILE
+    depth = count // 2
+    half = gff.shape[0] // 2
+    quarter = width
     rank = lax.axis_index("tensor")
-    peer = (lax.axis_index("dp"), 1 - rank)
+    dp = lax.axis_index("dp")
     early = 1.0 - rank.astype(f32)
-    meet([peer])
+    core, y, z_place = grid_place()
+    spot = y * (2 * depth - 1 - z_place) + (1 - y) * z_place
+    sibling = (dp + 1 - 2 * core, rank)
+    peer = (dp, 1 - rank)
+    ahead = ring_device((spot + 1) % count, depth, core)
+    behind = ring_device((spot + count - 1) % count, depth, core)
+    swaps = [sibling, peer, (dp + 2 - 4 * y, rank)]
+    step = 1
+    while step < depth:
+        bit = (z_place // step) % 2
+        swaps.append((dp + 4 * (step - 2 * step * bit), rank))
+        step *= 2
+    meet([ahead, behind] + swaps)
+
+    def part_rows(which, size):
+        return pl.ds(pl.multiple_of(which * size, size), size)
+
+    core_ff = peer_copy(gff.at[part_rows(1 - core, half), :], cr_ff, sems, 3, sibling)
+    core_a = peer_copy(ga.at[part_rows(1 - core, 2 * quarter), :], cr_a, sems, 4, sibling)
     hidden_copy = peer_copy(dhs, dhr, sems, 0, peer)
     hidden_copy.start()
+    core_ff.start()
+
+    ff_streams, a_streams = [], []
+    for kind, (cuts, group) in enumerate(((FF_CUTS, ff_streams), (A_CUTS, a_streams))):
+        own = acc_a if kind else acc_ff
+        size = own.shape[0] // count // 2
+        first_number = 2 * FF_CUTS * kind
+        for way in range(2):
+            for cut in range(cuts):
+                cols = pl.ds(cut * (width // cuts), width // cuts)
+                number = first_number + way * cuts + cut
+                group.append((number, kind, way, cols, size))
+    slots = (rs_ff, rs_a)
+    sums = (acc_ff, acc_a)
+    outs = (ff_o, a_o)
+    bases = (core * half, (core * 2 + rank) * quarter)
+
+    def chunk_rows(at, stream, base):
+        _, _, way, _, size = stream
+        return pl.ds(pl.multiple_of(base + (at % count) * 2 * size + way * size, size), size)
+
+    def toward(stream):
+        return behind if stream[2] else ahead
+
+    def sign(stream):
+        return -1 if stream[2] else 1
+
+    def spread_copy(stream, at, s):
+        number, kind, way, cols, _ = stream
+        return pltpu.make_async_remote_copy(
+            src_ref=sums[kind].at[chunk_rows(at, stream, 0), cols],
+            dst_ref=slots[kind].at[s, way, :, cols],
+            send_sem=r_send.at[number, s],
+            recv_sem=r_recv.at[number, s],
+            device_id=toward(stream),
+            device_id_type=MESH,
+        )
+
+    def gather_copy(stream, at, s):
+        number, kind, _, cols, _ = stream
+        where = outs[kind].at[chunk_rows(at, stream, bases[kind]), cols]
+        return pltpu.make_async_remote_copy(
+            src_ref=where,
+            dst_ref=where,
+            send_sem=g_send.at[number, s],
+            recv_sem=g_recv.at[number, s],
+            device_id=toward(stream),
+            device_id_type=MESH,
+        )
+
+    def across_copy(stream, at, s, base):
+        number, _, _, cols, _ = stream
+        where = a_o.at[chunk_rows(at, stream, base), cols]
+        return pltpu.make_async_remote_copy(
+            src_ref=where,
+            dst_ref=where,
+            send_sem=x_send.at[number - 2 * FF_CUTS, s],
+            recv_sem=x_recv.at[number - 2 * FF_CUTS, s],
+            device_id=peer,
+            device_id_type=MESH,
+        )
+
+    def fold_copy(stream, s):
+        number, _, way, cols, _ = stream
+        at = spot + count - sign(stream) * s
+        return pltpu.make_async_remote_copy(
+            src_ref=px.at[chunk_rows(at, stream, 0), cols],
+            dst_ref=xr.at[s, way, :, cols],
+            send_sem=y_send.at[number - 2 * FF_CUTS, s],
+            recv_sem=y_recv.at[number - 2 * FF_CUTS, s],
+            device_id=peer,
+            device_id_type=MESH,
+        )
+
+    def own_part(stream, at, s):
+        _, kind, way, cols, _ = stream
+        rows_in = chunk_rows(at, stream, bases[kind])
+        if kind == 0:
+            return gff[rows_in, cols].astype(f32) + cr_ff[chunk_rows(at, stream, 0), cols].astype(f32)
+        fold_copy(stream, s).wait_recv()
+        return (
+            ga[rows_in, cols].astype(f32)
+            + cr_a[chunk_rows(at, stream, rank * quarter), cols].astype(f32)
+            + xr[s, way, :, cols].astype(f32)
+        )
+
+    def ring_first(streams):
+        for stream in streams:
+            _, kind, _, cols, _ = stream
+            at = spot + count
+            sums[kind][chunk_rows(at, stream, 0), cols] = own_part(stream, at, 0).astype(bf16)
+            spread_copy(stream, at, 0).start()
+
+    def ring_spread(streams, s, last):
+        for stream in streams:
+            _, kind, way, cols, _ = stream
+            at = spot + count - sign(stream) * (s + 1)
+            own = own_part(stream, at, s + 1)
+            spread_copy(stream, at, s).wait_recv()
+            total = (own + slots[kind][s, way, :, cols].astype(f32)).astype(bf16)
+            if last:
+                outs[kind][chunk_rows(at, stream, bases[kind]), cols] = total
+                gather_copy(stream, at, 0).start()
+                if kind:
+                    across_copy(stream, at, 0, bases[1]).start()
+            else:
+                sums[kind][chunk_rows(at, stream, 0), cols] = total
+                spread_copy(stream, at, s + 1).start()
+
+    def ring_gather(streams, s, last):
+        for stream in streams:
+            kind = stream[1]
+            at = spot + 2 * count - sign(stream) * s
+            gather_copy(stream, at, s).wait_recv()
+            if not last:
+                gather_copy(stream, at, s + 1).start()
+            if kind:
+                across_copy(stream, at, s + 1, bases[1]).start()
+
     angle_tables(trig, span, cosb, sinb, ctab)
     diag = pair_mask()
     first, second = head_masks()
     first_low, second_low = first.astype(bf16), second.astype(bf16)
     diag_low = diag.astype(bf16)
     acc[...] = jnp.zeros_like(acc)
-    small_o[...] = small_in[...]
+    small[...] = small_in[...]
+    core_ff.wait()
+    ring_first(ff_streams)
     hidden_copy.wait()
+    ring_spread(ff_streams, 0, False)
 
     @pl.loop(0, rows // ROWBLOCK)
     def _(i):
@@ -636,7 +798,7 @@
         acc[16:24, :] += fold8(inner)
 
     for slot in range(3):
-        small_o[slot : slot + 1, :] = jnp.sum(
+        small[slot : slot + 1, :] = jnp.sum(
             acc[8 * slot : 8 * slot + 8, :], axis=0, keepdims=True
         )
 
@@ -666,14 +828,14 @@
     key_copy = peer_copy(dzs, dzr, sems, 2, peer)
     state_copy.start()
     key_copy.start()
+    ring_spread(ff_streams, 1, False)
 
     @pl.loop(0, tiles)
     def _(j):
         cols = tile_at(j, TILE)
-        ga_o[tile_at(3 * tiles + j, TILE), :] = mm_tn(mixb[:, cols], dlow[...]).astype(bf16)
-
-    @pl.loop(0, pairs)
-    def _(p):
+        ga[tile_at(3 * tiles + j, TILE), :] = mm_tn(mixb[:, cols], dlow[...]).astype(bf16)
+
+    def inside(p):
         lanes = tile_at(p, LANES)
         q, k, v = rq[:, lanes], rk[:, lanes], vv[:, lanes]
         d_numer = dn[:, lanes]
@@ -693,6 +855,10 @@
         dk[:, lanes] = sum_k
         dv[:, lanes] = sum_v
 
+    pl.loop(0, pairs // 2)(inside)
+    ring_spread(ff_streams, 2, False)
+    pl.loop(pairs // 2, pairs)(inside)
+    ring_spread(ff_streams, 3, False)
     state_copy.wait()
     key_copy.wait()
 
@@ -717,15 +883,20 @@
         dkl[:, lanes] = sum_k.astype(bf16)
         dvl[:, lanes] = sum_v.astype(bf16)
         for slot, value in ((6, sum_q), (7, sum_k), (8, sum_v)):
-            small_o[slot : slot + 1, lanes] = jnp.sum(value, axis=0, keepdims=True)
+            small[slot : slot + 1, lanes] = jnp.sum(value, axis=0, keepdims=True)
+
+    ring_spread(ff_streams, 4, False)
 
     for which, source in enumerate((dql, dkl, dvl)):
 
         @pl.loop(0, tiles)
         def _(j, which=which, source=source):
-            ga_o[tile_at(which * tiles + j, TILE), :] = mm_tn(
+            ga[tile_at(which * tiles + j, TILE), :] = mm_tn(
                 tok[:, tile_at(j, TILE)], source[...]
             ).astype(bf16)
+
+    core_a.start()
+    ring_spread(ff_streams, 5, False)
 
     @pl.loop(0, tiles)
     def _(j):
@@ -736,6 +907,84 @@
             + mm_nt(dkl[...], wk[cols, :])
             + mm_nt(dvl[...], wv[cols, :])
         )
+
+    def small_copy(index):
+        return peer_copy(small_o.at[index], small_r.at[index], (m_send, m_recv), index, swaps[index])
+
+    def swap_small(index):
+        small_copy(index).wait()
+        small_o[index + 1] = small_o[index] + small_r[index]
+        if index + 1 < len(swaps):
+            small_copy(index + 1).start()
+
+    small_o[0] = small[...]
+    small_copy(0).start()
+    core_a.wait()
+
+    @pl.loop(0, quarter // 96)
+    def _(i):
+        near = pl.ds(pl.multiple_of((core * 2 + 1 - rank) * quarter + i * 96, 96), 96)
+        far = pl.ds(pl.multiple_of((1 - rank) * quarter + i * 96, 96), 96)
+        px[tile_at(i, 96), :] = (ga[near, :].astype(f32) + cr_a[far, :].astype(f32)).astype(bf16)
+
+    for s in range(3):
+        for stream in a_streams:
+            fold_copy(stream, s).start()
+    ring_spread(ff_streams, count - 2, True)
+    swap_small(0)
+    ring_first(a_streams)
+
+    @pl.loop(0, count - 2)
+    def _(s):
+        @pl.when(s + 3 < count)
+        def _():
+            for stream in a_streams:
+                fold_copy(stream, s + 3).start()
+
+        ring_gather(ff_streams, s, False)
+        ring_spread(a_streams, s, False)
+
+    ring_gather(ff_streams, count - 2, True)
+    back_ff = peer_copy(
+        ff_o.at[part_rows(core, half), :], ff_o.at[part_rows(core, half), :], sems, 5, sibling
+    )
+    back_ff.start()
+    ring_spread(a_streams, count - 2, True)
+    for index in range(1, len(swaps)):
+        swap_small(index)
+
+    @pl.loop(0, count - 2)
+    def _(s):
+        ring_gather(a_streams, s, False)
+
+    ring_gather(a_streams, count - 2, True)
+    other = (core * 2 + 1 - rank) * quarter
+
+    @pl.loop(0, count)
+    def _(s):
+        for stream in a_streams:
+            at = spot + 2 * count + sign(stream) * (1 - s)
+            across_copy(stream, at, s, other).wait_recv()
+
+    back_a = peer_copy(
+        a_o.at[part_rows(core, 2 * quarter), :], a_o.at[part_rows(core, 2 * quarter), :], sems, 6, sibling
+    )
+    back_a.start()
+
+    @pl.loop(0, count - 1)
+    def _(s):
+        for stream in ff_streams + a_streams:
+            spread_copy(stream, spot, s).wait_send()
+            gather_copy(stream, spot, s).wait_send()
+
+    @pl.loop(0, count)
+    def _(s):
+        for stream in a_streams:
+            across_copy(stream, spot, s, bases[1]).wait_send()
+            fold_copy(stream, s).wait_send()
+
+    back_ff.wait()
+    back_a.wait()
 
 
 def in_vmem(count):
@@ -831,11 +1080,18 @@
         ),
         name="front",
     )(tokens, trig, span, vec, w_query, w_key, w_value, w_out, w_up, w_down, out_grad)
-    back_outs = shaped(wide, ((4 * width, width), bf16), ((smalls, width), f32))
-    d_tokens, ga, small = pl.pallas_call(
-        back_kernel,
+    count = lax.axis_size("dp") // 2
+    swaps = 2 + count.bit_length() - 1
+    half, quarter = units, width
+    ff_part, a_part = half // count // 2, quarter // count // 2
+    streams = 2 * (FF_CUTS + A_CUTS)
+    back_outs = shaped(
+        wide, (gff.shape, bf16), ((4 * width, width), bf16), ((swaps + 1, *small.shape), f32)
+    )
+    d_tokens, gff, ga, small = pl.pallas_call(
+        functools.partial(back_kernel, count),
         out_shape=back_outs,
-        in_specs=in_vmem(2) + smem + in_vmem(18),
+        in_specs=in_vmem(2) + smem + in_vmem(19),
         out_specs=tuple(in_vmem(len(back_outs))),
         scratch_shapes=[
             pltpu.VMEM((rows, width), bf16),
@@ -855,20 +1111,39 @@
             pltpu.VMEM((rows, width), bf16),
             *tables,
             pltpu.VMEM((24, width), f32),
-            pltpu.SemaphoreType.DMA((3,)),
-            pltpu.SemaphoreType.DMA((3,)),
+            pltpu.VMEM((4 * width, width), bf16),
+            pltpu.VMEM(small.shape, f32),
+            pltpu.VMEM((half, width), bf16),
+            pltpu.VMEM((2 * quarter, width), bf16),
+            pltpu.VMEM((quarter, width), bf16),
+            pltpu.VMEM((count, 2, a_part, width), bf16),
+            pltpu.VMEM((half, width), bf16),
+            pltpu.VMEM((quarter, width), bf16),
+            pltpu.VMEM((count - 1, 2, ff_part, width), bf16),
+            pltpu.VMEM((count - 1, 2, a_part, width), bf16),
+            pltpu.VMEM((swaps, *small.shape), f32),
+            pltpu.SemaphoreType.DMA((7,)),
+            pltpu.SemaphoreType.DMA((7,)),
+            pltpu.SemaphoreType.DMA((streams, count - 1)),
+            pltpu.SemaphoreType.DMA((streams, count - 1)),
+            pltpu.SemaphoreType.DMA((streams, count - 1)),
+            pltpu.SemaphoreType.DMA((streams, count - 1)),
+            pltpu.SemaphoreType.DMA((2 * A_CUTS, count)),
+            pltpu.SemaphoreType.DMA((2 * A_CUTS, count)),
+            pltpu.SemaphoreType.DMA((2 * A_CUTS, count)),
+            pltpu.SemaphoreType.DMA((2 * A_CUTS, count)),
+            pltpu.SemaphoreType.DMA((swaps,)),
+            pltpu.SemaphoreType.DMA((swaps,)),
         ],
         compiler_params=pltpu.CompilerParams(
-            collective_id=1, has_side_effects=True, vmem_limit_bytes=60 << 20
+            collective_id=1, has_side_effects=True, vmem_limit_bytes=62 << 20
         ),
         name="back",
     )(
         tokens, trig, span, vec, w_query, w_key, w_value, w_out,
-        dhs, dho, mixb, mixf, inv, rq, rk, vv, nrm, scl, st, z, small,
-    )
-    gff = lax.psum(gff, "dp")
-    ga = lax.psum(ga, ("dp", "tensor"))
-    small = lax.psum(small, ("dp", "tensor"))
+        dhs, dho, mixb, mixf, inv, rq, rk, vv, nrm, scl, st, z, small, gff,
+    )
+    small = small[swaps]
     halves = units // width
     g_up = jnp.concatenate(
         [gff[units + h * width : units + (h + 1) * width] for h in range(halves)], axis=1
@@ -907,6 +1182,8 @@
             and width % TILE == 0
             and w_up.shape[1] % width == 0
             and w_up.shape[1] // width <= 3
+            and mesh.shape["dp"] == 16
+            and width % (16 * mesh.shape["dp"]) == 0
         )
         return pair_device(*args) if fits else general_device(*args)
 

time: 369 us -> 224 us (0.61)
  waiting for transfers between devices: 185 us -> 0 us
  Pallas kernels: 99.6 us -> 194 us
  blocking collectives: 40.3 us -> 0 us
  between operations: 14.8 us -> 1.37 us
    psum x2 -> x0, waiting for transfers between devices: 185 us -> none  [the longest x1 142 us: pair_device(): ga = lax.psum(ga, ('dp', 'tensor'))]
    pallas_call x1, Pallas kernels: 32.6 us -> 127 us  [pair_device(): pl.pallas_call(functools.partial(back_kernel, count), out_shape=back_outs...]
    psum x1 -> x0, blocking collectives: 40.3 us -> none  [pair_device(): small = lax.psum(small, ('dp', 'tensor'))]
  transfers between devices with their start and end apart: 2 -> 0, of which waited for: 2 -> 0; matrix products, arithmetic and copies ran while one was open for 2% -> 0% of each run, Pallas kernels for 9% -> 0%
where the time goes in v3:
time: 224 us
  Pallas kernels  194 us (87%)
  local copies, waits for them, and re-layouts  15.3 us (7%)
  other arithmetic  13 us (6%)
    pallas_call x1, Pallas kernels, pair_device(): pl.pallas_call(functools.partial(back_kernel, count), out_shape=back_outs...  127 us
    pallas_call x1, Pallas kernels, pair_device(): pl.pallas_call(front_kernel, out_shape=front_outs, in_specs=in_vmem(2) +...  67 us
    unnamed x19, local copies, waits for them, and re-layouts  9.29 us

profile of v3, /device:TPU:0, one launch (start us, length us, event | category | flops | bytes accessed | tf_op | source)
XLA Modules:
  0.0 223.9 jit_solution(3789588008499400081)
XLA Ops:
  1.3 0.8 fusion.1
  2.1 0.7 select_select_fusion.trig
  2.8 0.8 dynamic-update-slice
  3.6 0.8 dynamic-update-slice.1
  4.5 0.9 dynamic-update-slice.2
  5.3 0.9 dynamic-update-slice.3
  6.2 0.9 dynamic-update-slice.4
  7.0 0.8 dynamic-update-slice.5
  7.9 0.9 dynamic-update-slice.6
  8.8 0.9 dynamic-update-slice.7
  9.6 0.9 dynamic-update-slice.8
  10.5 0.9 dynamic-update-slice.9
  11.4 0.6 pad_convert_fusion.vec
  12.0 67.0 %front.1 = (bf16[256,768]{1,0:T(8,128)(2,1)}, f32[16,768]{1,0:T(8,128)}, bf16[3072,768]{1,0:T(8,128)(2,1)}, bf16[256,768]{1,0:T(8,128)(2,1)}, f32[256,768]{1,0:T...) custom-call(bf16[256,768]{1,0:T(8,128)(2,1)} %tok.3, ...), custom_call_target="tpu_custom_call" | custom-call | tf_op jit(solution)/shard_map/front/pallas_call | solution.py:1052
  79.0 127.2 %back.1 = (f32[256,768]{1,0:T(8,128)}, bf16[3072,768]{1,0:T(8,128)(2,1)}, bf16[3072,768]{1,0:T(8,128)(2,1)}, f32[6,16,768]{2,1,0:T(8,128)}) custom-call(bf16[256,768]{1,0:T(8,128)(2,1)} %tok.3, f32[8,256]{1,0:T(8,128)} %select_select_fusion.trig, s32[1,1]{1,0:T(1,128)} %bitcast.2.span, f32[16,768]{1,0:T(8,128)} %pad_convert_fusion.vec, bf16[768,768]{1,0:T(8,128)(2,1)} %wq.3, ...), custom_call_target="tpu_custom_call" | custom-call | tf_op jit(solution)/shard_map/back/pallas_call | solution.py:1091
  206.2 1.7 slice_reduce_fusion
  207.9 0.8 slice.81
  208.7 0.6 reshape.69
  209.3 0.0 slice-start
  209.3 1.9 fusion.2
  211.3 0.0 slice-start.1
  211.3 4.3 %slice_convert_fusion = f32[1536,768]{1,0:T(8,128)} fusion(bf16[3072,768]{1,0:T(8,128)(2,1)} %get-tuple-element.55), kind=kLoop, calls=%fused_computation.1 | loop fusion | flops 1179648 | bytes 7077888 | tf_op jit(solution)/shard_map/convert_element_type | solution.py:1167
  215.5 2.8 %maximum_convert_fusion = f32[768,1536]{1,0:T(8,128)} fusion(bf16[768,768]{1,0:T(8,128)(2,1)S(1)} %get-tuple-element.66, bf16[768,768]{1,0:T(8,128)(2,1)S(1)} %get-tuple-element.65), kind=kLoop, calls=%fused_computation | loop fusion | flops 4718592 | bytes 7077888 | tf_op jit(solution)/shard_map/convert_element_type | solution.py:1165
  218.4 0.0 slice-done
  218.4 0.0 slice-done.1
  218.4 0.0 copy-start.1
  218.4 0.0 copy-start
  218.4 3.8 %slice_convert_fusion.1 = (f32[768,768]{1,0:T(8,128)}, f32[768,768]{1,0:T(8,128)}, f32[768,768]{1,0:T(8,128)}, f32[768,768]{1,0:T(8,128)}) fusion(bf16[3072,768]{1,0:T(8,128)(2,1)S(1)} %bitcast.4), kind=kLoop, calls=%fused_computation.2 | loop fusion | flops 2359296 | bytes 14155776 | tf_op jit(solution)/shard_map/convert_element_type | solution.py:1161
  222.2 0.0 copy-done.1
  222.2 0.7 copy.51
  223.0 0.0 copy-done
  223.0 0.9 copy.52
  (5 shorter events, 0.1 us)
Async XLA Ops:
  209.3 9.0 %slice-start = ((s8[4718592]{0:T(1024)(128)(4,1)}), s8[4194304]{0:T(1024)(128)(4,1)S(1)}, s32[]{:S(2)}) async-start(s8[4718592]{0:T(1024)(128)(4,1)} %bitcast.3), calls=%async_computation | async-start | bytes 8388608
  211.3 7.1 %slice-start.1 = ((s8[4718592]{0:T(1024)(128)(4,1)}), s8[524288]{0:T(1024)(128)(4,1)S(1)}, s32[]{:S(2)}) async-start(s8[4718592]{0:T(1024)(128)(4,1)} %bitcast.3), calls=%async_computation.1 | async-start | bytes 1048576
  218.4 3.9 %copy-start.1 = (bf16[256,768]{1,0:T(8,128)(2,1)S(1)}, bf16[256,768]{1,0:T(8,128)(2,1)}, u32[]{:S(2)}) copy-start(bf16[256,768]{1,0:T(8,128)(2,1)} %get-tuple-element.93) | copy-start | bytes 1179652
  218.4 4.6 %copy-start = (f32[256,768]{1,0:T(8,128)S(1)}, f32[256,768]{1,0:T(8,128)}, u32[]{:S(2)}) copy-start(f32[256,768]{1,0:T(8,128)} %get-tuple-element.94) | copy-start | bytes 2359300

commit v4 on v1

--- a/solution.py
+++ b/solution.py
@@ -293,6 +293,8 @@
 LANES = 2 * HD
 TILE = 256
 ROWBLOCK = 32
+FF_CUTS = 3
+A_CUTS = 3
 
 
 def tile_at(index, size):
@@ -333,21 +335,22 @@
     return ((row < HD) == (col < HD)).astype(f32)
 
 
-def first_row(block, which):
+def column_of(block, which):
     row = lax.broadcasted_iota(jnp.int32, block.shape, 0)
-    return jnp.where(row == which, block, 0.0)
-
-
-def column_of(block, which):
-    return contract(first_row(block, which), jnp.ones((8, LANES), f32), 0, 0, highest)
+    return contract(jnp.where(row == which, block, 0.0), jnp.ones((8, LANES), f32), 0, 0, highest)
 
 
 def squeeze_pair(square):
     return square[:HD] + square[HD:]
 
 
-def spread_pair(half, mask):
-    return jnp.concatenate([half, half], axis=0).astype(f32) * mask
+def spread_pair(part, mask):
+    return jnp.concatenate([part, part], axis=0).astype(f32) * mask
+
+
+def two_rows(top, below):
+    row = lax.broadcasted_iota(jnp.int32, (8, LANES), 0)
+    return jnp.where(row == 0, top, jnp.where(row == 1, below, 0.0))
 
 
 def fold8(value):
@@ -357,9 +360,11 @@
     return total
 
 
-def angle_tables(trig, span, cosb, sinb, ctab):
+def angle_tables(places, length, span, cosb, sinb, ctab):
     rows = cosb.shape[0]
-    block = trig[...]
+    angle = math.pi / 2 * places.astype(f32).reshape(1, rows) / (3 * length)
+    line = lax.broadcasted_iota(jnp.int32, (8, rows), 0)
+    block = jnp.where(line == 0, jnp.cos(angle), jnp.where(line == 1, jnp.sin(angle), 0.0))
     cosb[...] = column_of(block, 0)
     sinb[...] = column_of(block, 1)
     both = contract(block, block, 0, 0, highest)
@@ -380,44 +385,120 @@
     )
 
 
-def meet(devices):
-    barrier = pltpu.get_barrier_semaphore()
-    for device in devices:
-        pl.semaphore_signal(barrier, inc=1, device_id=device, device_id_type=MESH)
-    pl.semaphore_wait(barrier, len(devices))
-
-
-def front_kernel(
-    tok, trig, span, vec, wq, wk, wv, wo, wup, wdn, og,
-    res_o, small_o, gff_o, dhs_o, dho_o, mixb, mixf, inv, rq, rk, vv, nrm, scl, st_o, z_o,
-    hbuf, act, slope, dbuf, dpre, hid, tsend, trecv, zsend, zrecv, bsend, brecv,
-    numer, denom, ctab, cosb, sinb, acc, bup, send, recv,
+def ring_device(spot, depth, core):
+    far = spot // depth
+    z = far * (2 * depth - 1 - spot) + (1 - far) * spot
+    return ((z * 2 + far) * 2 + core, lax.axis_index("tensor"))
+
+
+def layer_norm(value):
+    centred = value - jnp.mean(value, axis=-1, keepdims=True)
+    scale = lax.rsqrt(jnp.mean(centred * centred, axis=-1, keepdims=True) + norm_eps)
+    return centred * scale, scale
+
+
+def layer_norm_back(grad, gain, normal, scale):
+    along = grad * gain
+    return (
+        along
+        - jnp.mean(along, axis=-1, keepdims=True)
+        - normal * jnp.mean(along * normal, axis=-1, keepdims=True)
+    ) * scale
+
+
+def block_kernel(
+    count, tok, places, span, bq, bk, bv, bo, g1, b1, bd, g2, b2, bup_in, og,
+    wq, wk, wv, wo, wup, wdn,
+    res_h, dtok_h, ff_h, a_h, small_h,
+    wa, wff, vec, hbuf, act, slope, dbuf, dpre, hid, numer, denom, tsend, trecv, zsend, zrecv,
+    bsend, brecv, res, gff, dhs, dhr, dho, mixb, mixf, inv, rq, rk, vv, nrm, scl, st, zst,
+    dres, dlow, dn, xs, dsend, drecv, dzs, dzr, dql, dkl, dvl, ctab, cosb, sinb, acc, bup,
+    cr_ff, cr_a, px, xr, rs_ff, rs_a, ff_o, a_o, smalls, small_r,
+    send, recv, r_send, r_recv, g_send, g_recv, x_send, x_recv, y_send, y_recv, m_send, m_recv,
+    w_sem, o_sem,
 ):
     sems = (send, recv)
     rows, width = tok.shape
     units = wup.shape[1]
+    halves = units // width
     pairs = width // LANES
     tiles = width // TILE
-    rank = lax.axis_index("tensor")
-    peer = (lax.axis_index("dp"), 1 - rank)
+    depth = count // 2
+    quarter = width
+    dq, dk, dv, ga = numer, denom, hid, wff
+    dp, rank = lax.axis_index("dp"), lax.axis_index("tensor")
     late = rank.astype(f32)
-    own, other = pl.ds(0, rows), pl.ds(rows, rows)
-    meet([peer])
-
-    for which, (weight, target) in enumerate(((wq, rq), (wk, rk), (wv, vv))):
-
-        @pl.loop(0, tiles)
-        def _(j, which=which, weight=weight, target=target):
-            cols = tile_at(j, TILE)
-            y = mm(tok[...], weight[:, cols]) + vec[which : which + 1, cols]
-            if which < 2:
-                y = jnp.maximum(y, 0.0)
-            target[:, cols] = y.astype(bf16)
-
-    angle_tables(trig, span, cosb, sinb, ctab)
+    early = 1.0 - late
+    core, y, z = dp % 2, (dp // 2) % 2, dp // 4
+    spot = y * (2 * depth - 1 - z) + (1 - y) * z
+    sibling = (dp + 1 - 2 * core, rank)
+    peer = (dp, 1 - rank)
+    ahead = ring_device((spot + 1) % count, depth, core)
+    behind = ring_device((spot + count - 1) % count, depth, core)
+    swaps = [sibling, peer, (dp + 2 - 4 * y, rank)]
+    step = 1
+    while step < depth:
+        bit = (z // step) % 2
+        swaps.append((dp + 4 * (step - 2 * step * bit), rank))
+        step *= 2
+    partners = [ahead, behind] + swaps
+    barrier = pltpu.get_barrier_semaphore()
+    for device in partners:
+        pl.semaphore_signal(barrier, inc=1, device_id=device, device_id_type=MESH)
+
+    loads = [
+        (wk, wa.at[pl.ds(width, width), :]),
+        (wv, wa.at[pl.ds(2 * width, width), :]),
+        (wq, wa.at[pl.ds(0, width), :]),
+        (wo, wa.at[pl.ds(3 * width, width), :]),
+    ]
+    for part in range(halves):
+        loads.append(
+            (wup.at[:, pl.ds(part * width, width)], wff.at[pl.ds(units + part * width, width), :])
+        )
+    loads.append((wdn, wff.at[pl.ds(0, units), :]))
+
+    def load(index):
+        return pltpu.make_async_copy(loads[index][0], loads[index][1], w_sem.at[index])
+
+    for index in range(len(loads)):
+        load(index).start()
+
+    def out_copy(source, target, at, slot):
+        return pltpu.make_async_copy(source.at[at, :], target.at[at, :], o_sem.at[slot])
+
+    for index, source in enumerate((bq, bk, bv, bo, g1, b1, bd, g2, b2)):
+        vec[index : index + 1, :] = source[...].astype(f32).reshape(1, width)
+    for part in range(halves):
+        piece = bup_in[pl.ds(part * width, width)]
+        vec[9 + part : 10 + part, :] = piece.astype(f32).reshape(1, width)
+    own, far_rows = pl.ds(0, rows), pl.ds(rows, rows)
+    my_places = places[pl.ds(pl.multiple_of(rank * rows, rows), rows)]
+    angle_tables(my_places, places.shape[0], span, cosb, sinb, ctab)
     diag = pair_mask()
     first, second = head_masks()
     first_low, second_low = first.astype(bf16), second.astype(bf16)
+    diag_low = diag.astype(bf16)
+    acc[...] = jnp.zeros_like(acc)
+    bup[...] = jnp.zeros_like(bup)
+    smalls[0] = jnp.zeros(smalls.shape[1:], f32)
+
+    def add_small(slot, line):
+        smalls[0, slot : slot + 1, :] = line
+
+    def project(which, target):
+        @pl.loop(0, tiles)
+        def _(j):
+            cols = tile_at(j, TILE)
+            value = mm(tok[...], wa[pl.ds(which * width, width), cols]) + vec[which : which + 1, cols]
+            if which < 2:
+                value = jnp.maximum(value, 0.0)
+            target[:, cols] = value.astype(bf16)
+
+    load(0).wait()
+    project(1, rk)
+    load(1).wait()
+    project(2, vv)
 
     @pl.loop(0, pairs)
     def _(p):
@@ -427,15 +508,18 @@
         kc, ks = (k * cosb[...]).astype(bf16), (k * sinb[...]).astype(bf16)
         tsend[p, 0] = squeeze_pair(mm_tn(kc, v) * diag).astype(bf16)
         tsend[p, 1] = squeeze_pair(mm_tn(ks, v) * diag).astype(bf16)
-        sum_c = jnp.sum(kc.astype(f32), axis=0, keepdims=True)
-        sum_s = jnp.sum(ks.astype(f32), axis=0, keepdims=True)
-        row = lax.broadcasted_iota(jnp.int32, (8, LANES), 0)
-        zsend[p] = jnp.where(row == 0, sum_c, jnp.where(row == 1, sum_s, 0.0))
-
+        zsend[p] = two_rows(
+            jnp.sum(kc.astype(f32), axis=0, keepdims=True),
+            jnp.sum(ks.astype(f32), axis=0, keepdims=True),
+        )
+
+    pl.semaphore_wait(barrier, len(partners))
     state_copy = peer_copy(tsend, trecv, sems, 0, peer)
     key_copy = peer_copy(zsend, zrecv, sems, 1, peer)
     state_copy.start()
     key_copy.start()
+    load(2).wait()
+    project(0, rq)
 
     @pl.loop(0, pairs)
     def _(p):
@@ -443,8 +527,7 @@
         q, k, v = rq[:, lanes], rk[:, lanes], vv[:, lanes]
         parts = []
         for mask, rest in ((first_low, second_low), (second_low, first_low)):
-            score = mm_nt(q * mask, k)
-            prob = (score * ctab[...]).astype(bf16)
+            prob = (mm_nt(q * mask, k) * ctab[...]).astype(bf16)
             parts.append(mm(prob, v * mask + rest))
         numer[:, lanes] = parts[0] * first + parts[1] * second
         denom[:, lanes] = pltpu.roll(parts[0] * second + parts[1] * first, HD, 1)
@@ -457,12 +540,12 @@
         lanes = tile_at(p, LANES)
         q = rq[:, lanes].astype(f32)
         qc, qs = (q * cosb[...]).astype(bf16), (q * sinb[...]).astype(bf16)
-        st_o[p] = (trecv[p].astype(f32) * late).astype(bf16)
+        st[p] = (trecv[p].astype(f32) * late).astype(bf16)
         zblock = zrecv[p] * late
-        z_o[p] = zblock
+        zst[p] = zblock
         num, den = numer[:, lanes], denom[:, lanes] + 1.0
         for part, feat in ((0, qc), (1, qs)):
-            num += mm(feat, spread_pair(st_o[p, part], diag).astype(bf16))
+            num += mm(feat, spread_pair(st[p, part], diag).astype(bf16))
             den += mm(feat, (column_of(zblock, part) * diag).astype(bf16))
         reciprocal = 1.0 / den
         mix = num * reciprocal
@@ -470,34 +553,38 @@
         mixf[:, lanes] = mix
         mixb[:, lanes] = mix.astype(bf16)
 
+    load(3).wait()
+
     @pl.loop(0, tiles)
     def _(j):
         cols = tile_at(j, TILE)
-        hid[:, cols] = tok[:, cols].astype(f32) + mm(mixb[...], wo[:, cols]) + vec[3:4, cols]
+        hid[:, cols] = (
+            tok[:, cols].astype(f32) + mm(mixb[...], wa[pl.ds(3 * width, width), cols]) + vec[3:4, cols]
+        )
 
     @pl.loop(0, rows // ROWBLOCK)
     def _(i):
         at = tile_at(i, ROWBLOCK)
-        value = hid[at, :]
-        centred = value - jnp.mean(value, axis=-1, keepdims=True)
-        scale = lax.rsqrt(jnp.mean(centred * centred, axis=-1, keepdims=True) + norm_eps)
-        normal = centred * scale
+        normal, scale = layer_norm(hid[at, :])
         hidden = normal * vec[4:5, :] + vec[5:6, :]
         nrm[at, :] = normal
         scl[at, :] = jnp.broadcast_to(scale, (ROWBLOCK, LANES))
         hid[at, :] = hidden
         hbuf[at, :] = hidden.astype(bf16)
 
-    hidden_copy = peer_copy(hbuf.at[own], hbuf.at[other], sems, 2, peer)
-    hidden_copy.start()
+    rows_copy = peer_copy(hbuf.at[own], hbuf.at[far_rows], sems, 2, peer)
+    rows_copy.start()
+    for index in range(4, len(loads)):
+        load(index).wait()
 
     def raise_rows(part):
-        for half in range(units // width):
+        for piece in range(halves):
 
             @pl.loop(0, tiles)
-            def _(j, half=half):
-                cols = tile_at(half * tiles + j, TILE)
-                pre = mm(hbuf[part, :], wup[:, cols]) + vec[9 + half : 10 + half, tile_at(j, TILE)]
+            def _(j, piece=piece):
+                cols, narrow = tile_at(piece * tiles + j, TILE), tile_at(j, TILE)
+                weight = wff[pl.ds(units + piece * width, width), narrow]
+                pre = mm(hbuf[part, :], weight) + vec[9 + piece : 10 + piece, narrow]
                 cdf = 0.5 * (1.0 + lax.erf(pre * (1.0 / math.sqrt(2.0))))
                 act[part, cols] = (pre * cdf).astype(bf16)
                 slope[part, cols] = cdf + pre * jnp.exp(-0.5 * pre * pre) * (
@@ -505,13 +592,13 @@
                 )
 
     raise_rows(own)
-    hidden_copy.wait()
-    raise_rows(other)
+    rows_copy.wait()
+    raise_rows(far_rows)
 
     @pl.loop(0, tiles)
     def _(j):
         cols = tile_at(j, TILE)
-        bsend[:, cols] = mm(act[other, :], wdn[:, cols]).astype(bf16)
+        bsend[:, cols] = mm(act[far_rows, :], wff[pl.ds(0, units), cols]).astype(bf16)
 
     branch_copy = peer_copy(bsend, brecv, sems, 3, peer)
     branch_copy.start()
@@ -519,116 +606,222 @@
     @pl.loop(0, tiles)
     def _(j):
         cols = tile_at(j, TILE)
-        hid[:, cols] += mm(act[own, :], wdn[:, cols]) + vec[6:7, cols]
-
-    acc[...] = jnp.zeros_like(acc)
+        hid[:, cols] += mm(act[own, :], wff[pl.ds(0, units), cols]) + vec[6:7, cols]
+
     branch_copy.wait()
 
     @pl.loop(0, rows // ROWBLOCK)
     def _(i):
         at = tile_at(i, ROWBLOCK)
-        value = hid[at, :] + brecv[at, :].astype(f32)
-        centred = value - jnp.mean(value, axis=-1, keepdims=True)
-        scale = lax.rsqrt(jnp.mean(centred * centred, axis=-1, keepdims=True) + norm_eps)
-        normal = centred * scale
-        res_o[at, :] = (normal * vec[7:8, :] + vec[8:9, :]).astype(bf16)
+        normal, scale = layer_norm(hid[at, :] + brecv[at, :].astype(f32))
+        res[at, :] = (normal * vec[7:8, :] + vec[8:9, :]).astype(bf16)
         grad = og[at, :].astype(f32)
-        along = grad * vec[7:8, :]
-        inner = (
-            along
-            - jnp.mean(along, axis=-1, keepdims=True)
-            - normal * jnp.mean(along * normal, axis=-1, keepdims=True)
-        ) * scale
-        dho_o[at, :] = inner
+        inner = layer_norm_back(grad, vec[7:8, :], normal, scale)
+        dho[at, :] = inner
         dbuf[at, :] = inner.astype(bf16)
         acc[0:8, :] += fold8(grad * normal)
         acc[8:16, :] += fold8(grad)
         acc[16:24, :] += fold8(inner)
 
-    grad_copy = peer_copy(dbuf.at[own], dbuf.at[other], sems, 4, peer)
+    grad_copy = peer_copy(dbuf.at[own], dbuf.at[far_rows], sems, 4, peer)
     grad_copy.start()
-
-    small_o[...] = jnp.zeros_like(small_o)
+    result_out = pltpu.make_async_copy(res, res_h, o_sem.at[0])
+    result_out.start()
     for slot in range(3):
-        small_o[3 + slot : 4 + slot, :] = jnp.sum(
-            acc[8 * slot : 8 * slot + 8, :], axis=0, keepdims=True
-        )
-    bup[...] = jnp.zeros_like(bup)
+        add_small(3 + slot, jnp.sum(acc[8 * slot : 8 * slot + 8, :], axis=0, keepdims=True))
 
     def lower_rows(part):
         @pl.loop(0, units // TILE)
         def _(j):
             cols = tile_at(j, TILE)
-            d_pre = mm_nt(dbuf[part, :], wdn[cols, :]) * slope[part, cols]
+            d_pre = mm_nt(dbuf[part, :], wff[cols, :]) * slope[part, cols]
             bup[:, cols] += fold8(d_pre)
             dpre[part, cols] = d_pre.astype(bf16)
 
+    def lower_hidden(part, cols, j):
+        total = 0.0
+        for piece in range(halves):
+            weight = wff[pl.ds(pl.multiple_of(units + piece * width + j * TILE, TILE), TILE), :]
+            total += mm_nt(dpre[part, piece * width : (piece + 1) * width], weight)
+        return total
+
     lower_rows(own)
     grad_copy.wait()
-    lower_rows(other)
+    lower_rows(far_rows)
 
     @pl.loop(0, tiles)
     def _(j):
         cols = tile_at(j, TILE)
-        dhs_o[:, cols] = mm_nt(dpre[other, :], wup[cols, :]).astype(bf16)
-        dho_o[:, cols] += mm_nt(dpre[own, :], wup[cols, :])
-
-    for half in range(units // width):
-        line = jnp.sum(bup[:, half * width : (half + 1) * width], axis=0, keepdims=True)
-        small_o[9 + half : 10 + half, :] = line * (1.0 - late)
-        small_o[9 + units // width + half : 10 + units // width + half, :] = line * late
+        dhs[:, cols] = lower_hidden(far_rows, cols, j).astype(bf16)
+
+    hidden_copy = peer_copy(dhs, dhr, sems, 5, peer)
+    hidden_copy.start()
 
     @pl.loop(0, units // TILE)
     def _(j):
         cols = tile_at(j, TILE)
-        gff_o[cols, :] = mm_tn(act[:, cols], dbuf[...]).astype(bf16)
-
-    for half in range(units // width):
+        gff[cols, :] = mm_tn(act[:, cols], dbuf[...]).astype(bf16)
+
+    for piece in range(halves):
 
         @pl.loop(0, tiles)
-        def _(j, half=half):
-            gff_o[pl.ds(units + half * width, width), tile_at(j, TILE)] = mm_tn(
-                hbuf[...], dpre[:, tile_at(half * tiles + j, TILE)]
+        def _(j, piece=piece):
+            gff[pl.ds(units + piece * width, width), tile_at(j, TILE)] = mm_tn(
+                hbuf[...], dpre[:, tile_at(piece * tiles + j, TILE)]
             ).astype(bf16)
 
-
-def back_kernel(
-    tok, trig, span, vec, wq, wk, wv, wo,
-    dhs, dho, mixb, mixf, inv, rq, rk, vv, nrm, scl, st, z, small_in,
-    dtok_o, ga_o, small_o,
-    dhr, dres, dlow, dn, xs, dsend, drecv, dzs, dzr, dq, dk, dv, dql, dkl, dvl,
-    ctab, cosb, sinb, acc, send, recv,
-):
-    sems = (send, recv)
-    rows, width = tok.shape
-    pairs = width // LANES
-    tiles = width // TILE
-    rank = lax.axis_index("tensor")
-    peer = (lax.axis_index("dp"), 1 - rank)
-    early = 1.0 - rank.astype(f32)
-    meet([peer])
-    hidden_copy = peer_copy(dhs, dhr, sems, 0, peer)
-    hidden_copy.start()
-    angle_tables(trig, span, cosb, sinb, ctab)
-    diag = pair_mask()
-    first, second = head_masks()
-    first_low, second_low = first.astype(bf16), second.astype(bf16)
-    diag_low = diag.astype(bf16)
+    def part_rows(which, size):
+        return pl.ds(pl.multiple_of(which * size, size), size)
+
+    core_ff = peer_copy(gff.at[part_rows(1 - core, units), :], cr_ff, sems, 8, sibling)
+    core_a = peer_copy(ga.at[part_rows(1 - core, 2 * quarter), :], cr_a, sems, 9, sibling)
+    core_ff.start()
+
+    ff_streams, a_streams = [], []
+    for kind, (cuts, group) in enumerate(((FF_CUTS, ff_streams), (A_CUTS, a_streams))):
+        size = (quarter if kind else units) // count // 2
+        for way in range(2):
+            for cut in range(cuts):
+                number = 2 * FF_CUTS * kind + way * cuts + cut
+                group.append((number, kind, way, pl.ds(cut * (size // cuts), size // cuts), cut, size))
+    slots = (rs_ff, rs_a)
+    sums = (gff, ga)
+    outs = (ff_o, a_o)
+    bases = (core * units, (core * 2 + rank) * quarter)
+
+    def chunk_rows(at, stream, base):
+        _, _, way, piece, cut, size = stream
+        start = base + (at % count) * 2 * size + way * size + cut * piece.size
+        return pl.ds(pl.multiple_of(start, piece.size), piece.size)
+
+    def toward(stream):
+        return behind if stream[2] else ahead
+
+    def sign(stream):
+        return -1 if stream[2] else 1
+
+    def spread_copy(stream, at, s):
+        number, kind, way, piece, _, _ = stream
+        return pltpu.make_async_remote_copy(
+            src_ref=sums[kind].at[chunk_rows(at, stream, bases[kind]), :],
+            dst_ref=slots[kind].at[s, way, piece, :],
+            send_sem=r_send.at[number, s],
+            recv_sem=r_recv.at[number, s],
+            device_id=toward(stream),
+            device_id_type=MESH,
+        )
+
+    def gather_copy(stream, at, s):
+        number, kind = stream[:2]
+        where = outs[kind].at[chunk_rows(at, stream, bases[kind]), :]
+        return pltpu.make_async_remote_copy(
+            src_ref=where,
+            dst_ref=where,
+            send_sem=g_send.at[number, s],
+            recv_sem=g_recv.at[number, s],
+            device_id=toward(stream),
+            device_id_type=MESH,
+        )
+
+    def across_copy(stream, at, s, base):
+        number = stream[0] - 2 * FF_CUTS
+        where = a_o.at[chunk_rows(at, stream, base), :]
+        return pltpu.make_async_remote_copy(
+            src_ref=where,
+            dst_ref=where,
+            send_sem=x_send.at[number, s],
+            recv_sem=x_recv.at[number, s],
+            device_id=peer,
+            device_id_type=MESH,
+        )
+
+    def fold_copy(stream, s):
+        number, _, way, piece, _, _ = stream
+        at = spot + count - sign(stream) * s
+        return pltpu.make_async_remote_copy(
+            src_ref=px.at[chunk_rows(at, stream, 0), :],
+            dst_ref=xr.at[s, way, piece, :],
+            send_sem=y_send.at[number - 2 * FF_CUTS, s],
+            recv_sem=y_recv.at[number - 2 * FF_CUTS, s],
+            device_id=peer,
+            device_id_type=MESH,
+        )
+
+    def own_part(stream, at, s):
+        _, kind, way, piece, _, _ = stream
+        rows_in = chunk_rows(at, stream, bases[kind])
+        if kind == 0:
+            return gff[rows_in, :].astype(f32) + cr_ff[chunk_rows(at, stream, 0), :].astype(f32)
+        fold_copy(stream, s).wait_recv()
+        return (
+            ga[rows_in, :].astype(f32)
+            + cr_a[chunk_rows(at, stream, rank * quarter), :].astype(f32)
+            + xr[s, way, piece, :].astype(f32)
+        )
+
+    def ring_first(streams):
+        for stream in streams:
+            kind, at = stream[1], spot + count
+            sums[kind][chunk_rows(at, stream, bases[kind]), :] = own_part(stream, at, 0).astype(bf16)
+            spread_copy(stream, at, 0).start()
+
+    def ring_spread(streams, s, last):
+        for stream in streams:
+            _, kind, way, piece, _, _ = stream
+            at = spot + count - sign(stream) * (s + 1)
+            target = chunk_rows(at, stream, bases[kind])
+            part = own_part(stream, at, s + 1)
+            spread_copy(stream, at, s).wait_recv()
+            total = (part + slots[kind][s, way, piece, :].astype(f32)).astype(bf16)
+            if last:
+                outs[kind][target, :] = total
+                gather_copy(stream, at, 0).start()
+                if kind:
+                    across_copy(stream, at, 0, bases[1]).start()
+            else:
+                sums[kind][target, :] = total
+                spread_copy(stream, at, s + 1).start()
+
+    def ring_gather(streams, s, last):
+        for stream in streams:
+            at = spot + 2 * count - sign(stream) * s
+            gather_copy(stream, at, s).wait_recv()
+            if not last:
+                gather_copy(stream, at, s + 1).start()
+            if stream[1]:
+                across_copy(stream, at, s + 1, bases[1]).start()
+
+    def small_copy(index):
+        return peer_copy(smalls.at[index], small_r.at[index], (m_send, m_recv), index, swaps[index])
+
+    def swap_small(index):
+        small_copy(index).wait()
+        smalls[index + 1] = smalls[index] + small_r[index]
+        if index + 1 < len(swaps):
+            small_copy(index + 1).start()
+
+    for piece in range(halves):
+        line = jnp.sum(bup[:, piece * width : (piece + 1) * width], axis=0, keepdims=True)
+        add_small(9 + piece, line * early)
+        add_small(9 + halves + piece, line * late)
+
+    @pl.loop(0, tiles)
+    def _(j):
+        cols = tile_at(j, TILE)
+        dho[:, cols] += lower_hidden(own, cols, j)
+
     acc[...] = jnp.zeros_like(acc)
-    small_o[...] = small_in[...]
+    core_ff.wait()
+    ring_first(ff_streams)
     hidden_copy.wait()
+    ring_spread(ff_streams, 0, False)
 
     @pl.loop(0, rows // ROWBLOCK)
     def _(i):
         at = tile_at(i, ROWBLOCK)
         grad = dho[at, :] + dhr[at, :].astype(f32)
         normal = nrm[at, :]
-        along = grad * vec[4:5, :]
-        inner = (
-            along
-            - jnp.mean(along, axis=-1, keepdims=True)
-            - normal * jnp.mean(along * normal, axis=-1, keepdims=True)
-        ) * scl[at, 0:1]
+        inner = layer_norm_back(grad, vec[4:5, :], normal, scl[at, 0:1])
         dres[at, :] = inner
         dlow[at, :] = inner.astype(bf16)
         acc[0:8, :] += fold8(grad * normal)
@@ -636,17 +829,17 @@
         acc[16:24, :] += fold8(inner)
 
     for slot in range(3):
-        small_o[slot : slot + 1, :] = jnp.sum(
-            acc[8 * slot : 8 * slot + 8, :], axis=0, keepdims=True
-        )
+        add_small(slot, jnp.sum(acc[8 * slot : 8 * slot + 8, :], axis=0, keepdims=True))
 
     @pl.loop(0, tiles)
     def _(j):
         cols = tile_at(j, TILE)
-        d_mixed = mm_nt(dlow[...], wo[cols, :]).astype(bf16).astype(f32)
+        d_mixed = mm_nt(dlow[...], wa[tile_at(3 * tiles + j, TILE), :]).astype(bf16).astype(f32)
         d_numer = (d_mixed * inv[:, cols]).astype(bf16)
         dn[:, cols] = d_numer
         xs[:, cols] = (d_numer.astype(f32) * mixf[:, cols]).astype(bf16)
+
+    ring_spread(ff_streams, 1, False)
 
     @pl.loop(0, pairs)
     def _(p):
@@ -657,28 +850,27 @@
         dsend[p, 0] = squeeze_pair(mm_tn(qc, d_numer) * diag).astype(bf16)
         dsend[p, 1] = squeeze_pair(mm_tn(qs, d_numer) * diag).astype(bf16)
         across = mm(xs[:, lanes], diag_low)
-        sum_c = jnp.sum(qc.astype(f32) * across, axis=0, keepdims=True)
-        sum_s = jnp.sum(qs.astype(f32) * across, axis=0, keepdims=True)
-        row = lax.broadcasted_iota(jnp.int32, (8, LANES), 0)
-        dzs[p] = -jnp.where(row == 0, sum_c, jnp.where(row == 1, sum_s, 0.0))
-
-    state_copy = peer_copy(dsend, drecv, sems, 1, peer)
-    key_copy = peer_copy(dzs, dzr, sems, 2, peer)
-    state_copy.start()
-    key_copy.start()
+        dzs[p] = -two_rows(
+            jnp.sum(qc.astype(f32) * across, axis=0, keepdims=True),
+            jnp.sum(qs.astype(f32) * across, axis=0, keepdims=True),
+        )
+
+    turn_copy = peer_copy(dsend, drecv, sems, 6, peer)
+    turn_keys = peer_copy(dzs, dzr, sems, 7, peer)
+    turn_copy.start()
+    turn_keys.start()
+    ring_spread(ff_streams, 2, False)
 
     @pl.loop(0, tiles)
     def _(j):
         cols = tile_at(j, TILE)
-        ga_o[tile_at(3 * tiles + j, TILE), :] = mm_tn(mixb[:, cols], dlow[...]).astype(bf16)
-
-    @pl.loop(0, pairs)
-    def _(p):
+        ga[tile_at(3 * tiles + j, TILE), :] = mm_tn(mixb[:, cols], dlow[...]).astype(bf16)
+
+    def inside(p):
         lanes = tile_at(p, LANES)
         q, k, v = rq[:, lanes], rk[:, lanes], vv[:, lanes]
         d_numer = dn[:, lanes]
-        turned = -pltpu.roll(xs[:, lanes].astype(f32), HD, 1)
-        turned = turned.astype(bf16)
+        turned = (-pltpu.roll(xs[:, lanes].astype(f32), HD, 1)).astype(bf16)
         sum_q = sum_k = sum_v = 0.0
         for mask, rest in ((first_low, second_low), (second_low, first_low)):
             q_head, k_head, d_head = q * mask, k * mask, d_numer * mask
@@ -693,8 +885,12 @@
         dk[:, lanes] = sum_k
         dv[:, lanes] = sum_v
 
-    state_copy.wait()
-    key_copy.wait()
+    pl.loop(0, pairs // 2)(inside)
+    ring_spread(ff_streams, 3, False)
+    pl.loop(pairs // 2, pairs)(inside)
+    ring_spread(ff_streams, 4, False)
+    turn_copy.wait()
+    turn_keys.wait()
 
     @pl.loop(0, pairs)
     def _(p):
@@ -703,7 +899,7 @@
         k = rk[:, lanes].astype(f32)
         d_numer, x = dn[:, lanes], xs[:, lanes]
         sum_q, sum_k, sum_v = dq[:, lanes], dk[:, lanes], dv[:, lanes]
-        zblock, dzblock = z[p], dzr[p] * early
+        zblock, dzblock = zst[p], dzr[p] * early
         for part, wave in ((0, cosb[...]), (1, sinb[...])):
             state = spread_pair(st[p, part], diag).astype(bf16)
             zmat = (column_of(zblock, part) * diag).astype(bf16)
@@ -717,29 +913,169 @@
         dkl[:, lanes] = sum_k.astype(bf16)
         dvl[:, lanes] = sum_v.astype(bf16)
         for slot, value in ((6, sum_q), (7, sum_k), (8, sum_v)):
-            small_o[slot : slot + 1, lanes] = jnp.sum(value, axis=0, keepdims=True)
+            smalls[0, slot : slot + 1, lanes] = jnp.sum(value, axis=0, keepdims=True)
+
+    small_copy(0).start()
+    ring_spread(ff_streams, 5, False)
 
     for which, source in enumerate((dql, dkl, dvl)):
 
         @pl.loop(0, tiles)
         def _(j, which=which, source=source):
-            ga_o[tile_at(which * tiles + j, TILE), :] = mm_tn(
+            ga[tile_at(which * tiles + j, TILE), :] = mm_tn(
                 tok[:, tile_at(j, TILE)], source[...]
             ).astype(bf16)
+
+    core_a.start()
+    ring_spread(ff_streams, count - 2, True)
 
     @pl.loop(0, tiles)
     def _(j):
         cols = tile_at(j, TILE)
-        dtok_o[:, cols] = (
-            dres[:, cols]
-            + mm_nt(dql[...], wq[cols, :])
-            + mm_nt(dkl[...], wk[cols, :])
-            + mm_nt(dvl[...], wv[cols, :])
+        dres[:, cols] += (
+            mm_nt(dql[...], wa[cols, :])
+            + mm_nt(dkl[...], wa[tile_at(tiles + j, TILE), :])
+            + mm_nt(dvl[...], wa[tile_at(2 * tiles + j, TILE), :])
         )
 
-
-def in_vmem(count):
-    return [pl.BlockSpec(memory_space=pltpu.VMEM)] * count
+    token_out = pltpu.make_async_copy(dres, dtok_h, o_sem.at[1])
+    token_out.start()
+    core_a.wait()
+
+    @pl.loop(0, quarter // 96)
+    def _(i):
+        near = pl.ds(pl.multiple_of((core * 2 + 1 - rank) * quarter + i * 96, 96), 96)
+        far = pl.ds(pl.multiple_of((1 - rank) * quarter + i * 96, 96), 96)
+        px[tile_at(i, 96), :] = (ga[near, :].astype(f32) + cr_a[far, :].astype(f32)).astype(bf16)
+
+    for s in range(3):
+        for stream in a_streams:
+            fold_copy(stream, s).start()
+    swap_small(0)
+    ring_first(a_streams)
+
+    def both_steps(s):
+        @pl.when(s + 3 < count)
+        def _():
+            for stream in a_streams:
+                fold_copy(stream, s + 3).start()
+
+        ring_gather(ff_streams, s, False)
+        ring_spread(a_streams, s, False)
+
+    pl.loop(0, 2)(both_steps)
+    swap_small(1)
+    pl.loop(2, 4)(both_steps)
+    swap_small(2)
+    pl.loop(4, count - 2)(both_steps)
+    swap_small(3)
+    ring_gather(ff_streams, count - 2, True)
+    own_ff, own_a = part_rows(core, units), part_rows(core, 2 * quarter)
+    back_ff = peer_copy(ff_o.at[own_ff, :], ff_o.at[own_ff, :], sems, 10, sibling)
+    back_ff.start()
+    near_ff = out_copy(ff_o, ff_h, own_ff, 2)
+    near_ff.start()
+    ring_spread(a_streams, count - 2, True)
+    pl.loop(0, 2)(lambda s: ring_gather(a_streams, s, False))
+    swap_small(4)
+    small_out = pltpu.make_async_copy(smalls.at[len(swaps)], small_h, o_sem.at[6])
+    small_out.start()
+    back_ff.wait()
+    far_ff = out_copy(ff_o, ff_h, part_rows(1 - core, units), 3)
+    far_ff.start()
+    pl.loop(2, count - 2)(lambda s: ring_gather(a_streams, s, False))
+    ring_gather(a_streams, count - 2, True)
+    crossed = (core * 2 + 1 - rank) * quarter
+
+    @pl.loop(0, count)
+    def _(s):
+        for stream in a_streams:
+            at = spot + 2 * count + sign(stream) * (1 - s)
+            across_copy(stream, at, s, crossed).wait_recv()
+
+    back_a = peer_copy(a_o.at[own_a, :], a_o.at[own_a, :], sems, 11, sibling)
+    back_a.start()
+    near_a = out_copy(a_o, a_h, own_a, 4)
+    near_a.start()
+
+    @pl.loop(0, count - 1)
+    def _(s):
+        for stream in ff_streams + a_streams:
+            spread_copy(stream, spot, s).wait_send()
+            gather_copy(stream, spot, s).wait_send()
+
+    @pl.loop(0, count)
+    def _(s):
+        for stream in a_streams:
+            across_copy(stream, spot, s, bases[1]).wait_send()
+            fold_copy(stream, s).wait_send()
+
+    back_a.wait()
+    far_a = out_copy(a_o, a_h, part_rows(1 - core, 2 * quarter), 5)
+    far_a.start()
+    for copy in (result_out, token_out, near_ff, far_ff, small_out, near_a, far_a):
+        copy.wait()
+
+
+def finish_kernel(halves, *refs):
+    g_out, up, down, small, res, dtok = refs[:4], refs[4 : 4 + halves], *refs[4 + halves : 8 + halves]
+    out = refs[8 + halves :]
+    late = lax.axis_index("tensor") > 0
+    for source, where in zip(g_out, (2, 4, 6, 8)):
+        out[where][...] = source[...].astype(f32)
+    width = res.shape[1]
+    for piece in range(halves):
+        out[12][:, piece * width : (piece + 1) * width] = up[piece][...].astype(f32)
+    out[14][...] = down[...].astype(f32)
+
+    @pl.when(pl.program_id(0) == 0)
+    def _():
+        out[0][...] = res[...]
+        out[1][...] = dtok[...]
+        for where, row in ((3, 6), (5, 7), (7, 8), (9, 2), (10, 0), (11, 1), (15, 5), (16, 3), (17, 4)):
+            out[where][...] = small[row : row + 1, :].reshape(width)
+        for piece in range(halves):
+            line = jnp.where(
+                late,
+                small[9 + halves + piece : 10 + halves + piece, :],
+                small[9 + piece : 10 + piece, :],
+            )
+            out[13][pl.ds(piece * width, width)] = line.reshape(width)
+
+
+def finish(rows, width, units, res, dtok, ff, a, small):
+    halves, steps = units // width, width // LANES
+    low = (LANES, width)
+    down_rows = units // steps
+
+    def whole(shape):
+        return pl.BlockSpec(shape, lambda i: (0,) * len(shape))
+
+    def at_block(shape, start):
+        return pl.BlockSpec(shape, lambda i: (start + i, 0))
+
+    in_specs = [at_block(low, which * steps) for which in range(4)]
+    in_specs += [at_block(low, units // LANES + piece * steps) for piece in range(halves)]
+    in_specs += [at_block((down_rows, width), 0), whole(small.shape), whole(res.shape), whole(dtok.shape)]
+    matrix, line = (width, width), (width,)
+    shapes = [
+        (res.shape, bf16), (dtok.shape, f32), (matrix, f32), (line, f32), (matrix, f32), (line, f32),
+        (matrix, f32), (line, f32), (matrix, f32), (line, f32), (line, f32), (line, f32),
+        ((width, units), f32), ((units,), f32), ((units, width), f32), (line, f32), (line, f32), (line, f32),
+    ]
+    special = {
+        2: at_block(low, 0), 4: at_block(low, 0), 6: at_block(low, 0), 8: at_block(low, 0),
+        12: at_block((LANES, units), 0), 14: at_block((down_rows, width), 0),
+    }
+    return pl.pallas_call(
+        functools.partial(finish_kernel, halves),
+        grid=(steps,),
+        out_shape=shaped(*shapes),
+        in_specs=in_specs,
+        out_specs=tuple(special.get(i, whole(shape)) for i, (shape, _) in enumerate(shapes)),
+        compiler_params=pltpu.CompilerParams(vmem_limit_bytes=62 << 20),
+        name="finish",
+    )(*([a] * 4), *([ff] * (halves + 1)), small, res, dtok)
 
 
 def shaped(*items):
@@ -768,145 +1104,87 @@
     norm2_bias,
     out_grad,
 ):
-    rank = lax.axis_index("tensor")
     rows, width = tokens.shape
     units = w_up.shape[1]
     pairs = width // LANES
-    length = positions.shape[0]
-    places = lax.dynamic_slice_in_dim(positions, rank * rows, rows, 0)
-    angle = math.pi / 2 * places.astype(f32) / (3 * length)
-    line = lax.broadcasted_iota(jnp.int32, (8, rows), 0)
-    trig = jnp.where(
-        line == 0, jnp.cos(angle)[None], jnp.where(line == 1, jnp.sin(angle)[None], 0.0)
-    )
-    span = span_sizes.reshape(1, 1)
-    vectors = [
-        b_query, b_key, b_value, b_out, norm1_gain, norm1_bias, b_down, norm2_gain, norm2_bias, b_up,
-    ]
-    vec = jnp.concatenate(vectors).astype(f32).reshape(-1, width)
-    vec = jnp.pad(vec, ((0, -vec.shape[0] % 8), (0, 0)))
-    smalls = 9 + 2 * (units // width)
-    smalls += -smalls % 8
-    state = (pairs, 2, HD, LANES)
-    zrows = (pairs, 8, LANES)
-    wide, low, both = ((rows, width), f32), ((rows, width), bf16), (2 * rows, width)
-    front_outs = shaped(
-        low, ((smalls, width), f32), ((2 * units, width), bf16), low, wide, low, wide, wide,
-        low, low, low, wide, ((rows, LANES), f32), (state, bf16), (zrows, f32),
-    )
-    tables = [
-        pltpu.VMEM((rows, rows), f32), pltpu.VMEM((rows, LANES), f32), pltpu.VMEM((rows, LANES), f32),
-    ]
-    smem = [pl.BlockSpec(memory_space=pltpu.SMEM)]
-    (
-        result, small, gff, dhs, dho, mixb, mixf, inv, rq, rk, vv, nrm, scl, st, z,
-    ) = pl.pallas_call(
-        front_kernel,
-        out_shape=front_outs,
-        in_specs=in_vmem(2) + smem + in_vmem(8),
-        out_specs=tuple(in_vmem(len(front_outs))),
-        scratch_shapes=[
-            pltpu.VMEM(both, bf16),
-            pltpu.VMEM((2 * rows, units), bf16),
-            pltpu.VMEM((2 * rows, units), f32),
-            pltpu.VMEM(both, bf16),
-            pltpu.VMEM((2 * rows, units), bf16),
-            pltpu.VMEM((rows, width), f32),
-            pltpu.VMEM(state, bf16),
-            pltpu.VMEM(state, bf16),
-            pltpu.VMEM(zrows, f32),
-            pltpu.VMEM(zrows, f32),
-            pltpu.VMEM((rows, width), bf16),
-            pltpu.VMEM((rows, width), bf16),
-            pltpu.VMEM((rows, width), f32),
-            pltpu.VMEM((rows, width), f32),
-            *tables,
-            pltpu.VMEM((24, width), f32),
-            pltpu.VMEM((8, units), f32),
-            pltpu.SemaphoreType.DMA((5,)),
-            pltpu.SemaphoreType.DMA((5,)),
-        ],
+    halves = units // width
+    count = lax.axis_size("dp") // 2
+    swaps = 2 + count.bit_length() - 1
+    streams = 2 * (FF_CUTS + A_CUTS)
+    ff_part, a_part = units // count // 2, width // count // 2
+    lines = 9 + 2 * halves
+    lines += -lines % 8
+
+    def low(*shape):
+        return pltpu.VMEM(shape, bf16)
+
+    def wide(*shape):
+        return pltpu.VMEM(shape, f32)
+
+    def sem(*shape):
+        return pltpu.SemaphoreType.DMA(shape)
+
+    state, zrows = (pairs, 2, HD, LANES), (pairs, 8, LANES)
+    own, pair = (rows, width), (2 * rows, width)
+    scratch = dict(
+        wa=low(4 * width, width), wff=low(2 * units, width), vec=wide(9 + halves + -(9 + halves) % 8, width),
+        hbuf=low(*pair), act=low(2 * rows, units), slope=wide(2 * rows, units), dbuf=low(*pair),
+        dpre=low(2 * rows, units), hid=wide(*own), numer=wide(*own), denom=wide(*own),
+        tsend=low(*state), trecv=low(*state), zsend=wide(*zrows), zrecv=wide(*zrows),
+        bsend=low(*own), brecv=low(*own), res=low(*own), gff=low(2 * units, width),
+        dhs=low(*own), dhr=low(*own), dho=wide(*own), mixb=low(*own), mixf=wide(*own), inv=wide(*own),
+        rq=low(*own), rk=low(*own), vv=low(*own), nrm=wide(*own), scl=wide(rows, LANES),
+        st=low(*state), zst=wide(*zrows), dres=wide(*own), dlow=low(*own), dn=low(*own), xs=low(*own),
+        dsend=low(*state), drecv=low(*state), dzs=wide(*zrows), dzr=wide(*zrows),
+        dql=low(*own), dkl=low(*own), dvl=low(*own),
+        ctab=wide(rows, rows), cosb=wide(rows, LANES), sinb=wide(rows, LANES),
+        acc=wide(24, width), bup=wide(8, units),
+        cr_ff=low(units, width), cr_a=low(2 * width, width), px=low(width, width),
+        xr=low(count, 2, a_part, width), rs_ff=low(count - 1, 2, ff_part, width),
+        rs_a=low(count - 1, 2, a_part, width), ff_o=low(2 * units, width), a_o=low(4 * width, width),
+        smalls=wide(swaps + 1, lines, width), small_r=wide(swaps, lines, width),
+        send=sem(12), recv=sem(12), r_send=sem(streams, count - 1), r_recv=sem(streams, count - 1),
+        g_send=sem(streams, count - 1), g_recv=sem(streams, count - 1),
+        x_send=sem(2 * A_CUTS, count), x_recv=sem(2 * A_CUTS, count),
+        y_send=sem(2 * A_CUTS, count), y_recv=sem(2 * A_CUTS, count),
+        m_send=sem(swaps), m_recv=sem(swaps), w_sem=sem(5 + halves), o_sem=sem(7),
+    )
+    vmem, anywhere = pl.BlockSpec(memory_space=pltpu.VMEM), pl.BlockSpec(memory_space=pl.ANY)
+    outs = shaped(
+        (own, bf16), (own, f32), ((2 * units, width), bf16), ((4 * width, width), bf16),
+        ((lines, width), f32),
+    )
+    res, dtok, ff, a, small = pl.pallas_call(
+        functools.partial(block_kernel, count),
+        out_shape=outs,
+        in_specs=[vmem] * 2 + [pl.BlockSpec(memory_space=pltpu.SMEM)] + [vmem] * 11 + [anywhere] * 6,
+        out_specs=tuple([anywhere] * len(outs)),
+        scratch_shapes=list(scratch.values()),
         compiler_params=pltpu.CompilerParams(
-            collective_id=0, has_side_effects=True, vmem_limit_bytes=60 << 20
+            collective_id=0, has_side_effects=True, vmem_limit_bytes=62 << 20
         ),
-        name="front",
-    )(tokens, trig, span, vec, w_query, w_key, w_value, w_out, w_up, w_down, out_grad)
-    back_outs = shaped(wide, ((4 * width, width), bf16), ((smalls, width), f32))
-    d_tokens, ga, small = pl.pallas_call(
-        back_kernel,
-        out_shape=back_outs,
-        in_specs=in_vmem(2) + smem + in_vmem(18),
-        out_specs=tuple(in_vmem(len(back_outs))),
-        scratch_shapes=[
-            pltpu.VMEM((rows, width), bf16),
-            pltpu.VMEM((rows, width), f32),
-            pltpu.VMEM((rows, width), bf16),
-            pltpu.VMEM((rows, width), bf16),
-            pltpu.VMEM((rows, width), bf16),
-            pltpu.VMEM(state, bf16),
-            pltpu.VMEM(state, bf16),
-            pltpu.VMEM(zrows, f32),
-            pltpu.VMEM(zrows, f32),
-            pltpu.VMEM((rows, width), f32),
-            pltpu.VMEM((rows, width), f32),
-            pltpu.VMEM((rows, width), f32),
-            pltpu.VMEM((rows, width), bf16),
-            pltpu.VMEM((rows, width), bf16),
-            pltpu.VMEM((rows, width), bf16),
-            *tables,
-            pltpu.VMEM((24, width), f32),
-            pltpu.SemaphoreType.DMA((3,)),
-            pltpu.SemaphoreType.DMA((3,)),
-        ],
-        compiler_params=pltpu.CompilerParams(
-            collective_id=1, has_side_effects=True, vmem_limit_bytes=60 << 20
-        ),
-        name="back",
+        name="block",
     )(
-        tokens, trig, span, vec, w_query, w_key, w_value, w_out,
-        dhs, dho, mixb, mixf, inv, rq, rk, vv, nrm, scl, st, z, small,
-    )
-    gff = lax.psum(gff, "dp")
-    ga = lax.psum(ga, ("dp", "tensor"))
-    small = lax.psum(small, ("dp", "tensor"))
-    halves = units // width
-    g_up = jnp.concatenate(
-        [gff[units + h * width : units + (h + 1) * width] for h in range(halves)], axis=1
-    )
-    g_upbias = lax.dynamic_slice_in_dim(small, 9 + rank * halves, halves, 0).reshape(units)
-    return (
-        result,
-        d_tokens,
-        ga[:width].astype(f32),
-        small[6],
-        ga[width : 2 * width].astype(f32),
-        small[7],
-        ga[2 * width : 3 * width].astype(f32),
-        small[8],
-        ga[3 * width :].astype(f32),
-        small[2],
-        small[0],
-        small[1],
-        g_up.astype(f32),
-        g_upbias,
-        gff[:units].astype(f32),
-        small[5],
-        small[3],
-        small[4],
-    )
+        tokens, positions, span_sizes.reshape(1, 1), b_query, b_key, b_value, b_out, norm1_gain,
+        norm1_bias, b_down, norm2_gain, norm2_bias, b_up, out_grad,
+        w_query, w_key, w_value, w_out, w_up, w_down,
+    )
+    return finish(rows, width, units, res, dtok, ff, a, small)
 
 
 def pick(mesh):
     def per_device(*args):
         tokens, span_sizes, w_up = args[0], args[2], args[13]
         rows, width = tokens.shape
+        units = w_up.shape[1]
         fits = (
             mesh.shape["tensor"] == 2
+            and mesh.shape["dp"] == 16
             and span_sizes.shape[0] == 1
             and rows % TILE == 0
+            and width == HEADS * HD
             and width % TILE == 0
-            and w_up.shape[1] % width == 0
-            and w_up.shape[1] // width <= 3
+            and units == 2 * width
         )
         return pair_device(*args) if fits else general_device(*args)
 

time: 369 us -> 188 us (0.51)
  waiting for transfers between devices: 185 us -> 0 us
  Pallas kernels: 99.6 us -> 186 us
  blocking collectives: 40.3 us -> 0 us
  local copies, waits for them, and re-layouts: 15 us -> 0 us
  other arithmetic: 13.9 us -> 0 us
  between operations: 14.8 us -> 1.32 us
    psum x2 -> x0, waiting for transfers between devices: 185 us -> none  [the longest x1 142 us: pair_device(): ga = lax.psum(ga, ('dp', 'tensor'))]
    pallas_call x2, Pallas kernels: 99.6 us -> 186 us  [the longest x1 174 us: pair_device(): pl.pallas_call(functools.partial(block_kernel, count), out_shape=outs, in...]
    psum x1 -> x0, blocking collectives: 40.3 us -> none  [pair_device(): small = lax.psum(small, ('dp', 'tensor'))]
    convert_element_type x3 -> x0, other arithmetic: 11.8 us -> none  [the longest x1 6.18 us: pair_device(): ga[3 * width:].astype(f32)]
    unnamed x19 -> x0, local copies, waits for them, and re-layouts: 11.1 us -> none
  transfers between devices with their start and end apart: 2 -> 0, of which waited for: 2 -> 0; matrix products, arithmetic and copies ran while one was open for 2% -> 0% of each run, Pallas kernels for 9% -> 0%
where the time goes in v4:
time: 188 us; the launch traced here: 187 us
  Pallas kernels  186 us (99%)
    pallas_call x1, Pallas kernels, pair_device(): pl.pallas_call(functools.partial(block_kernel, count), out_shape=outs, in...  174 us
    pallas_call x1, Pallas kernels, finish(): pl.pallas_call(functools.partial(finish_kernel, halves), grid=(steps,), o...  12.2 us

profile of v4, /device:TPU:0, one launch (start us, length us, event | category | flops | bytes accessed | tf_op | source)
XLA Modules:
  0.0 187.4 jit_solution(10759860043991889939)
XLA Ops:
  1.3 173.9 %block.1 = (bf16[256,768]{1,0:T(8,128)(2,1)}, f32[256,768]{1,0:T(8,128)}, bf16[3072,768]{1,0:T(8,128)(2,1)}, bf16[3072,768]{1,0:T(8,128)(2,1)}, f32[16,768]{1,0:T(8,128)}) custom-call(bf16[256,768]{1,0:T(8,128)(2,1)} %tok.1, s32[512]{0:T(512)} %places.1, s32[1,1]{1,0:T(1,128)} %bitcast.1.span, bf16[768]{0:T(1024)(128)(2,1)} %bq.1, bf16[768]{0:T(1024)(128)(2,1)} %bk.1, ...), custom_call_target="tpu_custom_call" | custom-call | tf_op jit(solution)/shard_map/block/pallas_call | solution.py:1157
  175.2 12.2 %finish.1 = (bf16[256,768]{1,0:T(8,128)(2,1)}, f32[256,768]{1,0:T(8,128)}, f32[768,768]{1,0:T(8,128)}, f32[768]{0:T(1024)}, f32[768,768]{1,0:T(8,128)}, /*index=...) custom-call(bf16[3072,768]{1,0:T(8,128)(2,1)} %get-tuple-element.23., ...), custom_call_target="tpu_custom_call" | custom-call | tf_op jit(solution)/shard_map/finish/pallas_call | solution.py:1070

commit v5 on v4

--- a/solution.py
+++ b/solution.py
@@ -295,6 +295,7 @@
 ROWBLOCK = 32
 FF_CUTS = 3
 A_CUTS = 3
+LINES = tuple("l" + str(index) for index in range(9))
 
 
 def tile_at(index, size):
@@ -407,15 +408,15 @@
 
 
 def block_kernel(
-    count, tok, places, span, bq, bk, bv, bo, g1, b1, bd, g2, b2, bup_in, og,
+    count, tok_h, places_h, span_h, bq, bk, bv, bo, g1, b1, bd, g2, b2, bup_in, og_h,
     wq, wk, wv, wo, wup, wdn,
     res_h, dtok_h, ff_h, a_h, small_h,
-    wa, wff, vec, hbuf, act, slope, dbuf, dpre, hid, numer, denom, tsend, trecv, zsend, zrecv,
+    tok, places, span, og, l0, l1, l2, l3, l4, l5, l6, l7, l8, bup_line, wa, wff, vec, hbuf, act, slope, dbuf, dpre, hid, numer, denom, tsend, trecv, zsend, zrecv,
     bsend, brecv, res, gff, dhs, dhr, dho, mixb, mixf, inv, rq, rk, vv, nrm, scl, st, zst,
     dres, dlow, dn, xs, dsend, drecv, dzs, dzr, dql, dkl, dvl, ctab, cosb, sinb, acc, bup,
     cr_ff, cr_a, px, xr, rs_ff, rs_a, ff_o, a_o, smalls, small_r,
-    send, recv, r_send, r_recv, g_send, g_recv, x_send, x_recv, y_send, y_recv, m_send, m_recv,
-    w_sem, o_sem,
+    send, recv, r_send, r_recv, g_send, g_recv, x_send, x_recv, s_recv, y_recv, m_send, m_recv,
+    w_sem, o_sem, l_sem,
 ):
     sems = (send, recv)
     rows, width = tok.shape
@@ -461,16 +462,30 @@
     def load(index):
         return pltpu.make_async_copy(loads[index][0], loads[index][1], w_sem.at[index])
 
-    for index in range(len(loads)):
+    small_loads = [(tok_h, tok), (places_h, places), (span_h, span)]
+    vectors = (bq, bk, bv, bo, g1, b1, bd, g2, b2)
+    lines = (l0, l1, l2, l3, l4, l5, l6, l7, l8)
+    small_loads += [pair for pair in zip(vectors, lines)]
+    small_loads += [(bup_in, bup_line), (og_h, og)]
+
+    def fetch(index):
+        return pltpu.make_async_copy(*small_loads[index], l_sem.at[index])
+
+    fetch(0).start()
+    for index in range(3):
         load(index).start()
+    for index in range(1, len(small_loads)):
+        fetch(index).start()
+    for index in range(1, len(small_loads) - 1):
+        fetch(index).wait()
 
     def out_copy(source, target, at, slot):
         return pltpu.make_async_copy(source.at[at, :], target.at[at, :], o_sem.at[slot])
 
-    for index, source in enumerate((bq, bk, bv, bo, g1, b1, bd, g2, b2)):
-        vec[index : index + 1, :] = source[...].astype(f32).reshape(1, width)
+    for index in range(len(vectors)):
+        vec[index : index + 1, :] = lines[index][...].astype(f32).reshape(1, width)
     for part in range(halves):
-        piece = bup_in[pl.ds(part * width, width)]
+        piece = bup_line[pl.ds(part * width, width)]
         vec[9 + part : 10 + part, :] = piece.astype(f32).reshape(1, width)
     own, far_rows = pl.ds(0, rows), pl.ds(rows, rows)
     my_places = places[pl.ds(pl.multiple_of(rank * rows, rows), rows)]
@@ -495,10 +510,13 @@
                 value = jnp.maximum(value, 0.0)
             target[:, cols] = value.astype(bf16)
 
+    fetch(0).wait()
     load(0).wait()
     project(1, rk)
     load(1).wait()
     project(2, vv)
+    for index in range(3, len(loads)):
+        load(index).start()
 
     @pl.loop(0, pairs)
     def _(p):
@@ -543,10 +561,10 @@
         st[p] = (trecv[p].astype(f32) * late).astype(bf16)
         zblock = zrecv[p] * late
         zst[p] = zblock
-        num, den = numer[:, lanes], denom[:, lanes] + 1.0
+        weighted = qc.astype(f32) * zblock[0:1, :] + qs.astype(f32) * zblock[1:2, :]
+        num, den = numer[:, lanes], denom[:, lanes] + 1.0 + mm(weighted.astype(bf16), diag_low)
         for part, feat in ((0, qc), (1, qs)):
             num += mm(feat, spread_pair(st[p, part], diag).astype(bf16))
-            den += mm(feat, (column_of(zblock, part) * diag).astype(bf16))
         reciprocal = 1.0 / den
         mix = num * reciprocal
         inv[:, lanes] = reciprocal
@@ -562,8 +580,12 @@
             tok[:, cols].astype(f32) + mm(mixb[...], wa[pl.ds(3 * width, width), cols]) + vec[3:4, cols]
         )
 
-    @pl.loop(0, rows // ROWBLOCK)
-    def _(i):
+    span_rows = rows // 2
+    near = [pl.ds(k * span_rows, span_rows) for k in range(2)]
+    away = [pl.ds(rows + k * span_rows, span_rows) for k in range(2)]
+    blocks = span_rows // ROWBLOCK
+
+    def norm_rows(i):
         at = tile_at(i, ROWBLOCK)
         normal, scale = layer_norm(hid[at, :])
         hidden = normal * vec[4:5, :] + vec[5:6, :]
@@ -572,10 +594,24 @@
         hid[at, :] = hidden
         hbuf[at, :] = hidden.astype(bf16)
 
-    rows_copy = peer_copy(hbuf.at[own], hbuf.at[far_rows], sems, 2, peer)
-    rows_copy.start()
+    def rows_copy(k):
+        return peer_copy(hbuf.at[near[k]], hbuf.at[away[k]], sems, 12 + k, peer)
+
+    def branch_copy(k):
+        return peer_copy(bsend.at[near[k]], brecv.at[near[k]], sems, 14 + k, peer)
+
+    def grad_copy(k):
+        return peer_copy(dbuf.at[near[k]], dbuf.at[away[k]], sems, 16 + k, peer)
+
+    def hidden_copy(k):
+        return peer_copy(dhs.at[near[k]], dhr.at[near[k]], sems, 18 + k, peer)
+
+    for k in range(2):
+        pl.loop(k * blocks, (k + 1) * blocks)(norm_rows)
+        rows_copy(k).start()
     for index in range(4, len(loads)):
         load(index).wait()
+    fetch(len(small_loads) - 1).wait()
 
     def raise_rows(part):
         for piece in range(halves):
@@ -592,26 +628,23 @@
                 )
 
     raise_rows(own)
-    rows_copy.wait()
-    raise_rows(far_rows)
-
-    @pl.loop(0, tiles)
-    def _(j):
-        cols = tile_at(j, TILE)
-        bsend[:, cols] = mm(act[far_rows, :], wff[pl.ds(0, units), cols]).astype(bf16)
-
-    branch_copy = peer_copy(bsend, brecv, sems, 3, peer)
-    branch_copy.start()
+    for k in range(2):
+        rows_copy(k).wait()
+        raise_rows(away[k])
+
+        @pl.loop(0, tiles)
+        def _(j, k=k):
+            cols = tile_at(j, TILE)
+            bsend[near[k], cols] = mm(act[away[k], :], wff[pl.ds(0, units), cols]).astype(bf16)
+
+        branch_copy(k).start()
 
     @pl.loop(0, tiles)
     def _(j):
         cols = tile_at(j, TILE)
         hid[:, cols] += mm(act[own, :], wff[pl.ds(0, units), cols]) + vec[6:7, cols]
 
-    branch_copy.wait()
-
-    @pl.loop(0, rows // ROWBLOCK)
-    def _(i):
+    def finish_rows(i):
         at = tile_at(i, ROWBLOCK)
         normal, scale = layer_norm(hid[at, :] + brecv[at, :].astype(f32))
         res[at, :] = (normal * vec[7:8, :] + vec[8:9, :]).astype(bf16)
@@ -623,8 +656,10 @@
         acc[8:16, :] += fold8(grad)
         acc[16:24, :] += fold8(inner)
 
-    grad_copy = peer_copy(dbuf.at[own], dbuf.at[far_rows], sems, 4, peer)
-    grad_copy.start()
+    for k in range(2):
+        branch_copy(k).wait()
+        pl.loop(k * blocks, (k + 1) * blocks)(finish_rows)
+        grad_copy(k).start()
     result_out = pltpu.make_async_copy(res, res_h, o_sem.at[0])
     result_out.start()
     for slot in range(3):
@@ -646,150 +681,188 @@
         return total
 
     lower_rows(own)
-    grad_copy.wait()
-    lower_rows(far_rows)
-
-    @pl.loop(0, tiles)
-    def _(j):
-        cols = tile_at(j, TILE)
-        dhs[:, cols] = lower_hidden(far_rows, cols, j).astype(bf16)
-
-    hidden_copy = peer_copy(dhs, dhr, sems, 5, peer)
-    hidden_copy.start()
-
-    @pl.loop(0, units // TILE)
-    def _(j):
-        cols = tile_at(j, TILE)
-        gff[cols, :] = mm_tn(act[:, cols], dbuf[...]).astype(bf16)
-
-    for piece in range(halves):
+    for k in range(2):
+        grad_copy(k).wait()
+        lower_rows(away[k])
 
         @pl.loop(0, tiles)
-        def _(j, piece=piece):
-            gff[pl.ds(units + piece * width, width), tile_at(j, TILE)] = mm_tn(
-                hbuf[...], dpre[:, tile_at(piece * tiles + j, TILE)]
-            ).astype(bf16)
+        def _(j, k=k):
+            cols = tile_at(j, TILE)
+            dhs[near[k], cols] = lower_hidden(away[k], cols, j).astype(bf16)
+
+        hidden_copy(k).start()
+
+    def make_down():
+        @pl.loop(0, units // TILE)
+        def _(j):
+            cols = tile_at(j, TILE)
+            gff[cols, :] = mm_tn(act[:, cols], dbuf[...]).astype(bf16)
+
+    def make_up():
+        for piece in range(halves):
+
+            @pl.loop(0, tiles)
+            def _(j, piece=piece):
+                gff[pl.ds(units + piece * width, width), tile_at(j, TILE)] = mm_tn(
+                    hbuf[...], dpre[:, tile_at(piece * tiles + j, TILE)]
+                ).astype(bf16)
 
     def part_rows(which, size):
         return pl.ds(pl.multiple_of(which * size, size), size)
 
     core_ff = peer_copy(gff.at[part_rows(1 - core, units), :], cr_ff, sems, 8, sibling)
-    core_a = peer_copy(ga.at[part_rows(1 - core, 2 * quarter), :], cr_a, sems, 9, sibling)
+    pl.when(core == 0)(make_up)
+    pl.when(core == 1)(make_down)
     core_ff.start()
-
+    pl.when(core == 0)(make_down)
+    pl.when(core == 1)(make_up)
+
+    band, per = width // 4, count // 4
     ff_streams, a_streams = [], []
     for kind, (cuts, group) in enumerate(((FF_CUTS, ff_streams), (A_CUTS, a_streams))):
         size = (quarter if kind else units) // count // 2
         for way in range(2):
             for cut in range(cuts):
                 number = 2 * FF_CUTS * kind + way * cuts + cut
-                group.append((number, kind, way, pl.ds(cut * (size // cuts), size // cuts), cut, size))
-    slots = (rs_ff, rs_a)
-    sums = (gff, ga)
-    outs = (ff_o, a_o)
-    bases = (core * units, (core * 2 + rank) * quarter)
-
-    def chunk_rows(at, stream, base):
-        _, _, way, piece, cut, size = stream
-        start = base + (at % count) * 2 * size + way * size + cut * piece.size
-        return pl.ds(pl.multiple_of(start, piece.size), piece.size)
-
-    def toward(stream):
-        return behind if stream[2] else ahead
-
-    def sign(stream):
-        return -1 if stream[2] else 1
-
-    def spread_copy(stream, at, s):
-        number, kind, way, piece, _, _ = stream
+                piece = size // cuts
+                group.append((number, kind, way, cut * piece, piece))
+    slots, sums, outs = (rs_ff, rs_a), (gff, ga), (ff_o, a_o)
+    ff_size, a_size = units // count // 2, quarter // count // 2
+    mine, theirs = core * 2 + rank, core * 2 + 1 - rank
+
+    def ff_rows(at, way, offset, length, base):
+        start = base + (at % count) * 2 * ff_size + way * ff_size + offset
+        return pl.ds(pl.multiple_of(start, 16), length)
+
+    def a_rows(at, way, offset, length, owner):
+        chunk = at % count
+        start = (chunk // per) * width + owner * band + (chunk % per) * 2 * a_size
+        return pl.ds(pl.multiple_of(start + way * a_size + offset, 16), length)
+
+    def line_rows(at, way, offset, length):
+        start = (at % count) * 2 * a_size + way * a_size + offset
+        return pl.ds(pl.multiple_of(start, 16), length)
+
+    def core_rows(at, way, offset, length):
+        chunk = at % count
+        start = (chunk // per) * 2 * band + rank * band + (chunk % per) * 2 * a_size
+        return pl.ds(pl.multiple_of(start + way * a_size + offset, 16), length)
+
+    def stream_rows(stream, at):
+        _, kind, way, offset, length = stream
+        if kind:
+            return a_rows(at, way, offset, length, mine)
+        return ff_rows(at, way, offset, length, core * units)
+
+    def toward(way):
+        return behind if way else ahead
+
+    def turn(way):
+        return -1 if way else 1
+
+    def remote(source, target, send_sem, recv_sem, device):
         return pltpu.make_async_remote_copy(
-            src_ref=sums[kind].at[chunk_rows(at, stream, bases[kind]), :],
-            dst_ref=slots[kind].at[s, way, piece, :],
-            send_sem=r_send.at[number, s],
-            recv_sem=r_recv.at[number, s],
-            device_id=toward(stream),
+            src_ref=source,
+            dst_ref=target,
+            send_sem=send_sem,
+            recv_sem=recv_sem,
+            device_id=device,
             device_id_type=MESH,
         )
 
+    def spread_copy(stream, at, s):
+        number, kind, way, offset, length = stream
+        return remote(
+            sums[kind].at[stream_rows(stream, at), :],
+            slots[kind].at[s, way, pl.ds(offset, length), :],
+            r_send.at[kind],
+            r_recv.at[number, s],
+            toward(way),
+        )
+
     def gather_copy(stream, at, s):
-        number, kind = stream[:2]
-        where = outs[kind].at[chunk_rows(at, stream, bases[kind]), :]
-        return pltpu.make_async_remote_copy(
-            src_ref=where,
-            dst_ref=where,
-            send_sem=g_send.at[number, s],
-            recv_sem=g_recv.at[number, s],
-            device_id=toward(stream),
-            device_id_type=MESH,
+        number, kind, way, _, _ = stream
+        where = outs[kind].at[stream_rows(stream, at), :]
+        return remote(where, where, g_send.at[kind], g_recv.at[number, s], toward(way))
+
+    def across_copy(way, s, owner):
+        at = spot + 2 * count + turn(way) * (1 - s)
+        where = a_o.at[a_rows(at, way, 0, a_size, owner), :]
+        return remote(where, where, x_send.at[0], x_recv.at[way, s], peer)
+
+    def side_copy(way, s, owner, lane):
+        at = spot + 2 * count + turn(way) * (1 - s)
+        where = a_o.at[a_rows(at, way, 0, a_size, owner), :]
+        return remote(where, where, x_send.at[1], s_recv.at[2 * lane + way, s], sibling)
+
+    def fold_copy(way, s):
+        at = spot + count - turn(way) * s
+        return remote(
+            px.at[line_rows(at, way, 0, a_size), :],
+            xr.at[s, way],
+            x_send.at[2],
+            y_recv.at[way, s],
+            peer,
         )
 
-    def across_copy(stream, at, s, base):
-        number = stream[0] - 2 * FF_CUTS
-        where = a_o.at[chunk_rows(at, stream, base), :]
-        return pltpu.make_async_remote_copy(
-            src_ref=where,
-            dst_ref=where,
-            send_sem=x_send.at[number, s],
-            recv_sem=x_recv.at[number, s],
-            device_id=peer,
-            device_id_type=MESH,
-        )
-
-    def fold_copy(stream, s):
-        number, _, way, piece, _, _ = stream
-        at = spot + count - sign(stream) * s
-        return pltpu.make_async_remote_copy(
-            src_ref=px.at[chunk_rows(at, stream, 0), :],
-            dst_ref=xr.at[s, way, piece, :],
-            send_sem=y_send.at[number - 2 * FF_CUTS, s],
-            recv_sem=y_recv.at[number - 2 * FF_CUTS, s],
-            device_id=peer,
-            device_id_type=MESH,
-        )
+    def start_folds(s):
+        for way in range(2):
+            fold_copy(way, s).start()
 
     def own_part(stream, at, s):
-        _, kind, way, piece, _, _ = stream
-        rows_in = chunk_rows(at, stream, bases[kind])
+        _, kind, way, offset, length = stream
+        value = sums[kind][stream_rows(stream, at), :].astype(f32)
         if kind == 0:
-            return gff[rows_in, :].astype(f32) + cr_ff[chunk_rows(at, stream, 0), :].astype(f32)
-        fold_copy(stream, s).wait_recv()
+            return value + cr_ff[ff_rows(at, way, offset, length, 0), :].astype(f32)
+        if offset == 0:
+            fold_copy(way, s).wait_recv()
         return (
-            ga[rows_in, :].astype(f32)
-            + cr_a[chunk_rows(at, stream, rank * quarter), :].astype(f32)
-            + xr[s, way, piece, :].astype(f32)
+            value
+            + cr_a[core_rows(at, way, offset, length), :].astype(f32)
+            + xr[s, way, pl.ds(offset, length), :].astype(f32)
         )
 
     def ring_first(streams):
         for stream in streams:
-            kind, at = stream[1], spot + count
-            sums[kind][chunk_rows(at, stream, bases[kind]), :] = own_part(stream, at, 0).astype(bf16)
+            at = spot + count
+            sums[stream[1]][stream_rows(stream, at), :] = own_part(stream, at, 0).astype(bf16)
             spread_copy(stream, at, 0).start()
 
-    def ring_spread(streams, s, last):
+    def pass_on(stream, s):
+        _, kind, way, offset, length = stream
+        if kind and offset + length == a_size:
+            across_copy(way, s, mine).start()
+            side_copy(way, s, mine, 0).start()
+
+    def ring_spread(streams, s, last=False):
         for stream in streams:
-            _, kind, way, piece, _, _ = stream
-            at = spot + count - sign(stream) * (s + 1)
-            target = chunk_rows(at, stream, bases[kind])
+            _, kind, way, offset, length = stream
+            at = spot + count - turn(way) * (s + 1)
+            target = stream_rows(stream, at)
             part = own_part(stream, at, s + 1)
             spread_copy(stream, at, s).wait_recv()
-            total = (part + slots[kind][s, way, piece, :].astype(f32)).astype(bf16)
+            arrived = slots[kind][s, way, pl.ds(offset, length), :].astype(f32)
+            total = (part + arrived).astype(bf16)
             if last:
                 outs[kind][target, :] = total
                 gather_copy(stream, at, 0).start()
-                if kind:
-                    across_copy(stream, at, 0, bases[1]).start()
+                pass_on(stream, 0)
             else:
                 sums[kind][target, :] = total
                 spread_copy(stream, at, s + 1).start()
 
-    def ring_gather(streams, s, last):
+    def ring_gather(streams, s, last=False):
         for stream in streams:
-            at = spot + 2 * count - sign(stream) * s
+            at = spot + 2 * count - turn(stream[2]) * s
             gather_copy(stream, at, s).wait_recv()
             if not last:
                 gather_copy(stream, at, s + 1).start()
-            if stream[1]:
-                across_copy(stream, at, s + 1, bases[1]).start()
+            pass_on(stream, s + 1)
+
+    def cross_over(s):
+        for way in range(2):
+            across_copy(way, s, theirs).wait_recv()
+            side_copy(way, s, theirs, 1).start()
 
     def small_copy(index):
         return peer_copy(smalls.at[index], small_r.at[index], (m_send, m_recv), index, swaps[index])
@@ -813,8 +886,9 @@
     acc[...] = jnp.zeros_like(acc)
     core_ff.wait()
     ring_first(ff_streams)
-    hidden_copy.wait()
-    ring_spread(ff_streams, 0, False)
+    hidden_copy(0).wait()
+    hidden_copy(1).wait()
+    ring_spread(ff_streams, 0)
 
     @pl.loop(0, rows // ROWBLOCK)
     def _(i):
@@ -839,7 +913,7 @@
         dn[:, cols] = d_numer
         xs[:, cols] = (d_numer.astype(f32) * mixf[:, cols]).astype(bf16)
 
-    ring_spread(ff_streams, 1, False)
+    ring_spread(ff_streams, 1)
 
     @pl.loop(0, pairs)
     def _(p):
@@ -859,12 +933,27 @@
     turn_keys = peer_copy(dzs, dzr, sems, 7, peer)
     turn_copy.start()
     turn_keys.start()
-    ring_spread(ff_streams, 2, False)
 
     @pl.loop(0, tiles)
     def _(j):
         cols = tile_at(j, TILE)
         ga[tile_at(3 * tiles + j, TILE), :] = mm_tn(mixb[:, cols], dlow[...]).astype(bf16)
+
+    def core_a(m):
+        there = pl.ds(pl.multiple_of(m * width + (1 - core) * 2 * band, 2 * band), 2 * band)
+        here = pl.ds(m * 2 * band, 2 * band)
+        return peer_copy(ga.at[there, :], cr_a.at[here, :], sems, (9, 11, 20, 21)[m], sibling)
+
+    def fill_px(m):
+        core_a(m).wait()
+        there = pl.ds(pl.multiple_of(m * width + theirs * band, band), band)
+        here = pl.ds(pl.multiple_of(m * 2 * band + (1 - rank) * band, band), band)
+        px[m * band : (m + 1) * band, :] = (
+            ga[there, :].astype(f32) + cr_a[here, :].astype(f32)
+        ).astype(bf16)
+
+    core_a(3).start()
+    ring_spread(ff_streams, 2)
 
     def inside(p):
         lanes = tile_at(p, LANES)
@@ -886,9 +975,8 @@
         dv[:, lanes] = sum_v
 
     pl.loop(0, pairs // 2)(inside)
-    ring_spread(ff_streams, 3, False)
+    ring_spread(ff_streams, 3)
     pl.loop(pairs // 2, pairs)(inside)
-    ring_spread(ff_streams, 4, False)
     turn_copy.wait()
     turn_keys.wait()
 
@@ -900,10 +988,10 @@
         d_numer, x = dn[:, lanes], xs[:, lanes]
         sum_q, sum_k, sum_v = dq[:, lanes], dk[:, lanes], dv[:, lanes]
         zblock, dzblock = zst[p], dzr[p] * early
+        along = mm(x, diag_low)
         for part, wave in ((0, cosb[...]), (1, sinb[...])):
             state = spread_pair(st[p, part], diag).astype(bf16)
-            zmat = (column_of(zblock, part) * diag).astype(bf16)
-            sum_q += wave * (mm_nt(d_numer, state) - mm_nt(x, zmat))
+            sum_q += wave * (mm_nt(d_numer, state) - along * zblock[part : part + 1, :])
             d_state = (spread_pair(drecv[p, part], diag) * early).astype(bf16)
             sum_k += wave * (mm_nt(v, d_state) + dzblock[part : part + 1, :]) * (1.0 / HD)
             sum_v += mm((k * wave * (1.0 / HD)).astype(bf16), d_state)
@@ -916,18 +1004,25 @@
             smalls[0, slot : slot + 1, lanes] = jnp.sum(value, axis=0, keepdims=True)
 
     small_copy(0).start()
-    ring_spread(ff_streams, 5, False)
-
-    for which, source in enumerate((dql, dkl, dvl)):
-
+
+    def make_grad(which, source):
         @pl.loop(0, tiles)
-        def _(j, which=which, source=source):
+        def _(j):
             ga[tile_at(which * tiles + j, TILE), :] = mm_tn(
                 tok[:, tile_at(j, TILE)], source[...]
             ).astype(bf16)
 
-    core_a.start()
-    ring_spread(ff_streams, count - 2, True)
+        core_a(which).start()
+
+    make_grad(2, dvl)
+    make_grad(0, dql)
+    fill_px(3)
+    make_grad(1, dkl)
+    fill_px(2)
+    fill_px(0)
+    fill_px(1)
+    for s in range(3):
+        start_folds(s)
 
     @pl.loop(0, tiles)
     def _(j):
@@ -940,80 +1035,80 @@
 
     token_out = pltpu.make_async_copy(dres, dtok_h, o_sem.at[1])
     token_out.start()
-    core_a.wait()
-
-    @pl.loop(0, quarter // 96)
-    def _(i):
-        near = pl.ds(pl.multiple_of((core * 2 + 1 - rank) * quarter + i * 96, 96), 96)
-        far = pl.ds(pl.multiple_of((1 - rank) * quarter + i * 96, 96), 96)
-        px[tile_at(i, 96), :] = (ga[near, :].astype(f32) + cr_a[far, :].astype(f32)).astype(bf16)
-
-    for s in range(3):
-        for stream in a_streams:
-            fold_copy(stream, s).start()
+    ring_first(a_streams)
     swap_small(0)
-    ring_first(a_streams)
-
-    def both_steps(s):
-        @pl.when(s + 3 < count)
-        def _():
-            for stream in a_streams:
-                fold_copy(stream, s + 3).start()
-
-        ring_gather(ff_streams, s, False)
-        ring_spread(a_streams, s, False)
-
-    pl.loop(0, 2)(both_steps)
+
+    def spread_both(s):
+        start_folds(s + 3)
+        ring_spread(a_streams, s)
+        ring_spread(ff_streams, s + 4)
+
+    def spread_gather(s):
+        ring_spread(a_streams, s)
+        ring_gather(ff_streams, s - 3)
+
+    def gather_both(s):
+        ring_gather(a_streams, s)
+        ring_gather(ff_streams, s + 4)
+        cross_over(s)
+
+    def gather_one(s):
+        ring_gather(a_streams, s)
+        cross_over(s)
+
+    pl.loop(0, 2)(spread_both)
     swap_small(1)
-    pl.loop(2, 4)(both_steps)
+    start_folds(5)
+    ring_spread(a_streams, 2)
+    ring_spread(ff_streams, 6, True)
+    start_folds(6)
+    start_folds(7)
     swap_small(2)
-    pl.loop(4, count - 2)(both_steps)
+    pl.loop(3, 6)(spread_gather)
     swap_small(3)
-    ring_gather(ff_streams, count - 2, True)
-    own_ff, own_a = part_rows(core, units), part_rows(core, 2 * quarter)
+    ring_spread(a_streams, 6, True)
+    ring_gather(ff_streams, 3)
+    pl.loop(0, 2)(gather_both)
+    swap_small(4)
+    small_out = pltpu.make_async_copy(smalls.at[len(swaps)], small_h, o_sem.at[6])
+    small_out.start()
+    ring_gather(a_streams, 2)
+    ring_gather(ff_streams, 6, True)
+    own_ff = part_rows(core, units)
     back_ff = peer_copy(ff_o.at[own_ff, :], ff_o.at[own_ff, :], sems, 10, sibling)
     back_ff.start()
     near_ff = out_copy(ff_o, ff_h, own_ff, 2)
     near_ff.start()
-    ring_spread(a_streams, count - 2, True)
-    pl.loop(0, 2)(lambda s: ring_gather(a_streams, s, False))
-    swap_small(4)
-    small_out = pltpu.make_async_copy(smalls.at[len(swaps)], small_h, o_sem.at[6])
-    small_out.start()
+    cross_over(2)
+    gather_one(3)
     back_ff.wait()
     far_ff = out_copy(ff_o, ff_h, part_rows(1 - core, units), 3)
     far_ff.start()
-    pl.loop(2, count - 2)(lambda s: ring_gather(a_streams, s, False))
-    ring_gather(a_streams, count - 2, True)
-    crossed = (core * 2 + 1 - rank) * quarter
+    pl.loop(4, 6)(gather_one)
+    ring_gather(a_streams, 6, True)
+    cross_over(6)
+    cross_over(7)
+
+    def drain(kind, source, total, sem):
+        where = source.at[pl.ds(0, total), :]
+        remote(where, where, sem, x_recv.at[0, 0], peer).wait_send()
+
+    for kind, size in ((0, ff_size), (1, a_size)):
+        drain(kind, sums[kind], 2 * (count - 1) * size, r_send.at[kind])
+        drain(kind, outs[kind], 2 * (count - 1) * size, g_send.at[kind])
+    drain(1, px, 2 * count * a_size, x_send.at[2])
 
     @pl.loop(0, count)
     def _(s):
-        for stream in a_streams:
-            at = spot + 2 * count + sign(stream) * (1 - s)
-            across_copy(stream, at, s, crossed).wait_recv()
-
-    back_a = peer_copy(a_o.at[own_a, :], a_o.at[own_a, :], sems, 11, sibling)
-    back_a.start()
-    near_a = out_copy(a_o, a_h, own_a, 4)
-    near_a.start()
-
-    @pl.loop(0, count - 1)
-    def _(s):
-        for stream in ff_streams + a_streams:
-            spread_copy(stream, spot, s).wait_send()
-            gather_copy(stream, spot, s).wait_send()
-
-    @pl.loop(0, count)
-    def _(s):
-        for stream in a_streams:
-            across_copy(stream, spot, s, bases[1]).wait_send()
-            fold_copy(stream, s).wait_send()
-
-    back_a.wait()
-    far_a = out_copy(a_o, a_h, part_rows(1 - core, 2 * quarter), 5)
-    far_a.start()
-    for copy in (result_out, token_out, near_ff, far_ff, small_out, near_a, far_a):
+        for way in range(2):
+            for lane, owner in ((0, (1 - core) * 2 + rank), (1, (1 - core) * 2 + 1 - rank)):
+                side_copy(way, s, owner, lane).wait_recv()
+
+    whole_a = pltpu.make_async_copy(a_o, a_h, o_sem.at[4])
+    whole_a.start()
+    drain(1, a_o, 2 * count * a_size, x_send.at[0])
+    drain(1, a_o, 4 * count * a_size, x_send.at[1])
+    for copy in (result_out, token_out, near_ff, far_ff, small_out, whole_a):
         copy.wait()
 
 
@@ -1127,6 +1222,8 @@
     state, zrows = (pairs, 2, HD, LANES), (pairs, 8, LANES)
     own, pair = (rows, width), (2 * rows, width)
     scratch = dict(
+        tok=low(*own), places=pltpu.VMEM(positions.shape, jnp.int32), span=pltpu.SMEM((1, 1), jnp.int32),
+        og=low(*own), **{name: low(width) for name in LINES}, bup_line=low(units),
         wa=low(4 * width, width), wff=low(2 * units, width), vec=wide(9 + halves + -(9 + halves) % 8, width),
         hbuf=low(*pair), act=low(2 * rows, units), slope=wide(2 * rows, units), dbuf=low(*pair),
         dpre=low(2 * rows, units), hid=wide(*own), numer=wide(*own), denom=wide(*own),
@@ -1143,13 +1240,12 @@
         xr=low(count, 2, a_part, width), rs_ff=low(count - 1, 2, ff_part, width),
         rs_a=low(count - 1, 2, a_part, width), ff_o=low(2 * units, width), a_o=low(4 * width, width),
         smalls=wide(swaps + 1, lines, width), small_r=wide(swaps, lines, width),
-        send=sem(12), recv=sem(12), r_send=sem(streams, count - 1), r_recv=sem(streams, count - 1),
-        g_send=sem(streams, count - 1), g_recv=sem(streams, count - 1),
-        x_send=sem(2 * A_CUTS, count), x_recv=sem(2 * A_CUTS, count),
-        y_send=sem(2 * A_CUTS, count), y_recv=sem(2 * A_CUTS, count),
-        m_send=sem(swaps), m_recv=sem(swaps), w_sem=sem(5 + halves), o_sem=sem(7),
-    )
-    vmem, anywhere = pl.BlockSpec(memory_space=pltpu.VMEM), pl.BlockSpec(memory_space=pl.ANY)
+        send=sem(22), recv=sem(22), r_send=sem(2), r_recv=sem(streams, count - 1),
+        g_send=sem(2), g_recv=sem(streams, count - 1), x_send=sem(3), x_recv=sem(2, count),
+        s_recv=sem(4, count), y_recv=sem(2, count),
+        m_send=sem(swaps), m_recv=sem(swaps), w_sem=sem(5 + halves), o_sem=sem(7), l_sem=sem(14),
+    )
+    anywhere = pl.BlockSpec(memory_space=pl.ANY)
     outs = shaped(
         (own, bf16), (own, f32), ((2 * units, width), bf16), ((4 * width, width), bf16),
         ((lines, width), f32),
@@ -1157,7 +1253,7 @@
     res, dtok, ff, a, small = pl.pallas_call(
         functools.partial(block_kernel, count),
         out_shape=outs,
-        in_specs=[vmem] * 2 + [pl.BlockSpec(memory_space=pltpu.SMEM)] + [vmem] * 11 + [anywhere] * 6,
+        in_specs=[anywhere] * 20,
         out_specs=tuple([anywhere] * len(outs)),
         scratch_shapes=list(scratch.values()),
         compiler_params=pltpu.CompilerParams(

time: 188 us -> 173 us (0.920)
  Pallas kernels: 186 us -> 170 us
    pallas_call x1, Pallas kernels: 174 us -> 158 us  [pair_device(): pl.pallas_call(functools.partial(block_kernel, count), out_shape=outs, in...]
where the time goes in v5:
time: 173 us; the launch traced here: 172 us
  Pallas kernels  170 us (98%)
    pallas_call x1, Pallas kernels, pair_device(): pl.pallas_call(functools.partial(block_kernel, count), out_shape=outs, in...  158 us
    pallas_call x1, Pallas kernels, finish(): pl.pallas_call(functools.partial(finish_kernel, halves), grid=(steps,), o...  12.2 us

profile of v5, /device:TPU:0, one launch (start us, length us, event | category | flops | bytes accessed | tf_op | source)
XLA Modules:
  0.0 171.9 jit_solution(9460393618984192458)
XLA Ops:
  1.3 158.2 %block.1 = (bf16[256,768]{1,0:T(8,128)(2,1)}, f32[256,768]{1,0:T(8,128)}, bf16[3072,768]{1,0:T(8,128)(2,1)}, bf16[3072,768]{1,0:T(8,128)(2,1)}, f32[16,768]{1,0:T(8,128)}) custom-call(bf16[256,768]{1,0:T(8,128)(2,1)} %tok_h.1, s32[512]{0:T(512)} %places_h.1, s32[1,1]{1,0:T(1,128)} %bitcast.1.span_h, bf16[768]{0:T(1024)(128)(2,1)} %bq.1, bf16[768]{0:T(1024)(128)(2,1)} %bk.1, ...), custom_call_target="tpu_custom_call" | custom-call | tf_op jit(solution)/shard_map/block/pallas_call | solution.py:1253
  159.5 12.2 %finish.1 = (bf16[256,768]{1,0:T(8,128)(2,1)}, f32[256,768]{1,0:T(8,128)}, f32[768,768]{1,0:T(8,128)}, f32[768]{0:T(1024)}, f32[768,768]{1,0:T(8,128)}, /*index=...) custom-call(bf16[3072,768]{1,0:T(8,128)(2,1)} %get-tuple-element.23., ...), custom_call_target="tpu_custom_call" | custom-call | tf_op jit(solution)/shard_map/finish/pallas_call | solution.py:1165

commit v6 on v5

--- a/solution.py
+++ b/solution.py
@@ -293,6 +293,7 @@
 LANES = 2 * HD
 TILE = 256
 ROWBLOCK = 32
+FINISH = 256
 FF_CUTS = 3
 A_CUTS = 3
 LINES = tuple("l" + str(index) for index in range(9))
@@ -828,11 +829,16 @@
             sums[stream[1]][stream_rows(stream, at), :] = own_part(stream, at, 0).astype(bf16)
             spread_copy(stream, at, 0).start()
 
+    def store_chunk(way, s, owner):
+        rows_at = a_rows(spot + 2 * count + turn(way) * (1 - s), way, 0, a_size, owner)
+        pltpu.make_async_copy(a_o.at[rows_at, :], a_h.at[rows_at, :], o_sem.at[4]).start()
+
     def pass_on(stream, s):
         _, kind, way, offset, length = stream
         if kind and offset + length == a_size:
             across_copy(way, s, mine).start()
             side_copy(way, s, mine, 0).start()
+            store_chunk(way, s, mine)
 
     def ring_spread(streams, s, last=False):
         for stream in streams:
@@ -863,6 +869,13 @@
         for way in range(2):
             across_copy(way, s, theirs).wait_recv()
             side_copy(way, s, theirs, 1).start()
+            store_chunk(way, s, theirs)
+
+    def side_done(lane, s):
+        owner = (1 - core) * 2 + (1 - rank if lane else rank)
+        for way in range(2):
+            side_copy(way, s, owner, lane).wait_recv()
+            store_chunk(way, s, owner)
 
     def small_copy(index):
         return peer_copy(smalls.at[index], small_r.at[index], (m_send, m_recv), index, swaps[index])
@@ -888,7 +901,6 @@
     ring_first(ff_streams)
     hidden_copy(0).wait()
     hidden_copy(1).wait()
-    ring_spread(ff_streams, 0)
 
     @pl.loop(0, rows // ROWBLOCK)
     def _(i):
@@ -913,7 +925,6 @@
         dn[:, cols] = d_numer
         xs[:, cols] = (d_numer.astype(f32) * mixf[:, cols]).astype(bf16)
 
-    ring_spread(ff_streams, 1)
 
     @pl.loop(0, pairs)
     def _(p):
@@ -933,6 +944,7 @@
     turn_keys = peer_copy(dzs, dzr, sems, 7, peer)
     turn_copy.start()
     turn_keys.start()
+    ring_spread(ff_streams, 0)
 
     @pl.loop(0, tiles)
     def _(j):
@@ -953,7 +965,6 @@
         ).astype(bf16)
 
     core_a(3).start()
-    ring_spread(ff_streams, 2)
 
     def inside(p):
         lanes = tile_at(p, LANES)
@@ -975,8 +986,9 @@
         dv[:, lanes] = sum_v
 
     pl.loop(0, pairs // 2)(inside)
-    ring_spread(ff_streams, 3)
+    ring_spread(ff_streams, 1)
     pl.loop(pairs // 2, pairs)(inside)
+    ring_spread(ff_streams, 2)
     turn_copy.wait()
     turn_keys.wait()
 
@@ -1015,11 +1027,12 @@
         core_a(which).start()
 
     make_grad(2, dvl)
+    ring_spread(ff_streams, 3)
     make_grad(0, dql)
-    fill_px(3)
     make_grad(1, dkl)
-    fill_px(2)
-    fill_px(0)
+    for m in (3, 2, 0):
+        fill_px(m)
+    ring_spread(ff_streams, 4)
     fill_px(1)
     for s in range(3):
         start_folds(s)
@@ -1035,59 +1048,62 @@
 
     token_out = pltpu.make_async_copy(dres, dtok_h, o_sem.at[1])
     token_out.start()
+    ring_spread(ff_streams, 5)
     ring_first(a_streams)
     swap_small(0)
 
-    def spread_both(s):
-        start_folds(s + 3)
-        ring_spread(a_streams, s)
-        ring_spread(ff_streams, s + 4)
-
     def spread_gather(s):
         ring_spread(a_streams, s)
-        ring_gather(ff_streams, s - 3)
-
-    def gather_both(s):
-        ring_gather(a_streams, s)
-        ring_gather(ff_streams, s + 4)
-        cross_over(s)
-
-    def gather_one(s):
-        ring_gather(a_streams, s)
-        cross_over(s)
-
-    pl.loop(0, 2)(spread_both)
+        ring_gather(ff_streams, s - 1)
+
+    start_folds(3)
+    ring_spread(a_streams, 0)
+    ring_spread(ff_streams, 6, True)
     swap_small(1)
-    start_folds(5)
-    ring_spread(a_streams, 2)
-    ring_spread(ff_streams, 6, True)
+
+    @pl.loop(1, 3)
+    def _(s):
+        start_folds(s + 3)
+        spread_gather(s)
+
+    swap_small(2)
     start_folds(6)
     start_folds(7)
-    swap_small(2)
     pl.loop(3, 6)(spread_gather)
     swap_small(3)
     ring_spread(a_streams, 6, True)
-    ring_gather(ff_streams, 3)
-    pl.loop(0, 2)(gather_both)
-    swap_small(4)
-    small_out = pltpu.make_async_copy(smalls.at[len(swaps)], small_h, o_sem.at[6])
-    small_out.start()
-    ring_gather(a_streams, 2)
+    ring_gather(ff_streams, 5)
+    ring_gather(a_streams, 0)
     ring_gather(ff_streams, 6, True)
     own_ff = part_rows(core, units)
     back_ff = peer_copy(ff_o.at[own_ff, :], ff_o.at[own_ff, :], sems, 10, sibling)
     back_ff.start()
     near_ff = out_copy(ff_o, ff_h, own_ff, 2)
     near_ff.start()
-    cross_over(2)
-    gather_one(3)
+    cross_over(0)
+    side_done(0, 0)
+    swap_small(4)
+    small_out = pltpu.make_async_copy(smalls.at[len(swaps)], small_h, o_sem.at[6])
+    small_out.start()
+
+    def gather_one(s):
+        ring_gather(a_streams, s)
+        cross_over(s)
+        side_done(0, s)
+        side_done(1, s - 1)
+
+    gather_one(1)
     back_ff.wait()
     far_ff = out_copy(ff_o, ff_h, part_rows(1 - core, units), 3)
     far_ff.start()
-    pl.loop(4, 6)(gather_one)
+    pl.loop(2, 6)(gather_one)
     ring_gather(a_streams, 6, True)
     cross_over(6)
+    side_done(0, 6)
+    side_done(1, 5)
     cross_over(7)
+    side_done(0, 7)
+    side_done(1, 6)
 
     def drain(kind, source, total, sem):
         where = source.at[pl.ds(0, total), :]
@@ -1098,16 +1114,10 @@
         drain(kind, outs[kind], 2 * (count - 1) * size, g_send.at[kind])
     drain(1, px, 2 * count * a_size, x_send.at[2])
 
-    @pl.loop(0, count)
-    def _(s):
-        for way in range(2):
-            for lane, owner in ((0, (1 - core) * 2 + rank), (1, (1 - core) * 2 + 1 - rank)):
-                side_copy(way, s, owner, lane).wait_recv()
-
+    drain(1, a_o, 2 * count * a_size, x_send.at[0])
+    side_done(1, 7)
+    drain(1, a_o, 4 * count * a_size, x_send.at[1])
     whole_a = pltpu.make_async_copy(a_o, a_h, o_sem.at[4])
-    whole_a.start()
-    drain(1, a_o, 2 * count * a_size, x_send.at[0])
-    drain(1, a_o, 4 * count * a_size, x_send.at[1])
     for copy in (result_out, token_out, near_ff, far_ff, small_out, whole_a):
         copy.wait()
 
@@ -1139,8 +1149,8 @@
 
 
 def finish(rows, width, units, res, dtok, ff, a, small):
-    halves, steps = units // width, width // LANES
-    low = (LANES, width)
+    halves, steps = units // width, width // FINISH
+    low = (FINISH, width)
     down_rows = units // steps
 
     def whole(shape):
@@ -1150,7 +1160,7 @@
         return pl.BlockSpec(shape, lambda i: (start + i, 0))
 
     in_specs = [at_block(low, which * steps) for which in range(4)]
-    in_specs += [at_block(low, units // LANES + piece * steps) for piece in range(halves)]
+    in_specs += [at_block(low, units // FINISH + piece * steps) for piece in range(halves)]
     in_specs += [at_block((down_rows, width), 0), whole(small.shape), whole(res.shape), whole(dtok.shape)]
     matrix, line = (width, width), (width,)
     shapes = [
@@ -1160,7 +1170,7 @@
     ]
     special = {
         2: at_block(low, 0), 4: at_block(low, 0), 6: at_block(low, 0), 8: at_block(low, 0),
-        12: at_block((LANES, units), 0), 14: at_block((down_rows, width), 0),
+        12: at_block((FINISH, units), 0), 14: at_block((down_rows, width), 0),
     }
     return pl.pallas_call(
         functools.partial(finish_kernel, halves),

time: 173 us -> 164 us (0.948)
  Pallas kernels: 170 us -> 162 us
    pallas_call x1, Pallas kernels: 158 us -> 151 us  [pair_device(): pl.pallas_call(functools.partial(block_kernel, count), out_shape=outs, in...]
where the time goes in v6:
time: 164 us; the launch traced here: 163 us
  Pallas kernels  162 us (99%)
    pallas_call x1, Pallas kernels, pair_device(): pl.pallas_call(functools.partial(block_kernel, count), out_shape=outs, in...  151 us
    pallas_call x1, Pallas kernels, finish(): pl.pallas_call(functools.partial(finish_kernel, halves), grid=(steps,), o...  10.7 us

profile of v6, /device:TPU:0, one launch (start us, length us, event | category | flops | bytes accessed | tf_op | source)
XLA Modules:
  0.0 163.1 jit_solution(1502706653931279129)
XLA Ops:
  1.3 150.9 %block.1 = (bf16[256,768]{1,0:T(8,128)(2,1)}, f32[256,768]{1,0:T(8,128)}, bf16[3072,768]{1,0:T(8,128)(2,1)}, bf16[3072,768]{1,0:T(8,128)(2,1)}, f32[16,768]{1,0:T(8,128)}) custom-call(bf16[256,768]{1,0:T(8,128)(2,1)} %tok_h.1, s32[512]{0:T(512)} %places_h.1, s32[1,1]{1,0:T(1,128)} %bitcast.1.span_h, bf16[768]{0:T(1024)(128)(2,1)} %bq.1, bf16[768]{0:T(1024)(128)(2,1)} %bk.1, ...), custom_call_target="tpu_custom_call" | custom-call | tf_op jit(solution)/shard_map/block/pallas_call | solution.py:1263
  152.2 10.7 %finish.1 = (bf16[256,768]{1,0:T(8,128)(2,1)}, f32[256,768]{1,0:T(8,128)}, f32[768,768]{1,0:T(8,128)}, f32[768]{0:T(1024)}, f32[768,768]{1,0:T(8,128)}, /*index=...) custom-call(bf16[3072,768]{1,0:T(8,128)(2,1)} %get-tuple-element.23., ...), custom_call_target="tpu_custom_call" | custom-call | tf_op jit(solution)/shard_map/finish/pallas_call | solution.py:1175

commit v7 on v6

--- a/solution.py
+++ b/solution.py
@@ -296,6 +296,7 @@
 FINISH = 256
 FF_CUTS = 3
 A_CUTS = 3
+RING_ROWS = 16
 LINES = tuple("l" + str(index) for index in range(9))
 
 
@@ -416,7 +417,7 @@
     bsend, brecv, res, gff, dhs, dhr, dho, mixb, mixf, inv, rq, rk, vv, nrm, scl, st, zst,
     dres, dlow, dn, xs, dsend, drecv, dzs, dzr, dql, dkl, dvl, ctab, cosb, sinb, acc, bup,
     cr_ff, cr_a, px, xr, rs_ff, rs_a, ff_o, a_o, smalls, small_r,
-    send, recv, r_send, r_recv, g_send, g_recv, x_send, x_recv, s_recv, y_recv, m_send, m_recv,
+    send, recv, r_send, r_recv, g_send, g_recv, x_send, x_recv, t_recv, s_recv, y_recv, m_send, m_recv,
     w_sem, o_sem, l_sem,
 ):
     sems = (send, recv)
@@ -682,41 +683,52 @@
         return total
 
     lower_rows(own)
-    for k in range(2):
-        grad_copy(k).wait()
-        lower_rows(away[k])
-
+    def send_hidden(k):
         @pl.loop(0, tiles)
-        def _(j, k=k):
+        def _(j):
             cols = tile_at(j, TILE)
             dhs[near[k], cols] = lower_hidden(away[k], cols, j).astype(bf16)
 
         hidden_copy(k).start()
 
-    def make_down():
-        @pl.loop(0, units // TILE)
+    grad_copy(0).wait()
+    lower_rows(away[0])
+    send_hidden(0)
+    grad_copy(1).wait()
+    lower_rows(away[1])
+
+    def make_down(part):
+        @pl.loop(part * tiles, (part + 1) * tiles)
         def _(j):
             cols = tile_at(j, TILE)
             gff[cols, :] = mm_tn(act[:, cols], dbuf[...]).astype(bf16)
 
-    def make_up():
-        for piece in range(halves):
-
-            @pl.loop(0, tiles)
-            def _(j, piece=piece):
-                gff[pl.ds(units + piece * width, width), tile_at(j, TILE)] = mm_tn(
-                    hbuf[...], dpre[:, tile_at(piece * tiles + j, TILE)]
-                ).astype(bf16)
+    def make_up(part):
+        @pl.loop(0, tiles)
+        def _(j):
+            gff[pl.ds(units + part * width, width), tile_at(j, TILE)] = mm_tn(
+                hbuf[...], dpre[:, tile_at(part * tiles + j, TILE)]
+            ).astype(bf16)
 
     def part_rows(which, size):
         return pl.ds(pl.multiple_of(which * size, size), size)
 
-    core_ff = peer_copy(gff.at[part_rows(1 - core, units), :], cr_ff, sems, 8, sibling)
-    pl.when(core == 0)(make_up)
-    pl.when(core == 1)(make_down)
-    core_ff.start()
-    pl.when(core == 0)(make_down)
-    pl.when(core == 1)(make_up)
+    def core_ff(part):
+        start = pl.multiple_of((1 - core) * units + part * width, width)
+        return peer_copy(
+            gff.at[pl.ds(start, width), :],
+            cr_ff.at[pl.ds(part * width, width), :],
+            sems, (8, 22, 23)[part], sibling,
+        )
+
+    for part in range(halves):
+        pl.when(core == 0)(functools.partial(make_up, part))
+        pl.when(core == 1)(functools.partial(make_down, part))
+        core_ff(part).start()
+    send_hidden(1)
+    for part in range(halves):
+        pl.when(core == 0)(functools.partial(make_down, part))
+        pl.when(core == 1)(functools.partial(make_up, part))
 
     band, per = width // 4, count // 4
     ff_streams, a_streams = [], []
@@ -786,10 +798,15 @@
         where = outs[kind].at[stream_rows(stream, at), :]
         return remote(where, where, g_send.at[kind], g_recv.at[number, s], toward(way))
 
-    def across_copy(way, s, owner):
+    def across_copy(way, s, owner, first):
+        at, skip = spot + 2 * count + turn(way) * (1 - s), 0 if first else RING_ROWS
+        where = a_o.at[a_rows(at, way, skip, a_size - skip, owner), :]
+        return remote(where, where, x_send.at[0], x_recv.at[way, s], peer)
+
+    def round_copy(way, s):
         at = spot + 2 * count + turn(way) * (1 - s)
-        where = a_o.at[a_rows(at, way, 0, a_size, owner), :]
-        return remote(where, where, x_send.at[0], x_recv.at[way, s], peer)
+        where = a_o.at[a_rows(at, way, 0, RING_ROWS, theirs), :]
+        return remote(where, where, x_send.at[3], t_recv.at[way, s], toward(way))
 
     def side_copy(way, s, owner, lane):
         at = spot + 2 * count + turn(way) * (1 - s)
@@ -833,10 +850,10 @@
         rows_at = a_rows(spot + 2 * count + turn(way) * (1 - s), way, 0, a_size, owner)
         pltpu.make_async_copy(a_o.at[rows_at, :], a_h.at[rows_at, :], o_sem.at[4]).start()
 
-    def pass_on(stream, s):
+    def pass_on(stream, s, first=False):
         _, kind, way, offset, length = stream
         if kind and offset + length == a_size:
-            across_copy(way, s, mine).start()
+            across_copy(way, s, mine, first).start()
             side_copy(way, s, mine, 0).start()
             store_chunk(way, s, mine)
 
@@ -852,7 +869,7 @@
             if last:
                 outs[kind][target, :] = total
                 gather_copy(stream, at, 0).start()
-                pass_on(stream, 0)
+                pass_on(stream, 0, True)
             else:
                 sums[kind][target, :] = total
                 spread_copy(stream, at, s + 1).start()
@@ -863,11 +880,17 @@
             gather_copy(stream, at, s).wait_recv()
             if not last:
                 gather_copy(stream, at, s + 1).start()
+        for stream in streams:
             pass_on(stream, s + 1)
 
-    def cross_over(s):
+    def cross_over(s, first=False, last=False):
         for way in range(2):
-            across_copy(way, s, theirs).wait_recv()
+            across_copy(way, s, theirs, first).wait_recv()
+            if not first:
+                round_copy(way, s - 1).wait_recv()
+            if not last:
+                round_copy(way, s).start()
+        for way in range(2):
             side_copy(way, s, theirs, 1).start()
             store_chunk(way, s, theirs)
 
@@ -877,6 +900,11 @@
             side_copy(way, s, owner, lane).wait_recv()
             store_chunk(way, s, owner)
 
+    def ff_part(q):
+        s, cut = q // FF_CUTS, q % FF_CUTS
+        piece = ff_size // FF_CUTS
+        ring_spread([(way * FF_CUTS + cut, 0, way, cut * piece, piece) for way in range(2)], s)
+
     def small_copy(index):
         return peer_copy(smalls.at[index], small_r.at[index], (m_send, m_recv), index, swaps[index])
 
@@ -897,7 +925,8 @@
         dho[:, cols] += lower_hidden(own, cols, j)
 
     acc[...] = jnp.zeros_like(acc)
-    core_ff.wait()
+    for part in range(halves):
+        core_ff(part).wait()
     ring_first(ff_streams)
     hidden_copy(0).wait()
     hidden_copy(1).wait()
@@ -917,6 +946,8 @@
     for slot in range(3):
         add_small(slot, jnp.sum(acc[8 * slot : 8 * slot + 8, :], axis=0, keepdims=True))
 
+    ff_part(0)
+
     @pl.loop(0, tiles)
     def _(j):
         cols = tile_at(j, TILE)
@@ -924,6 +955,8 @@
         d_numer = (d_mixed * inv[:, cols]).astype(bf16)
         dn[:, cols] = d_numer
         xs[:, cols] = (d_numer.astype(f32) * mixf[:, cols]).astype(bf16)
+
+    ff_part(1)
 
 
     @pl.loop(0, pairs)
@@ -944,7 +977,7 @@
     turn_keys = peer_copy(dzs, dzr, sems, 7, peer)
     turn_copy.start()
     turn_keys.start()
-    ring_spread(ff_streams, 0)
+    ff_part(2)
 
     @pl.loop(0, tiles)
     def _(j):
@@ -965,6 +998,7 @@
         ).astype(bf16)
 
     core_a(3).start()
+    ff_part(3)
 
     def inside(p):
         lanes = tile_at(p, LANES)
@@ -985,10 +1019,11 @@
         dk[:, lanes] = sum_k
         dv[:, lanes] = sum_v
 
-    pl.loop(0, pairs // 2)(inside)
-    ring_spread(ff_streams, 1)
-    pl.loop(pairs // 2, pairs)(inside)
-    ring_spread(ff_streams, 2)
+    @pl.loop(0, pairs)
+    def _(p):
+        inside(p)
+        ff_part(4 + p)
+
     turn_copy.wait()
     turn_keys.wait()
 
@@ -1016,6 +1051,7 @@
             smalls[0, slot : slot + 1, lanes] = jnp.sum(value, axis=0, keepdims=True)
 
     small_copy(0).start()
+    ff_part(10)
 
     def make_grad(which, source):
         @pl.loop(0, tiles)
@@ -1027,15 +1063,15 @@
         core_a(which).start()
 
     make_grad(2, dvl)
-    ring_spread(ff_streams, 3)
+    ff_part(11)
     make_grad(0, dql)
+    ff_part(12)
     make_grad(1, dkl)
-    for m in (3, 2, 0):
+    ff_part(13)
+    for m in (3, 2, 0, 1):
         fill_px(m)
-    ring_spread(ff_streams, 4)
-    fill_px(1)
-    for s in range(3):
-        start_folds(s)
+    start_folds(0)
+    ff_part(14)
 
     @pl.loop(0, tiles)
     def _(j):
@@ -1048,6 +1084,7 @@
 
     token_out = pltpu.make_async_copy(dres, dtok_h, o_sem.at[1])
     token_out.start()
+    start_folds(1)
     ring_spread(ff_streams, 5)
     ring_first(a_streams)
     swap_small(0)
@@ -1056,20 +1093,18 @@
         ring_spread(a_streams, s)
         ring_gather(ff_streams, s - 1)
 
-    start_folds(3)
+    start_folds(2)
     ring_spread(a_streams, 0)
     ring_spread(ff_streams, 6, True)
     swap_small(1)
 
-    @pl.loop(1, 3)
-    def _(s):
-        start_folds(s + 3)
+    def spread_fold(s):
+        start_folds(s + 2)
         spread_gather(s)
 
+    pl.loop(1, 3)(spread_fold)
     swap_small(2)
-    start_folds(6)
-    start_folds(7)
-    pl.loop(3, 6)(spread_gather)
+    pl.loop(3, 6)(spread_fold)
     swap_small(3)
     ring_spread(a_streams, 6, True)
     ring_gather(ff_streams, 5)
@@ -1080,7 +1115,7 @@
     back_ff.start()
     near_ff = out_copy(ff_o, ff_h, own_ff, 2)
     near_ff.start()
-    cross_over(0)
+    cross_over(0, first=True)
     side_done(0, 0)
     swap_small(4)
     small_out = pltpu.make_async_copy(smalls.at[len(swaps)], small_h, o_sem.at[6])
@@ -1101,7 +1136,7 @@
     cross_over(6)
     side_done(0, 6)
     side_done(1, 5)
-    cross_over(7)
+    cross_over(7, last=True)
     side_done(0, 7)
     side_done(1, 6)
 
@@ -1114,7 +1149,8 @@
         drain(kind, outs[kind], 2 * (count - 1) * size, g_send.at[kind])
     drain(1, px, 2 * count * a_size, x_send.at[2])
 
-    drain(1, a_o, 2 * count * a_size, x_send.at[0])
+    drain(1, a_o, 2 * count * a_size - 2 * (count - 1) * RING_ROWS, x_send.at[0])
+    drain(1, a_o, 2 * (count - 1) * RING_ROWS, x_send.at[3])
     side_done(1, 7)
     drain(1, a_o, 4 * count * a_size, x_send.at[1])
     whole_a = pltpu.make_async_copy(a_o, a_h, o_sem.at[4])
@@ -1250,8 +1286,9 @@
         xr=low(count, 2, a_part, width), rs_ff=low(count - 1, 2, ff_part, width),
         rs_a=low(count - 1, 2, a_part, width), ff_o=low(2 * units, width), a_o=low(4 * width, width),
         smalls=wide(swaps + 1, lines, width), small_r=wide(swaps, lines, width),
-        send=sem(22), recv=sem(22), r_send=sem(2), r_recv=sem(streams, count - 1),
-        g_send=sem(2), g_recv=sem(streams, count - 1), x_send=sem(3), x_recv=sem(2, count),
+        send=sem(24), recv=sem(24), r_send=sem(2), r_recv=sem(streams, count - 1),
+        g_send=sem(2), g_recv=sem(streams, count - 1), x_send=sem(4), x_recv=sem(2, count),
+        t_recv=sem(2, count - 1),
         s_recv=sem(4, count), y_recv=sem(2, count),
         m_send=sem(swaps), m_recv=sem(swaps), w_sem=sem(5 + halves), o_sem=sem(7), l_sem=sem(14),
     )

time: 164 us -> 162 us (0.988)
  Pallas kernels: 162 us -> 160 us
where the time goes in v7:
time: 162 us
  Pallas kernels  160 us (99%)
    pallas_call x1, Pallas kernels, pair_device(): pl.pallas_call(functools.partial(block_kernel, count), out_shape=outs, in...  149 us
    pallas_call x1, Pallas kernels, finish(): pl.pallas_call(functools.partial(finish_kernel, halves), grid=(steps,), o...  10.7 us

profile of v7, /device:TPU:0, one launch (start us, length us, event | category | flops | bytes accessed | tf_op | source)
XLA Modules:
  0.0 161.5 jit_solution(15393833316624872924)
XLA Ops:
  1.3 149.3 %block.1 = (bf16[256,768]{1,0:T(8,128)(2,1)}, f32[256,768]{1,0:T(8,128)}, bf16[3072,768]{1,0:T(8,128)(2,1)}, bf16[3072,768]{1,0:T(8,128)(2,1)}, f32[16,768]{1,0:T(8,128)}) custom-call(bf16[256,768]{1,0:T(8,128)(2,1)} %tok_h.1, s32[512]{0:T(512)} %places_h.1, s32[1,1]{1,0:T(1,128)} %bitcast.1.span_h, bf16[768]{0:T(1024)(128)(2,1)} %bq.1, bf16[768]{0:T(1024)(128)(2,1)} %bk.1, ...), custom_call_target="tpu_custom_call" | custom-call | tf_op jit(solution)/shard_map/block/pallas_call | solution.py:1300
  150.6 10.7 %finish.1 = (bf16[256,768]{1,0:T(8,128)(2,1)}, f32[256,768]{1,0:T(8,128)}, f32[768,768]{1,0:T(8,128)}, f32[768]{0:T(1024)}, f32[768,768]{1,0:T(8,128)}, /*index=...) custom-call(bf16[3072,768]{1,0:T(8,128)(2,1)} %get-tuple-element.23., ...), custom_call_target="tpu_custom_call" | custom-call | tf_op jit(solution)/shard_map/finish/pallas_call | solution.py:1211

commit v8 on v7

--- a/solution.py
+++ b/solution.py
@@ -363,13 +363,15 @@
     return total
 
 
-def angle_tables(places, length, span, cosb, sinb, ctab):
-    rows = cosb.shape[0]
+def angle_lines(places, length):
+    rows = places.shape[0]
     angle = math.pi / 2 * places.astype(f32).reshape(1, rows) / (3 * length)
     line = lax.broadcasted_iota(jnp.int32, (8, rows), 0)
-    block = jnp.where(line == 0, jnp.cos(angle), jnp.where(line == 1, jnp.sin(angle), 0.0))
-    cosb[...] = column_of(block, 0)
-    sinb[...] = column_of(block, 1)
+    return jnp.where(line == 0, jnp.cos(angle), jnp.where(line == 1, jnp.sin(angle), 0.0))
+
+
+def angle_products(block, span, ctab):
+    rows = ctab.shape[0]
     both = contract(block, block, 0, 0, highest)
     row = lax.broadcasted_iota(jnp.int32, (rows, rows), 0)
     col = lax.broadcasted_iota(jnp.int32, (rows, rows), 1)
@@ -491,7 +493,9 @@
         vec[9 + part : 10 + part, :] = piece.astype(f32).reshape(1, width)
     own, far_rows = pl.ds(0, rows), pl.ds(rows, rows)
     my_places = places[pl.ds(pl.multiple_of(rank * rows, rows), rows)]
-    angle_tables(my_places, places.shape[0], span, cosb, sinb, ctab)
+    angles = angle_lines(my_places, places.shape[0])
+    cosb[...] = column_of(angles, 0)
+    sinb[...] = column_of(angles, 1)
     diag = pair_mask()
     first, second = head_masks()
     first_low, second_low = first.astype(bf16), second.astype(bf16)
@@ -503,25 +507,14 @@
     def add_small(slot, line):
         smalls[0, slot : slot + 1, :] = line
 
-    def project(which, target):
-        @pl.loop(0, tiles)
-        def _(j):
-            cols = tile_at(j, TILE)
-            value = mm(tok[...], wa[pl.ds(which * width, width), cols]) + vec[which : which + 1, cols]
-            if which < 2:
-                value = jnp.maximum(value, 0.0)
-            target[:, cols] = value.astype(bf16)
-
-    fetch(0).wait()
-    load(0).wait()
-    project(1, rk)
-    load(1).wait()
-    project(2, vv)
-    for index in range(3, len(loads)):
-        load(index).start()
-
-    @pl.loop(0, pairs)
-    def _(p):
+    def project(which, target, j):
+        cols = tile_at(j, TILE)
+        value = mm(tok[...], wa[pl.ds(which * width, width), cols]) + vec[which : which + 1, cols]
+        if which < 2:
+            value = jnp.maximum(value, 0.0)
+        target[:, cols] = value.astype(bf16)
+
+    def make_state(p):
         lanes = tile_at(p, LANES)
         k = rk[:, lanes].astype(f32) * (1.0 / HD)
         v = vv[:, lanes]
@@ -533,13 +526,29 @@
             jnp.sum(ks.astype(f32), axis=0, keepdims=True),
         )
 
-    pl.semaphore_wait(barrier, len(partners))
-    state_copy = peer_copy(tsend, trecv, sems, 0, peer)
+    together = TILE // LANES
+
+    def state_copy(j):
+        where = pl.ds(j * together, together)
+        return peer_copy(tsend.at[where], trecv.at[where], sems, (0, 24, 25)[j], peer)
+
     key_copy = peer_copy(zsend, zrecv, sems, 1, peer)
-    state_copy.start()
+    fetch(0).wait()
+    load(0).wait()
+    load(1).wait()
+    for index in range(3, len(loads)):
+        load(index).start()
+    for j in range(tiles):
+        project(1, rk, j)
+        project(2, vv, j)
+        pl.loop(j * together, (j + 1) * together)(make_state)
+        if j == 0:
+            pl.semaphore_wait(barrier, len(partners))
+        state_copy(j).start()
     key_copy.start()
+    angle_products(angles, span, ctab)
     load(2).wait()
-    project(0, rq)
+    pl.loop(0, tiles)(functools.partial(project, 0, rq))
 
     @pl.loop(0, pairs)
     def _(p):
@@ -552,7 +561,8 @@
         numer[:, lanes] = parts[0] * first + parts[1] * second
         denom[:, lanes] = pltpu.roll(parts[0] * second + parts[1] * first, HD, 1)
 
-    state_copy.wait()
+    for j in range(tiles):
+        state_copy(j).wait()
     key_copy.wait()
 
     @pl.loop(0, pairs)
@@ -1090,8 +1100,9 @@
     swap_small(0)
 
     def spread_gather(s):
-        ring_spread(a_streams, s)
-        ring_gather(ff_streams, s - 1)
+        for cut in range(FF_CUTS):
+            ring_spread(a_streams[cut::A_CUTS], s)
+            ring_gather(ff_streams[cut::FF_CUTS], s - 1)
 
     start_folds(2)
     ring_spread(a_streams, 0)
@@ -1286,7 +1297,7 @@
         xr=low(count, 2, a_part, width), rs_ff=low(count - 1, 2, ff_part, width),
         rs_a=low(count - 1, 2, a_part, width), ff_o=low(2 * units, width), a_o=low(4 * width, width),
         smalls=wide(swaps + 1, lines, width), small_r=wide(swaps, lines, width),
-        send=sem(24), recv=sem(24), r_send=sem(2), r_recv=sem(streams, count - 1),
+        send=sem(26), recv=sem(26), r_send=sem(2), r_recv=sem(streams, count - 1),
         g_send=sem(2), g_recv=sem(streams, count - 1), x_send=sem(4), x_recv=sem(2, count),
         t_recv=sem(2, count - 1),
         s_recv=sem(4, count), y_recv=sem(2, count),

time: 162 us -> 161 us (level)
  no operation moved by 1% of the time
where the time goes in v8:
time: 161 us
  Pallas kernels  159 us (99%)
    pallas_call x1, Pallas kernels, pair_device(): pl.pallas_call(functools.partial(block_kernel, count), out_shape=outs, in...  148 us
    pallas_call x1, Pallas kernels, finish(): pl.pallas_call(functools.partial(finish_kernel, halves), grid=(steps,), o...  10.7 us

profile of v8, /device:TPU:0, one launch (start us, length us, event | category | flops | bytes accessed | tf_op | source)
XLA Modules:
  0.0 160.6 jit_solution(11906860861735280458)
XLA Ops:
  1.3 148.4 %block.1 = (bf16[256,768]{1,0:T(8,128)(2,1)}, f32[256,768]{1,0:T(8,128)}, bf16[3072,768]{1,0:T(8,128)(2,1)}, bf16[3072,768]{1,0:T(8,128)(2,1)}, f32[16,768]{1,0:T(8,128)}) custom-call(bf16[256,768]{1,0:T(8,128)(2,1)} %tok_h.1, s32[512]{0:T(512)} %places_h.1, s32[1,1]{1,0:T(1,128)} %bitcast.1.span_h, bf16[768]{0:T(1024)(128)(2,1)} %bq.1, bf16[768]{0:T(1024)(128)(2,1)} %bk.1, ...), custom_call_target="tpu_custom_call" | custom-call | tf_op jit(solution)/shard_map/block/pallas_call | solution.py:1311
  149.7 10.7 %finish.1 = (bf16[256,768]{1,0:T(8,128)(2,1)}, f32[256,768]{1,0:T(8,128)}, f32[768,768]{1,0:T(8,128)}, f32[768]{0:T(1024)}, f32[768,768]{1,0:T(8,128)}, /*index=...) custom-call(bf16[3072,768]{1,0:T(8,128)(2,1)} %get-tuple-element.23., ...), custom_call_target="tpu_custom_call" | custom-call | tf_op jit(solution)/shard_map/finish/pallas_call | solution.py:1222

commit v9 on v8

--- a/solution.py
+++ b/solution.py
@@ -292,7 +292,7 @@
 MESH = pl.DeviceIdType.MESH
 LANES = 2 * HD
 TILE = 256
-ROWBLOCK = 32
+ROWBLOCK = 64
 FINISH = 256
 FF_CUTS = 3
 A_CUTS = 3

time: 161 us -> 161 us (level)
  no operation moved by 1% of the time
where the time goes in v9:
time: 161 us; the launch traced here: 160 us
  Pallas kernels  159 us (99%)
    pallas_call x1, Pallas kernels, pair_device(): pl.pallas_call(functools.partial(block_kernel, count), out_shape=outs, in...  148 us
    pallas_call x1, Pallas kernels, finish(): pl.pallas_call(functools.partial(finish_kernel, halves), grid=(steps,), o...  10.7 us

profile of v9, /device:TPU:0, one launch (start us, length us, event | category | flops | bytes accessed | tf_op | source)
XLA Modules:
  0.0 160.2 jit_solution(11707967872418009870)
XLA Ops:
  1.3 148.0 %block.1 = (bf16[256,768]{1,0:T(8,128)(2,1)}, f32[256,768]{1,0:T(8,128)}, bf16[3072,768]{1,0:T(8,128)(2,1)}, bf16[3072,768]{1,0:T(8,128)(2,1)}, f32[16,768]{1,0:T(8,128)}) custom-call(bf16[256,768]{1,0:T(8,128)(2,1)} %tok_h.1, s32[512]{0:T(512)} %places_h.1, s32[1,1]{1,0:T(1,128)} %bitcast.1.span_h, bf16[768]{0:T(1024)(128)(2,1)} %bq.1, bf16[768]{0:T(1024)(128)(2,1)} %bk.1, ...), custom_call_target="tpu_custom_call" | custom-call | tf_op jit(solution)/shard_map/block/pallas_call | solution.py:1311
  149.3 10.7 %finish.1 = (bf16[256,768]{1,0:T(8,128)(2,1)}, f32[256,768]{1,0:T(8,128)}, f32[768,768]{1,0:T(8,128)}, f32[768]{0:T(1024)}, f32[768,768]{1,0:T(8,128)}, /*index=...) custom-call(bf16[3072,768]{1,0:T(8,128)(2,1)} %get-tuple-element.23., ...), custom_call_target="tpu_custom_call" | custom-call | tf_op jit(solution)/shard_map/finish/pallas_call | solution.py:1222
